TPU v7x, 32 devices: a whole 2x2x4 slice. The times are simulated.
32 devices in a mesh: dp: 8 (over z, x), tensor: 4 (over y, core).
Axes of the slice: x: 2, y: 2, z: 4, core: 2. Of those that a mesh axis runs over, the one named last changes fastest.
Arguments:
- tokens: bfloat16 [32768, 768], P('dp'), may hold values from -6 to 6
- cotangent: bfloat16 [32768, 768], P('dp'), may hold values from -6 to 6
- short_len: int32 [128], P('dp'), may hold values from 64 to 128, as said below
- long_len: int32 [32], P('dp'), may hold values from 256 to 512, as said below
- short_count: int32 [8], P('dp'), may hold values from 8 to 16, as said below
- long_count: int32 [8], P('dp'), may hold values from 0 to 4, as said below
- query_weight: bfloat16 [768, 768], P(None, 'tensor'), may hold values from -0.3125 to 0.3125
- query_bias: bfloat16 [768], P('tensor'), may hold values from -3 to 3
- key_weight: bfloat16 [768, 768], P(None, 'tensor'), may hold values from -0.3125 to 0.3125
- value_weight: bfloat16 [768, 768], P(None, 'tensor'), may hold values from -0.21875 to 0.21875
- value_bias: bfloat16 [768], P('tensor'), may hold values from -3 to 3
- output_weight: bfloat16 [768, 768], P('tensor'), may hold values from -0.875 to 0.875
- output_bias: bfloat16 [768], replicated, may hold values from -3 to 3
- first_gain: bfloat16 [768], replicated, may hold values from 0.5 to 1.5
- first_shift: bfloat16 [768], replicated, may hold values from -3 to 3
- up_weight: bfloat16 [768, 3072], P(None, 'tensor'), may hold values from -0.21875 to 0.21875
- up_bias: bfloat16 [3072], P('tensor'), may hold values from -3 to 3
- down_weight: bfloat16 [3072, 768], P('tensor'), may hold values from -0.109375 to 0.109375
- down_bias: bfloat16 [768], replicated, may hold values from -2 to 2
- second_gain: bfloat16 [768], replicated, may hold values from 0.5 to 1.5
- second_shift: bfloat16 [768], replicated, may hold values from -3 to 3
Outputs:
- layer_output: bfloat16 [32768, 768], P('dp')
- input_grad: float32 [32768, 768], P('dp')
- grad_query_weight: float32 [768, 768], P(None, 'tensor')
- grad_query_bias: float32 [768], P('tensor')
- grad_key_weight: float32 [768, 768], P(None, 'tensor')
- grad_value_weight: float32 [768, 768], P(None, 'tensor')
- grad_value_bias: float32 [768], P('tensor')
- grad_output_weight: float32 [768, 768], P('tensor')
- grad_output_bias: float32 [768], replicated
- grad_first_gain: float32 [768], replicated
- grad_first_shift: float32 [768], replicated
- grad_up_weight: float32 [768, 3072], P(None, 'tensor')
- grad_up_bias: float32 [3072], P('tensor')
- grad_down_weight: float32 [3072, 768], P('tensor')
- grad_down_bias: float32 [768], replicated
- grad_second_gain: float32 [768], replicated
- grad_second_shift: float32 [768], replicated
Inputs may be any that keep to these rules, and one draw needn't show every extreme that they name: `short_len`: some slot has exactly 128 valid tokens. `long_len`: some slot has exactly 512 valid tokens. `short_count`: slots at or beyond the count hold no valid tokens; some index of dp has all 16 live. `long_count`: slots at or beyond the count hold no valid tokens; some index of dp has all 4 live.
All inputs are finite; a program needn't handle non-finite values.
Results may differ from a plain program's by a relative error of at most 0.02.
Values may be sent and summed in bfloat16 or wider, within the bound.
No kernel may reach another device: no remote copies, remote signals or barrier semaphores. Data moves between devices by JAX's collectives and lax.ppermute only.
A program may use at most 256 MiB of HBM per device.

v0:
```python
import functools

import jax
import jax.numpy as jnp
from jax import lax
from jax.experimental import pallas as pl
from jax.experimental.pallas import tpu as pltpu
from jax.sharding import PartitionSpec as P

HEAD_DIM = 64
SHORT_LEN = 128
LONG_LEN = 512
ROWS = 512
SLOTS = ROWS // SHORT_LEN
PAIR = 2 * HEAD_DIM
MASKED = -30000.0
F32 = jnp.float32
BF16 = jnp.bfloat16
VMEM_LIMIT = 60 * 1024 * 1024


def nn(left, right):
    return lax.dot_general(left, right, (((1,), (0,)), ((), ())), preferred_element_type=F32)


def nt(left, right):
    return lax.dot_general(left, right, (((1,), (1,)), ((), ())), preferred_element_type=F32)


def tn(left, right):
    return lax.dot_general(left, right, (((0,), (0,)), ((), ())), preferred_element_type=F32)


def fold_rows(values):
    return jnp.sum(values.reshape(-1, 8, values.shape[-1]), axis=0)


def total_rows(values):
    return jnp.sum(values, axis=0, keepdims=True)


def by_rows(size, body):
    def step(n, carry):
        body(pl.ds(pl.multiple_of(n * 64, 64), 64))
        return carry

    lax.fori_loop(0, size // 64, step, 0)


def clear(ref):
    def body(span):
        for j in range(ref.shape[0]):
            ref[j, span] = jnp.zeros((64, ref.shape[2]), ref.dtype)

    by_rows(ref.shape[1], body)


def copy_rows(source, target, at=0):
    def body(span):
        target[pl.ds(pl.multiple_of(at + span.start, 16), 64)] = source[span].astype(target.dtype)

    if source.shape[0] % 64:
        target[pl.ds(at, source.shape[0])] = source[...].astype(target.dtype)
    else:
        by_rows(source.shape[0], body)


def half_mask(which):
    lanes = lax.broadcasted_iota(jnp.int32, (1, PAIR), 1)
    return (lanes >= HEAD_DIM) if which else (lanes < HEAD_DIM)


def short_valid(meta, block, slot):
    index = SLOTS * (2 * block + meta[0][0]) + slot
    return jnp.where(index < meta[3][0], meta[1][index], 0)


def long_valid(meta, block, short_blocks):
    index = 2 * (block - short_blocks) + 1 - meta[0][0]
    return jnp.where(index < meta[4][0], meta[2][index], 0)


def norm_rows(values):
    centre = values - jnp.mean(values, axis=-1, keepdims=True)
    scale = lax.rsqrt(jnp.mean(centre * centre, axis=-1, keepdims=True) + 1e-12)
    return centre * scale, scale


def norm_back(incoming, normed, scale, gain):
    grad = incoming * gain
    inner = grad - jnp.mean(grad, axis=-1, keepdims=True)
    inner = inner - normed * jnp.mean(grad * normed, axis=-1, keepdims=True)
    return scale * inner


def load_attention_weights(pieces, wqkv, wout, bias, sems):
    width = wqkv.shape[0] // 6
    copies = []
    for j, piece in enumerate(pieces):
        for k in range(3):
            copies.append(
                (piece.at[pl.ds(k * width, width)], wqkv.at[pl.ds((2 * k + j) * width, width)])
            )
        copies.append((piece.at[pl.ds(3 * width, width)], wout.at[pl.ds(j * width, width)]))
        copies.append((piece.at[pl.ds(4 * width, 16)], bias.at[pl.ds(16 * j, 16)]))
    started = [pltpu.make_async_copy(s, d, sems.at[n]) for n, (s, d) in enumerate(copies)]
    for copy in started:
        copy.start()
    for copy in started:
        copy.wait()


def flat_row(ref):
    return ref[...].astype(F32).reshape(1, ref.shape[0])


def pack_kernel(at, wq, wk, wv, wo, qb, vb, ub, ob, g1, s1, db, g2, s2, piece, vec, wide):
    width = wq.shape[0]
    d = piece.shape[1]
    piece[0:width] = wq[...]
    piece[width : 2 * width] = wk[...]
    piece[2 * width : 3 * width] = wv[...]
    piece[3 * width : 4 * width] = wo[...]
    index = lax.broadcasted_iota(jnp.int32, (16, 1), 0)
    wide[...] = jnp.zeros_like(wide)
    wide[0:1, 0:width] = flat_row(qb)
    wide[1:2, 0:width] = flat_row(vb)
    row_q, row_v, row_u = wide[0:1], wide[1:2], flat_row(ub)
    lead = jnp.where(lax.broadcasted_iota(jnp.int32, (1, d), 1) < d // 2, row_u, 0.0)
    trail = pltpu.roll(row_u - lead, d // 2, 1)
    mine = jnp.where(at[0] == 0, lead, trail)
    far = jnp.where(at[0] == 0, trail, lead)
    rows = [row_u, row_q, pltpu.roll(row_q, width, 1), row_v, pltpu.roll(row_v, width, 1)]
    block = jnp.zeros((16, d), F32)
    for n, row in enumerate(rows + [None] * 4 + [mine, far]):
        if row is not None:
            block = jnp.where(index == n, row, block)
    piece[4 * width : 4 * width + 16] = block.astype(BF16)
    for n, row in enumerate((ob, g1, s1, db, g2, s2)):
        vec[n : n + 1] = flat_row(row)
    vec[6:8] = jnp.zeros((2, d), F32)


def place_kernel(core, other, whole, out):
    out[...] = other[...].astype(out.dtype)


def route_halves_kernel(at, mine, partner, keep, send):
    half = keep.shape[0]
    for out, which in ((keep, at[0]), (send, 1 - at[0])):
        base = which * half

        def body(span):
            rows = pl.ds(pl.multiple_of(base + span.start, 16), 64)
            out[span] = (mine[rows].astype(F32) + partner[rows].astype(F32)).astype(BF16)

        by_rows(half, body)


def route_quarters_kernel(at, keep, other, *outs):
    size = outs[0].shape[0]
    for k, out in enumerate(outs):
        span = pl.ds(pl.multiple_of((at[0] ^ k) * size, 16), size)
        out[...] = (keep[span].astype(F32) + other[span].astype(F32)).astype(BF16)


def add_kernel(at, *refs):
    def body(span):
        refs[-1][span] = sum(ref[span].astype(F32) for ref in refs[:-1]).astype(BF16)

    size = refs[-1].shape[0]
    if size % 64:
        body(pl.ds(0, size))
    else:
        by_rows(size, body)


def choose_kernel(at, own, other, out):
    central = jnp.logical_or(at[0] == 1, at[0] == 2)

    @pl.when(central)
    def _():
        out[...] = own[...]

    @pl.when(jnp.logical_not(central))
    def _():
        out[...] = other[...]


def join_kernel(at, *refs):
    out = refs[-1]
    size = refs[0].shape[0]
    for k, ref in enumerate(refs[:-1]):
        copy_rows(ref, out, pl.multiple_of((at[0] ^ k) * size, 16))


def finish_kernel(at, own, other, *refs):
    outs, whole = refs[:-1], refs[-1]
    join_kernel(at, own, other, whole)
    start = 0
    for out in outs:
        copy_rows(whole.at[pl.ds(start, out.shape[0])], out)
        start += out.shape[0]


def stacked(values):
    zero = jnp.zeros_like(values)
    return jnp.concatenate([jnp.where(half_mask(e), values, zero) for e in range(2)], axis=0)


def unstacked(values):
    size = values.shape[0] // 2
    return jnp.where(half_mask(0), values[:size], values[size:])


def attention_heads_forward(start, count, short_blocks, meta, x, weights, qkv, mixed, logs, stat):
    wqkv, bias, head_bias = weights
    block = pl.program_id(0) + start
    half = mixed.shape[1]

    @pl.when(pl.program_id(0) == 0)
    def _():
        small = bias[...].astype(F32)
        head_bias[0] = (small[1:2] + small[18:19])[:, 0:half]
        head_bias[1] = jnp.zeros((1, half), F32)
        head_bias[2] = (small[3:4] + small[20:21])[:, 0:half]

    def project(k, carry):
        span = pl.ds(pl.multiple_of(k * half, half), half)
        qkv[:, span] = (nt(x[...], wqkv[span]) + head_bias[k]).astype(BF16)
        return carry

    lax.fori_loop(0, 3, project, 0)
    stat[...] = jnp.zeros_like(stat)
    lanes = lax.broadcasted_iota(jnp.int32, (1, 128), 1)

    def tiles(pair, spans):
        column = pl.multiple_of(pair * PAIR, PAIR)
        q, scores = [], []
        for query_at, queries, key_at, keys, valid in spans:
            part = qkv[query_at : query_at + queries, pl.ds(column, PAIR)] * jnp.asarray(0.125, BF16)
            key_part = qkv[key_at : key_at + keys, pl.ds(half + column, PAIR)]
            scores.append(nt(stacked(part), key_part))
        live = [lax.broadcasted_iota(jnp.int32, (1, t[3]), 1) < t[4] for t in spans]
        scores = [jnp.where(a, v, MASKED) for a, v in zip(live, scores)]
        top = [jnp.max(v, axis=-1, keepdims=True) for v in scores]
        weights = [jnp.exp(v - m) for v, m in zip(scores, top)]
        total = [jnp.sum(v, axis=-1, keepdims=True) for v in weights]
        out = [
            nn(v.astype(BF16), qkv[t[2] : t[2] + t[3], pl.ds(2 * half + column, PAIR)])
            for v, t in zip(weights, spans)
        ]
        for (query_at, queries, *_), m, n, v in zip(spans, top, total, out):
            log = m + jnp.log(n)
            rows = stat[query_at : query_at + queries]
            rows = jnp.where(lanes == 2 * pair, log[:queries], rows)
            stat[query_at : query_at + queries] = jnp.where(lanes == 2 * pair + 1, log[queries:], rows)
            mixed[query_at : query_at + queries, pl.ds(column, PAIR)] = unstacked(v * (1.0 / n)).astype(BF16)

    def short_path():
        spans = [
            (slot * SHORT_LEN, SHORT_LEN, slot * SHORT_LEN, SHORT_LEN, short_valid(meta, block, slot))
            for slot in range(SLOTS)
        ]

        def body(pair, carry):
            tiles(pair, spans)
            return carry

        lax.fori_loop(0, half // PAIR, body, 0)

    def long_path():
        valid = long_valid(meta, block, short_blocks)
        spans = [(part * 256, 256, 0, LONG_LEN, valid) for part in range(2)]

        def body(pair, carry):
            tiles(pair, spans)
            return carry

        lax.fori_loop(0, half // PAIR, body, 0)

    if start < short_blocks:
        pl.when(block < short_blocks)(short_path)
    if start + count > short_blocks:
        pl.when(block >= short_blocks)(long_path)
    logs[...] = stat[...].T[0:8]


def attention_forward_kernel(
    start, count, short_blocks, core, slen, llen, scount, lcount, x, a0, a1, qkv, mixed, logs,
    wqkv, wout, bias, sems, stat, head_bias,
):
    @pl.when(pl.program_id(0) == 0)
    def _():
        load_attention_weights((a0, a1), wqkv, wout, bias, sems)

    meta = (core, slen, llen, scount, lcount)
    attention_heads_forward(start, count, short_blocks, meta, x, (wqkv, bias, head_bias), qkv, mixed, logs, stat)


def attention_finish_kernel(
    start, count, short_blocks, core, slen, llen, scount, lcount, x, a2, a3, mixed_near, a0, a1, vec, *rest,
):
    qkv, mixed, logs, normed, scale_rows, wqkv, wout, bias, near_out, sems, stat, head_bias = rest[-12:]

    @pl.when(pl.program_id(0) == 0)
    def _():
        width = near_out.shape[0] // 2
        near = [
            pltpu.make_async_copy(
                piece.at[pl.ds(3 * width, width)], near_out.at[pl.ds(j * width, width)], sems.at[10 + j]
            )
            for j, piece in enumerate((a0, a1))
        ]
        for copy in near:
            copy.start()
        load_attention_weights((a2, a3), wqkv, wout, bias, sems)
        for copy in near:
            copy.wait()

    meta = (core, slen, llen, scount, lcount)
    attention_heads_forward(start, count, short_blocks, meta, x, (wqkv, bias, head_bias), qkv, mixed, logs, stat)
    hidden = x[...].astype(F32) + vec[0:1]
    hidden = hidden + nn(mixed_near[...], near_out[...]) + nn(mixed[...], wout[...])
    rows, scale = norm_rows(hidden)
    normed[...] = rows.astype(BF16)
    scale_rows[...] = jnp.broadcast_to(scale, scale_rows.shape)


def weight_copies(side, ups, downs, up_all, down_all, sems):
    half = ups[2].shape[1]
    spans = [pl.ds(pl.multiple_of(at * half, 16), half) for at in (side[0], 1 - side[0])]
    copies = []
    for j in range(2):
        copies.append([(ups[j], up_all.at[j]), (downs[j], down_all.at[j])])
    for j in range(2):
        pairs = []
        for n in range(2):
            part = pl.ds(n * half, half)
            pairs.append((ups[2 + 2 * n + j], up_all.at[2 + j, :, part]))
            pairs.append((downs[2 + j].at[spans[n]], down_all.at[2 + j, part]))
        copies.append(pairs)
    return [
        [pltpu.make_async_copy(s, d, sems.at[4 * j + n]) for n, (s, d) in enumerate(pairs)]
        for j, pairs in enumerate(copies)
    ]


def start_weights(copies):
    for pairs in copies:
        for copy in pairs:
            copy.start()


def wait_weights(copies, step):
    for at in range(2):

        @pl.when(jnp.logical_and(pl.program_id(0) == 0, step == at))
        def _():
            for pairs in copies[2 * at : 2 * at + 2]:
                for copy in pairs:
                    copy.wait()


def ffn_forward_kernel(short_blocks, core, slen, llen, scount, lcount, side, normed, cotangent, *rest):
    ups, downs, biases = rest[0:6], rest[6:10], rest[10:14]
    vec, layer_out, layer_rows, grad_low, slope, down_mine, down_partner, sums = rest[14:22]
    active, down_sum, vec_sum, up_all, down_all, bias_all, total, sems = rest[22:]
    meta = (core, slen, llen, scount, lcount)
    block = pl.program_id(0)
    units = up_all.shape[2]
    half = units // 2
    copies = weight_copies(side, ups, downs, up_all, down_all, sems)

    @pl.when(block == 0)
    def _():
        start_weights(copies)
        clear(down_sum)
        vec_sum[...] = jnp.zeros_like(vec_sum)
        for j in range(2):
            bias_all[j] = biases[j][0:1].astype(F32)
            for n in range(2):
                bias_all[2 + j, :, n * half : (n + 1) * half] = biases[2 + j][9 + n : 10 + n, 0:half].astype(F32)

    first = normed[...].astype(F32) * vec[1:2] + vec[2:3]
    first_low = first.astype(BF16)
    total[...] = first + vec[3:4]

    def groups(step, carry):
        wait_weights(copies, step)
        for e in range(2):
            j = 2 * step + e
            inner = nn(first_low, up_all[j]) + bias_all[j]
            chance = 0.5 * (1.0 + lax.erf(inner * 0.7071067811865476))
            low_units = (inner * chance).astype(BF16)
            slope[:, pl.ds(pl.multiple_of(j * units, units), units)] = (
                chance + inner * jnp.exp(-0.5 * inner * inner) * 0.3989422804014327
            ).astype(BF16)
            active[j] = low_units
            total[...] += nn(low_units, down_all[j])
        return carry

    lax.fori_loop(0, 2, groups, 0)
    rows, scale = norm_rows(total[...])
    result = (rows * vec[4:5] + vec[5:6]).astype(BF16)
    layer_out[...] = result
    layer_rows[...] = result
    position = lax.broadcasted_iota(jnp.int32, (ROWS, 1), 0)
    slot = position // SHORT_LEN
    short_limit = jnp.zeros((ROWS, 1), jnp.int32)
    for n in range(SLOTS):
        short_limit = jnp.where(slot == n, short_valid(meta, jnp.minimum(block, short_blocks - 1), n), short_limit)
    long_limit = long_valid(meta, jnp.maximum(block, short_blocks), short_blocks)
    is_short = block < short_blocks
    alive = jnp.where(is_short, position % SHORT_LEN, position) < jnp.where(
        is_short, short_limit, long_limit
    )
    upstream = jnp.where(alive, cotangent[...].astype(F32), 0.0)
    grad = norm_back(upstream, rows, scale, vec[4:5])
    low = grad.astype(BF16)
    grad_low[...] = low
    vec_sum[0] += fold_rows(upstream * rows)
    vec_sum[1] += fold_rows(upstream)
    vec_sum[2] += fold_rows(grad)
    for j in range(2):
        down_sum[j] += tn(active[j], low)

    @pl.when(block == pl.num_programs(0) - 1)
    def _():
        copy_rows(down_sum.at[0], down_mine)
        copy_rows(down_sum.at[1], down_partner)
        sums[...] = jnp.zeros_like(sums)
        for n in range(3):
            sums[n : n + 1] = total_rows(vec_sum[n])


def ffn_backward_kernel(side, grad_low, slope, normed, stat, mixed, sums_two, *rest):
    ups, downs = rest[0:6], rest[6:10]
    vec, hidden_low, mine, partner = rest[10:14]
    up_sum, out_sum, vec_sum, kept, up_all, down_all, total, sems = rest[14:]
    block = pl.program_id(0)
    units = up_sum.shape[2]
    width = mixed.shape[1] // 2
    copies = weight_copies(side, ups, downs, up_all, down_all, sems)

    @pl.when(block == 0)
    def _():
        start_weights(copies)
        clear(up_sum)
        out_sum[...] = jnp.zeros_like(out_sum)
        vec_sum[...] = jnp.zeros_like(vec_sum)

    low = grad_low[...]
    total[...] = low.astype(F32)

    def groups(step, carry):
        wait_weights(copies, step)
        for e in range(2):
            j = 2 * step + e
            inner = nt(low, down_all[j]) * slope[:, pl.ds(pl.multiple_of(j * units, units), units)].astype(F32)
            inner_low = inner.astype(BF16)
            total[...] += nt(inner_low, up_all[j])
            vec_sum[j] += fold_rows(inner)
            kept[j] = inner_low
        return carry

    lax.fori_loop(0, 2, groups, 0)
    rows = normed[...].astype(F32)
    first_low = (rows * vec[1:2] + vec[2:3]).astype(BF16)
    for j in range(2):
        up_sum[j] += tn(first_low, kept[j])
    incoming = total[...]
    grad = norm_back(incoming, rows, stat[:, 0:1], vec[1:2])
    vec_sum[4] += fold_rows(incoming * rows)
    vec_sum[5] += fold_rows(incoming)
    vec_sum[6] += fold_rows(grad)
    grad_attn = grad.astype(BF16)
    hidden_low[...] = grad_attn
    out_sum[...] += tn(mixed[...], grad_attn)

    @pl.when(block == pl.num_programs(0) - 1)
    def _():
        index = lax.broadcasted_iota(jnp.int32, (16, 1), 0)
        shared = [sums_two[n : n + 1] for n in range(3)] + [total_rows(vec_sum[n]) for n in range(4, 7)]
        for j, out in enumerate((mine, partner)):
            copy_rows(up_sum.at[j], out)
            copy_rows(out_sum.at[pl.ds(j * width, width)], out, units)
            out[units + width :] = jnp.zeros((out.shape[0] - units - width, out.shape[1]), BF16)
            rows_out = jnp.zeros((16, out.shape[1]), F32)
            for n, row in enumerate(shared + [total_rows(vec_sum[j])]):
                rows_out = jnp.where(index == n, row, rows_out)
            out[units + width : units + width + 16] = rows_out.astype(BF16)


def attention_heads_backward(start, short_blocks, meta, logs, qkv, mixed, mixed_grad, low_qkv, delta):
    block = pl.program_id(0) + start
    half = mixed.shape[1]
    own = (mixed_grad[...].astype(F32) * mixed[...].astype(F32)).astype(BF16)
    head = lax.broadcasted_iota(jnp.int32, (8, half), 1) // HEAD_DIM
    pick = jnp.where(head == lax.broadcasted_iota(jnp.int32, (8, half), 0), 1.0, 0.0)
    delta[...] = nt(pick.astype(BF16), own)

    index = lax.broadcasted_iota(jnp.int32, (8, 1), 0)

    def tiles(pair, size, valids):
        column = pl.multiple_of(pair * PAIR, PAIR)
        spans = [pl.ds(n * size, size) for n in range(len(valids))]

        def rows(ref, span):
            picked = [total_rows(jnp.where(index == 2 * pair + e, ref[:, span], 0.0)) for e in range(2)]
            return jnp.concatenate(picked, axis=1)

        q = [stacked(qkv[t, pl.ds(column, PAIR)] * jnp.asarray(0.125, BF16)) for t in spans]
        g = [stacked(mixed_grad[t, pl.ds(column, PAIR)]) for t in spans]
        k = [qkv[t, pl.ds(half + column, PAIR)] for t in spans]
        scores = [nt(b, a) for a, b in zip(q, k)]
        grads = [nt(qkv[t, pl.ds(2 * half + column, PAIR)], a) for t, a in zip(spans, g)]
        place = lax.broadcasted_iota(jnp.int32, (size, 1), 0)
        probs = [
            jnp.where(place < valid, jnp.exp(v - rows(logs, t)), 0.0)
            for v, t, valid in zip(scores, spans, valids)
        ]
        scores = [(p * (v - rows(delta, t))).astype(BF16) for p, v, t in zip(probs, grads, spans)]
        dq = [tn(v, b) for v, b in zip(scores, k)]
        dk = [nn(v, a) for v, a in zip(scores, q)]
        dv = [nn(p.astype(BF16), a) for p, a in zip(probs, g)]
        for t, a, b, c in zip(spans, dq, dk, dv):
            low_qkv[t, pl.ds(column, PAIR)] = (unstacked(a) * 0.125).astype(BF16)
            low_qkv[t, pl.ds(half + column, PAIR)] = b.astype(BF16)
            low_qkv[t, pl.ds(2 * half + column, PAIR)] = c.astype(BF16)

    if start < short_blocks:
        valids = [short_valid(meta, block, slot) for slot in range(SLOTS)]
        size = SHORT_LEN
    else:
        valids = [long_valid(meta, block, short_blocks)]
        size = LONG_LEN

    def body(pair, carry):
        tiles(pair, size, valids)
        return carry

    lax.fori_loop(0, half // PAIR, body, 0)


def attention_backward_kernel(
    start, short_blocks, core, slen, llen, scount, lcount, hidden_low, stat, qkv, mixed, x,
    a0, a1, *rest,
):
    if start:
        sums_in, vec_in, low_qkv, mine, partner = rest[:5]
    else:
        low_qkv, qkv_out, vec_out = rest[:3]
    wqkv, wout, bias, sems, mixed_grad, delta, qkv_sum, vec_sum = rest[-8:]
    meta = (core, slen, llen, scount, lcount)
    block = pl.program_id(0)
    half = mixed.shape[1]
    width = half // 2

    @pl.when(block == 0)
    def _():
        load_attention_weights((a0, a1), wqkv, wout, bias, sems)
        if start:
            qkv_sum[...] = sums_in[...]
            vec_sum[...] = vec_in[...]
        else:
            clear(qkv_sum)
            vec_sum[...] = jnp.zeros_like(vec_sum)

    mixed_grad[...] = nt(hidden_low[...], wout[...]).astype(BF16)
    attention_heads_backward(start, short_blocks, meta, stat, qkv, mixed, mixed_grad, low_qkv, delta)
    vec_sum[0] += fold_rows(low_qkv[:, 0:half].astype(F32))
    vec_sum[1] += fold_rows(low_qkv[:, 2 * half : 3 * half].astype(F32))

    for k in range(3):
        qkv_sum[k] += tn(low_qkv[:, k * half : (k + 1) * half], x[...])

    @pl.when(block == pl.num_programs(0) - 1)
    def _():
        if not start:
            qkv_out[...] = qkv_sum[...]
            vec_out[...] = vec_sum[...]
        else:
            index = lax.broadcasted_iota(jnp.int32, (16, 1), 0)
            heads = [total_rows(vec_sum[n]) for n in range(2)]
            for j, out in enumerate((mine, partner)):
                for k in range(3):
                    out[k * width : (k + 1) * width] = qkv_sum[k, j * width : (j + 1) * width].astype(BF16)
                out[3 * width :] = jnp.zeros((out.shape[0] - 3 * width, out.shape[1]), BF16)
                rows_out = jnp.zeros((16, half), F32)
                for n, row in enumerate(heads):
                    row = pltpu.roll(row, half - width, 1) if j else row
                    rows_out = jnp.where(index == n, row, rows_out)
                out[3 * width : 3 * width + 16, 0:half] = rows_out.astype(BF16)


def attention_input_kernel(
    start, short_blocks, core, slen, llen, scount, lcount, hidden_low, stat, qkv, mixed, low_near,
    a2, a3, a0, a1, *rest,
):
    input_rows, input_grad = rest[-10:-8]
    wqkv, wout, bias, near_qkv, sems, low_qkv, mixed_grad, delta = rest[-8:]
    meta = (core, slen, llen, scount, lcount)

    @pl.when(pl.program_id(0) == 0)
    def _():
        width = near_qkv.shape[0] // 6
        near = [
            pltpu.make_async_copy(
                piece.at[pl.ds(k * width, width)],
                near_qkv.at[pl.ds((2 * k + j) * width, width)],
                sems.at[10 + 2 * k + j],
            )
            for k in range(3)
            for j, piece in enumerate((a0, a1))
        ]
        for copy in near:
            copy.start()
        load_attention_weights((a2, a3), wqkv, wout, bias, sems)
        for copy in near:
            copy.wait()

    low = hidden_low[...]
    mixed_grad[...] = nt(low, wout[...]).astype(BF16)
    attention_heads_backward(start, short_blocks, meta, stat, qkv, mixed, mixed_grad, low_qkv, delta)
    total = low.astype(F32) + nn(low_near[...], near_qkv[...]) + nn(low_qkv[...], wqkv[...])
    input_rows[...] = total.astype(BF16)
    input_grad[...] = total


def const_spec(shape):
    return pl.BlockSpec(
        shape, lambda *_: (0,) * len(shape), pipeline_mode=pl.Buffered(1)
    )


def any_spec():
    return pl.BlockSpec(memory_space=pl.ANY)


def own_spec(width, start=0):
    return pl.BlockSpec((ROWS, width), lambda i, *_: (i + start, 0))


def whole_call(body, name, which, operands, shapes, scratch=(), keep=False, limit=24):
    moved = sum(v.size * v.dtype.itemsize for v in list(operands) + list(shapes))
    vmem = pl.BlockSpec(memory_space=pltpu.VMEM)
    if not keep:
        operands = [pltpu.with_memory_space_constraint(v, pltpu.VMEM) for v in operands]
        shapes = [pltpu.VMEM(v.shape, v.dtype) for v in shapes]
    return pl.pallas_call(
        body,
        name=name,
        in_specs=[pl.BlockSpec(memory_space=pltpu.SMEM)] + [vmem] * len(operands),
        out_specs=[vmem] * len(shapes),
        out_shape=shapes,
        scratch_shapes=list(scratch),
        compiler_params=pltpu.CompilerParams(vmem_limit_bytes=limit * 1024 * 1024),
        cost_estimate=pl.CostEstimate(flops=0, bytes_accessed=moved, transcendentals=0),
    )(which, *operands)


def spread(body, name, grid, in_specs, out_specs, out_shape, scratch=(), prefetch=0, flops=0, moved=0, exps=0, alias=None):
    return pl.pallas_call(
        body,
        name=name,
        grid_spec=pltpu.PrefetchScalarGridSpec(
            num_scalar_prefetch=prefetch,
            grid=grid,
            in_specs=in_specs,
            out_specs=out_specs,
            scratch_shapes=list(scratch),
        ),
        out_shape=out_shape,
        input_output_aliases=alias or {},
        compiler_params=pltpu.CompilerParams(
            dimension_semantics=("arbitrary",), vmem_limit_bytes=VMEM_LIMIT
        ),
        cost_estimate=pl.CostEstimate(flops=flops, bytes_accessed=moved, transcendentals=exps),
    )


def per_device(
    tokens,
    cotangent,
    short_len,
    long_len,
    short_count,
    long_count,
    query_weight,
    query_bias,
    key_weight,
    value_weight,
    value_bias,
    output_weight,
    output_bias,
    first_gain,
    first_shift,
    up_weight,
    up_bias,
    down_weight,
    down_bias,
    second_gain,
    second_shift,
):
    d = tokens.shape[1]
    width = query_weight.shape[1]
    units = up_weight.shape[1]
    half = 2 * width
    piece_rows = 4 * width + 16
    short_blocks = short_len.shape[0] * SHORT_LEN // (2 * ROWS)
    long_blocks = long_len.shape[0] * LONG_LEN // (2 * ROWS)
    blocks = short_blocks + long_blocks
    rows = blocks * ROWS
    core = lax.axis_index("tensor") % 2
    side = lax.axis_index("dp") % 2
    core_id = core.astype(jnp.int32).reshape(1)
    meta = (core_id, short_len, long_len, short_count, long_count)
    sds = jax.ShapeDtypeStruct

    def swap(values, bit, axis="tensor"):
        size = lax.axis_size(axis)
        return lax.ppermute(values, axis, [(i, i ^ bit) for i in range(size)])

    def after(value, *others):
        return lax.optimization_barrier((value,) + others)[0]

    def global_spec(start=0, flip=0):
        def index(i, core, *_):
            i = i + start
            first = core[0] if flip == 0 else 1 - core[0]
            return (2 * i + jnp.where(i < short_blocks, first, 1 - first), 0)

        return pl.BlockSpec((ROWS, d), index)

    vec_spec = const_spec((8, d))
    row_spec = own_spec(d)

    side_id = side.astype(jnp.int32).reshape(1)
    line_id = (lax.axis_index("dp") // 2).astype(jnp.int32).reshape(1)
    vectors = [query_bias, value_bias, up_bias, output_bias, first_gain, first_shift,
               down_bias, second_gain, second_shift]
    a0, vec = whole_call(
        pack_kernel, "pack", side_id,
        [query_weight.T, key_weight.T, value_weight.T, output_weight, *vectors],
        [sds((piece_rows, d), BF16), sds((8, d), F32)], [pltpu.VMEM((8, d), F32)], True, 61,
    )
    up_split = lax.dynamic_slice_in_dim(up_weight, side * (units // 2), units // 2, 1)
    def boundary(lead, *values):
        out = lax.optimization_barrier((lead,) + values)
        return out[0], list(out[1:])

    a1 = after(swap(a0, 1), up_split)
    a2 = swap(a0, 2)

    weight_scratch = [
        pltpu.VMEM((3 * half, d), BF16),
        pltpu.VMEM((half, d), BF16),
        pltpu.VMEM((32, d), BF16),
    ]
    sems = pltpu.SemaphoreType.DMA((16,))
    stat_scratch = pltpu.VMEM((ROWS, 128), F32)

    def log_spec(start=0):
        return pl.BlockSpec((8, ROWS), lambda i, *_: (i + start, 0))

    head_shapes = [sds((rows, 3 * half), BF16), sds((rows, half), BF16), sds((8 * blocks, ROWS), F32)]
    head_flops = 2 * rows * d * 3 * half + 4 * rows * 320 * half
    qkv_near, mixed_near, stat_near = spread(
        functools.partial(attention_forward_kernel, 0, blocks, short_blocks), "attention_near", (blocks,),
        [global_spec()] + [any_spec()] * 2, [own_spec(3 * half), own_spec(half), log_spec()], head_shapes,
        weight_scratch + [sems, stat_scratch, pltpu.VMEM((3, 1, half), F32)], 5,
        head_flops, rows * d * 8, rows * 320 * 6,
    )(*meta, tokens, a0, a1)

    stat_near, (a2,) = boundary(stat_near, a2)
    u2 = swap(after(up_split, a2), 2)
    d2 = swap(after(down_weight, a2), 2)
    a3 = swap(a2, 1)
    u1 = swap(after(up_weight, a3), 1)

    def far_forward(start, count, extra, alias):
        return spread(
            functools.partial(attention_finish_kernel, start, count, short_blocks), "attention_far", (count,),
            [global_spec(start)] + [any_spec()] * 2 + [own_spec(half, start)] + [any_spec()] * 2 + [vec_spec]
            + [any_spec()] * len(extra),
            [own_spec(3 * half, start), own_spec(half, start), log_spec(start), own_spec(d, start), own_spec(128, start)],
            head_shapes + [sds((rows, d), BF16), sds((rows, 128), F32)],
            weight_scratch + [pltpu.VMEM((half, d), BF16), sems, stat_scratch, pltpu.VMEM((3, 1, half), F32)], 5,
            (head_flops + 2 * rows * d * d) * count // blocks, count * ROWS * d * 10, count * ROWS * 320 * 6, alias,
        )(*meta, tokens, a2, a3, mixed_near, a0, a1, vec, *extra)

    far = list(far_forward(0, short_blocks, [], None))
    far[3], (u2, u1, down_near) = boundary(far[3], u2, u1, down_weight)
    u4 = swap(u2, 1, "dp")
    u3, d1 = swap(u2, 1), swap(down_near, 1)
    qkv_far, mixed_far, stat_far, normed, scale_one = far_forward(
        short_blocks, long_blocks, far, {12 + n: n for n in range(5)}
    )
    normed, (u4, u3, d2, d1) = boundary(normed, u4, u3, d2, d1)
    u5, d3 = swap(u4, 1), swap(d2, 1)
    ups = (up_weight, u1, u2, u3, u4, u5)
    downs = (down_weight, d1, d2, d3)
    bias_spec = pl.BlockSpec((16, d), lambda *_: (4 * width // 16, 0), pipeline_mode=pl.Buffered(1))
    up_specs = [any_spec()] * len(ups)
    down_specs = [any_spec()] * len(downs)
    ffn_scratch = [
        pltpu.VMEM((4, d, units), BF16),
        pltpu.VMEM((4, units, d), BF16),
    ]
    ffn_sems = pltpu.SemaphoreType.DMA((16,))
    whole_out, out_rows, grad_low, slope, down_mine, down_partner, sums_two = spread(
        functools.partial(ffn_forward_kernel, short_blocks), "ffn_forward", (blocks,),
        [row_spec, global_spec()] + up_specs + down_specs + [bias_spec] * 4 + [vec_spec],
        [global_spec(), row_spec, row_spec, own_spec(4 * units)] + [const_spec((units, d))] * 2 + [vec_spec],
        [sds((2 * rows, d), BF16), sds((rows, d), BF16), sds((rows, d), BF16), sds((rows, 4 * units), BF16)]
        + [sds((units, d), BF16)] * 2 + [sds((8, d), F32)],
        [pltpu.VMEM((4, ROWS, units), BF16), pltpu.VMEM((2, units, d), F32), pltpu.VMEM((3, 8, d), F32)]
        + ffn_scratch + [pltpu.VMEM((4, 1, units), F32), pltpu.VMEM((ROWS, d), F32), ffn_sems],
        6, 2 * rows * d * 10 * units, rows * d * 20, rows * 8 * units,
    )(*meta, side_id, normed, cotangent, *ups, *downs, a0, a1, a2, a3, vec)

    custom = lax.axis_size("dp") == 8

    line_steps = (
        [(0, 1), (3, 2)],
        [(1, 2), (2, 1)],
        [(1, 0), (2, 3)],
    )

    def along_line(values, stage):
        pairs = [(2 * i + n, 2 * j + n) for i, j in line_steps[stage] for n in range(2)]
        return lax.ppermute(values, "dp", pairs)

    class Reduction:
        def __init__(self, mine, partner, central):
            self.mine, self.size, self.central = mine, mine.shape[0], central
            self.moved = [swap(partner, 1)]
            self.stage = 0

        def part(self, count):
            return sds((self.size // count, d), BF16)

        def step(self):
            got = self.moved
            stage, self.stage = self.stage, self.stage + 1
            if not custom:
                if stage == 0:
                    total = (self.mine.astype(F32) + got[0].astype(F32)).astype(BF16)
                    self.moved = [lax.psum(total, "dp")]
                return self.moved[0]
            if stage == 0:
                self.keep, send = whole_call(
                    route_halves_kernel, "halves", side_id, [self.mine, got[0]], [self.part(2)] * 2
                )
                sent, self.moved = [send], [swap(send, 1, "dp")]
            elif self.central and stage < 4:
                (self.keep,) = whole_call(add_kernel, "add", line_id, [self.keep, got[0]], [self.part(2)])
                sent, self.moved = [self.keep], [along_line(self.keep, stage - 1)]
            elif self.central and stage == 4:
                (self.keep,) = whole_call(choose_kernel, "choose", line_id, [self.keep, got[0]], [self.part(2)])
                sent, self.moved = [self.keep], [swap(self.keep, 1, "dp")]
            elif stage == 1:
                self.keep, *sent = whole_call(
                    route_quarters_kernel, "quarters", line_id, [self.keep, got[0]], [self.part(8)] * 4
                )
                self.moved = [swap(v, 2 * (k + 1), "dp") for k, v in enumerate(sent)]
            elif stage == 2:
                (self.keep,) = whole_call(add_kernel, "add", line_id, [self.keep, *got], [self.part(8)])
                sent = [self.keep]
                self.moved = [swap(self.keep, 2 * k, "dp") for k in (1, 2, 3)]
            elif stage == 3:
                (self.keep,) = whole_call(
                    join_kernel, "join_quarters", line_id, [self.keep, *got], [self.part(2)]
                )
                sent, self.moved = [self.keep], [swap(self.keep, 1, "dp")]
            return sent[0]

        def finish(self, *sizes):
            shapes = [sds((n, d), F32) for n in sizes]
            if not custom:
                total = self.moved[0].astype(F32)
                cuts = [sum(sizes[:n]) for n in range(len(sizes))]
                return [total[at : at + n] for at, n in zip(cuts, sizes)]
            operands = [self.keep, self.moved[0]]
            return whole_call(
                finish_kernel, "finish", side_id, operands, shapes, [pltpu.VMEM((self.size, d), F32)], True
            )

    def settle(lead, reductions, *extra):
        lead, values = boundary(lead, *[v for r in reductions for v in r.moved], *extra)
        for r in reductions:
            count = len(r.moved)
            r.moved, values = values[:count], values[count:]
        return (lead, *values)

    grad_low, down_mine, down_partner = lax.optimization_barrier((grad_low, down_mine, down_partner))
    down_reduce = Reduction(down_mine, down_partner, True)
    tie = down_reduce.step()
    grad_low = after(grad_low, tie)
    moved_out = swap(after(out_rows, tie), 1)

    pack_rows = units + width + 64
    hidden_low, mine, partner = spread(
        ffn_backward_kernel, "ffn_backward", (blocks,),
        [row_spec, own_spec(4 * units), row_spec, own_spec(128), own_spec(half), vec_spec]
        + up_specs + down_specs + [vec_spec],
        [row_spec] + [const_spec((pack_rows, d))] * 2,
        [sds((rows, d), BF16)] + [sds((pack_rows, d), BF16)] * 2,
        [pltpu.VMEM((2, d, units), F32), pltpu.VMEM((half, d), F32), pltpu.VMEM((7, 8, d), F32),
         pltpu.VMEM((4, ROWS, units), BF16)] + ffn_scratch + [pltpu.VMEM((ROWS, d), F32), ffn_sems],
        1, 2 * rows * d * 10 * units, rows * d * 16, 0,
    )(side_id, grad_low, slope, normed, scale_one, mixed_near, sums_two, *ups, *downs, vec)
    hidden_low, mine, partner, moved_out = settle(hidden_low, [down_reduce], mine, partner, moved_out)
    tie = down_reduce.step()
    partner = after(partner, tie)
    up_reduce = Reduction(mine, partner, True)
    tie = up_reduce.step()
    hidden_low = after(hidden_low, tie)

    qkv_rows = 3 * width + 64
    sums = [sds((3, half, d), F32), sds((2, 8, half), F32)]
    sum_specs = [const_spec(v.shape) for v in sums]

    def near_backward(start, count, extra, extra_specs, outs, out_specs, alias):
        return spread(
            functools.partial(attention_backward_kernel, start, short_blocks), "attention_near_backward", (count,),
            [own_spec(d, start), log_spec(start), own_spec(3 * half, start), own_spec(half, start), global_spec(start)]
            + [any_spec()] * 2 + extra_specs,
            [own_spec(3 * half)] + out_specs,
            [sds((count * ROWS, 3 * half), BF16)] + outs,
            weight_scratch + [sems, pltpu.VMEM((ROWS, half), BF16), pltpu.VMEM((8, ROWS), F32),
                              pltpu.VMEM((3, half, d), F32), pltpu.VMEM((2, 8, half), F32)],
            5, count * ROWS * (10 * d * half + 3200 * half), count * ROWS * d * 16, count * ROWS * 320 * 6,
        )(*meta, hidden_low, stat_near, qkv_near, mixed_near, tokens, a0, a1, *extra)

    low_short, *sums_short = near_backward(0, short_blocks, [], [], sums, sum_specs, None)
    (low_short,) = settle(low_short, [down_reduce, up_reduce])
    tie = down_reduce.step()
    tie_two = up_reduce.step()
    sums_short[1] = after(sums_short[1], tie, tie_two)
    low_long, mine, partner = near_backward(
        short_blocks, long_blocks, sums_short, sum_specs,
        [sds((qkv_rows, d), BF16)] * 2, [const_spec((qkv_rows, d))] * 2, None,
    )
    low_long, mine, partner = settle(low_long, [down_reduce, up_reduce], mine, partner)
    ties = [down_reduce.step(), up_reduce.step()]
    qkv_reduce = Reduction(mine, after(partner, *ties), False)
    ties += [qkv_reduce.step()]

    def far_backward(start, count, low_near, extra, alias):
        return spread(
            functools.partial(attention_input_kernel, start, short_blocks), "attention_far_backward", (count,),
            [own_spec(d, start), log_spec(start), own_spec(3 * half, start), own_spec(half, start), own_spec(3 * half)]
            + [any_spec()] * (4 + len(extra)),
            [own_spec(d, start), global_spec(start)], [sds((rows, d), BF16), sds((2 * rows, d), F32)],
            weight_scratch + [pltpu.VMEM((3 * half, d), BF16), sems, pltpu.VMEM((ROWS, 3 * half), BF16),
                              pltpu.VMEM((ROWS, half), BF16), pltpu.VMEM((8, ROWS), F32)],
            5, count * ROWS * (14 * d * half + 3200 * half), count * ROWS * d * 16, count * ROWS * 320 * 6, alias,
        )(*meta, hidden_low, stat_far, qkv_far, mixed_far, low_near, a2, a3, a0, a1, *extra)

    low_short = after(low_short, *ties)
    rows_short, whole_in = far_backward(0, short_blocks, low_short, [], None)
    (rows_short,) = settle(rows_short, [down_reduce, up_reduce, qkv_reduce])
    ties = [qkv_reduce.step(), up_reduce.step(), down_reduce.step()]
    low_long = after(low_long, *ties)
    rows_all, whole_in = far_backward(
        short_blocks, long_blocks, low_long, [rows_short, whole_in], {14: 0, 15: 1}
    )
    (rows_all,) = settle(rows_all, [down_reduce, up_reduce, qkv_reduce])
    tie = qkv_reduce.step()
    tie = after(tie, up_reduce.step())
    down_reduce.moved[0] = after(down_reduce.moved[0], tie)
    (grad_down,) = down_reduce.finish(units)
    moved_rows = swap(after(rows_all, tie), 1)

    def place(whole, other, start, count):
        return spread(
            place_kernel, "place", (count,), [own_spec(d), any_spec()], global_spec(start, 1),
            sds(whole.shape, whole.dtype), (), 1, 0, other.size * 6, 0, {2: 0},
        )(core_id, other, whole)

    layer_output = place(whole_out, after(moved_out, tie), 0, blocks)
    layer_output, moved_rows = settle(layer_output, [qkv_reduce], moved_rows)
    tie = qkv_reduce.step()
    input_grad = place(whole_in, after(moved_rows, tie), 0, blocks)
    up_reduce.moved[0] = after(up_reduce.moved[0], tie)
    grad_up, grad_out, small = up_reduce.finish(units, width, 16)
    grad_up, input_grad = settle(grad_up, [qkv_reduce], input_grad)
    grad_query, grad_key, grad_value, heads = qkv_reduce.finish(width, width, width, 16)
    return (
        layer_output,
        input_grad,
        grad_query.T,
        heads[0, :width],
        grad_key.T,
        grad_value.T,
        heads[1, :width],
        grad_out,
        small[5],
        small[3],
        small[4],
        grad_up,
        small[6],
        grad_down,
        small[2],
        small[0],
        small[1],
    )

def solution(mesh):
    return jax.shard_map(
        per_device,
        mesh=mesh,
        in_specs=(
            P("dp", None),
            P("dp", None),
            P("dp"),
            P("dp"),
            P("dp"),
            P("dp"),
            P(None, "tensor"),
            P("tensor"),
            P(None, "tensor"),
            P(None, "tensor"),
            P("tensor"),
            P("tensor", None),
            P(),
            P(),
            P(),
            P(None, "tensor"),
            P("tensor"),
            P("tensor", None),
            P(),
            P(),
            P(),
        ),
        out_specs=(
            P("dp", None),
            P("dp", None),
            P(None, "tensor"),
            P("tensor"),
            P(None, "tensor"),
            P(None, "tensor"),
            P("tensor"),
            P("tensor", None),
            P(),
            P(),
            P(),
            P(None, "tensor"),
            P("tensor"),
            P("tensor", None),
            P(),
            P(),
            P(),
        ),
        check_vma=False,
    )
```

profile of v0, /device:TPU:0, one launch (start us, length us, event | category | flops | bytes accessed | tf_op | source)
XLA Modules:
  0.0 315.0 jit_solution(10395760772328715770)
XLA Ops:
  0.7 2.5 pack.1
  3.7 2.6 collective-permute-start.1
  7.6 1.1 constant_dynamic-slice_fusion
  8.7 1.0 copy-done.7
  9.7 21.5 %attention_near.1 = (bf16[2048,1152]{1,0:T(8,128)(2,1)}, bf16[2048,384]{1,0:T(8,128)(2,1)}, f32[32,512]{1,0:T(8,128)}) custom-call(s32[1]{0:T(128)} %bitcast.core, s32[16]{0:T(128)} %slen.15, s32[4]{0:T(128)} %llen.15, s32[1]{0:T(128)S(6)} %copy.56.scount, s32[1]{0:T(128)S(6)} %copy.57.lcount, bf16[4096,768]{1,0:T(8,128)(2,1)} %x.9, ...), custom_call_target="tpu_custom_call" | custom-call | flops 4630511616 | bytes 12582912 | tf_op jit(solution)/shard_map/attention_near/pallas_call | solution.py:769
  31.2 2.4 collective-permute-done.1.a2.rest_12_
  33.6 2.9 collective-permute-done.2.a3.rest_13_
  36.6 1.8 collective-permute-start.3
  38.6 14.8 %attention_far.2 = (bf16[2048,1152]{1,0:T(8,128)(2,1)}, bf16[2048,384]{1,0:T(8,128)(2,1)}, f32[32,512]{1,0:T(8,128)}, bf16[2048,768]{1,0:T(8,128)(2,1)}, f32[2048,128]{1,0:T(8,128)}) custom-call(s32[1]{0:T(128)} %bitcast.core, s32[16]{0:T(128)} %slen.15, s32[4]{0:T(128)} %llen.15, s32[1]{0:T(128)S(6)} %copy.56.scount, s32[1]{0:T(128)S(6)} %copy.57.lcount, ...), custom_call_target="tpu_custom_call" | custom-call | flops 3523215360 | bytes 7864320 | tf_op jit(solution)/shard_map/attention_far/pallas_call | solution.py:783
  54.1 1.7 collective-permute-start.5
  55.8 17.2 %attention_far.3 = (bf16[2048,1152]{1,0:T(8,128)(2,1)}, bf16[2048,384]{1,0:T(8,128)(2,1)}, f32[32,512]{1,0:T(8,128)}, bf16[2048,768]{1,0:T(8,128)(2,1)}, f32[2048,128]{1,0:T(8,128)}) custom-call(s32[1]{0:T(128)} %bitcast.core, s32[16]{0:T(128)} %slen.15, s32[4]{0:T(128)} %llen.15, ...), custom_call_target="tpu_custom_call", output_to_operand_aliasing={{0}: (12, {}), {1}: (13, {}), {2}: (14, {}), {3}: (15, {}),... | custom-call | flops 3523215360 | bytes 7864320 | tf_op jit(solution)/shard_map/attention_far/pallas_call | solution.py:783
  73.0 4.5 %collective-permute-done.7.rest_8_ = bf16[768,768]{1,0:T(8,128)(2,1)} collective-permute-done((bf16[768,768]{1,0:T(8,128)(2,1)}, bf16[768,768]{1,0:T(8,128)(2,1)}, u32[]{:S(2)}, u32[]{:S(2)}) %collective-permute-start.7) | collective-permute-done | bytes 1179680 | tf_op jit(solution)/shard_map/ppermute | solution.py:723
  78.2 3.1 collective-permute-done.9.rest_5_
  81.3 0.8 copy-done.15
  82.2 1.0 copy-done.11
  83.2 46.3 %ffn_forward.1 = (bf16[4096,768]{1,0:T(8,128)(2,1)}, bf16[2048,768]{1,0:T(8,128)(2,1)}, bf16[2048,768]{1,0:T(8,128)(2,1)}, bf16[2048,3072]{1,0:T(8,128)(2,1)}, b...) custom-call(s32[1]{0:T(128)} %bitcast.core, s32[16]{0:T(128)} %slen.15, s32[4]{0:T(128)} %llen.15, ...), custom_call_target="tpu_custom_call" | custom-call | flops 24159191040 | bytes 31457280 | tf_op jit(solution)/shard_map/ffn_forward/pallas_call | solution.py:812
  129.7 2.9 collective-permute-done.11.partner
  132.6 1.3 copy-done.1
  134.4 1.7 collective-permute-start.12
  136.1 40.4 %ffn_backward.1 = (bf16[2048,768]{1,0:T(8,128)(2,1)}, bf16[1024,768]{1,0:T(8,128)(2,1)}, bf16[1024,768]{1,0:T(8,128)(2,1)}) custom-call(s32[1]{0:T(128)} %bitcast.1.at.side, bf16[2048,768]{1,0:T(8,128)(2,1)} %get-tuple-element.163.grad_low, bf16[2048,3072]{1,0:T(8,128)(2,1)} %get-tuple-element.164.slope, bf16[2048,768]{1,0:T(8,128)(2,1)} %get-tuple-element.150.normed, ...), custom_call_target="tpu_custom_call" | custom-call | flops 24159191040 | bytes 25165824 | tf_op jit(solution)/shard_map/ffn_backward/pallas_call | solution.py:904
  176.9 3.5 %collective-permute-done.14.partner = bf16[1024,768]{1,0:T(8,128)(2,1)S(1)} collective-permute-done((bf16[1024,768]{1,0:T(8,128)(2,1)}, bf16[1024,768]{1,0:T(8,128)(2,1)S(1)}, u32[]{:S(2)}, u32[]{:S(2)}) %collective-permute-start.14) | collective-permute-done | bytes 1572896 | tf_op jit(solution)/shard_map/ppermute | solution.py:723
  181.3 3.8 %collective-permute-start.15 = (bf16[384,768]{1,0:T(8,128)(2,1)S(1)}, bf16[384,768]{1,0:T(8,128)(2,1)S(1)}, u32[]{:S(2)}, u32[]{:S(2)}) collective-permute-start(bf16[384,768]{1,0:T(8,128)(2,1)S(1)} %add.28.refs_0_), channel_id=1, source_target_pairs={{0,8},{4,12},{24,16},{28,20},{1,9},{5,13},{25,17},{29,21},{2,10},{... | collective-permute-start | bytes 1769480 | tf_op jit(solution)/shard_map/ppermute | solution.py:833
  185.0 15.5 %attention_near_backward.2 = (bf16[1024,1152]{1,0:T(8,128)(2,1)}, f32[3,384,768]{2,1,0:T(8,128)}, f32[2,8,384]{2,1,0:T(8,128)}) custom-call(s32[1]{0:T(128)} %bitcast.core, s32[16]{0:T(128)} %slen.15, s32[4]{0:T(128)} %llen.15, s32[1]{0:T(128)S(6)} %copy.56.scount, s32[1]{0:T(128)S(6)} %copy.57.lcount, bf16[2048,768]{1,0:T(8,128)(2,1)} %get-tuple-element.180.hidden_low, ...), custom_call_target="tpu_custom_call" | custom-call | flops 4278190080 | bytes 12582912 | tf_op jit(solution)/shard_map/attention_near_backward/pallas_call | solution.py:926
  200.8 3.5 %collective-permute-start.18 = (bf16[512,768]{1,0:T(8,128)(2,1)S(1)}, bf16[512,768]{1,0:T(8,128)(2,1)S(1)}, u32[]{:S(2)}, u32[]{:S(2)}) collective-permute-start(bf16[512,768]{1,0:T(8,128)(2,1)S(1)} %add.30.refs_0_), channel_id=1, source_target_pairs={{0,8},{4,12},{24,16},{28,20},{1,9},{5,13},{25,17},{29,21},{2,10},{... | collective-permute-start | bytes 2359304 | tf_op jit(solution)/shard_map/ppermute | solution.py:833
  205.2 21.8 %attention_near_backward.3 = (bf16[1024,1152]{1,0:T(8,128)(2,1)}, bf16[640,768]{1,0:T(8,128)(2,1)}, bf16[640,768]{1,0:T(8,128)(2,1)}) custom-call(s32[1]{0:T(128)} %bitcast.core, s32[16]{0:T(128)} %slen.15, s32[4]{0:T(128)} %llen.15, s32[1]{0:T(128)S(6)} %copy.56.scount, s32[1]{0:T(128)S(6)} %copy.57.lcount, ...), custom_call_target="tpu_custom_call" | custom-call | flops 4278190080 | bytes 12582912 | tf_op jit(solution)/shard_map/attention_near_backward/pallas_call | solution.py:926
  227.4 0.7 copy-done.12
  228.2 0.7 collective-permute-start.21
  228.9 1.3 collective-permute-start.20
  230.8 1.1 halves.5
  232.4 16.9 %attention_far_backward.2 = (bf16[2048,768]{1,0:T(8,128)(2,1)}, f32[4096,768]{1,0:T(8,128)}) custom-call(s32[1]{0:T(128)} %bitcast.core, s32[16]{0:T(128)} %slen.15, s32[4]{0:T(128)} %llen.15, s32[1]{0:T(128)S(6)} %copy.56.scount, s32[1]{0:T(128)S(6)} %copy.57.lcount, bf16[2048,768]{1,0:T(8,128)(2,1)} %get-tuple-element.180.hidden_low, ...), custom_call_target="tpu_custom_call" | custom-call | flops 5486149632 | bytes 12582912 | tf_op jit(solution)/shard_map/attention_far_backward/pallas_call | solution.py:952
  249.3 0.8 copy-done.5
  250.3 1.3 collective-permute-start.24
  251.7 1.5 collective-permute-start.23
  253.3 3.4 %collective-permute-start.25 = (bf16[80,768]{1,0:T(8,128)(2,1)S(1)}, bf16[80,768]{1,0:T(8,128)(2,1)S(1)}, u32[]{:S(2)}, u32[]{:S(2)}) collective-permute-start(bf16[80,768]{1,0:T(8,128)(2,1)S(1)} %get-tuple-element.209), channel_id=1, source_target_pairs={{0,8},{4,12},{8,0},{12,4},{16,24},{20,28},{24,16},{28,20},{1,9},{5... | collective-permute-start | bytes 368648 | tf_op jit(solution)/shard_map/ppermute | solution.py:723
  256.7 1.1 collective-permute-start.26
  257.8 1.4 collective-permute-start.27
  259.2 22.9 %attention_far_backward.3 = (bf16[2048,768]{1,0:T(8,128)(2,1)}, f32[4096,768]{1,0:T(8,128)}) custom-call(s32[1]{0:T(128)} %bitcast.core, s32[16]{0:T(128)} %slen.15, s32[4]{0:T(128)} %llen.15, s32[1]{0:T(128)S(6)} %copy.56.scount, s32[1]{0:T(128)S(6)} %copy.57.lcount, ...), custom_call_target="tpu_custom_call", output_to_operand_aliasing={{0}: (14, {}), {1}: (15, {})} | custom-call | flops 5486149632 | bytes 12582912 | tf_op jit(solution)/shard_map/attention_far_backward/pallas_call | solution.py:952
  283.0 2.4 collective-permute-start.30
  285.5 1.9 collective-permute-start.28
  287.4 4.2 %place.2 = bf16[4096,768]{1,0:T(8,128)(2,1)} custom-call(s32[1]{0:T(128)} %bitcast.core, bf16[2048,768]{1,0:T(8,128)(2,1)} %collective-permute-done.13.other, bf16[4096,768]{1,0:T(8,128)(2,1)} %get-tuple-element.224.whole), custom_call_target="tpu_custom_call", output_to_operand_aliasing={{}: (2, {})} | custom-call | bytes 9437184 | tf_op jit(solution)/shard_map/place/pallas_call | solution.py:978
  291.6 5.2 %collective-permute-done.29.refs_2_ = bf16[80,768]{1,0:T(8,128)(2,1)S(1)} collective-permute-done((bf16[80,768]{1,0:T(8,128)(2,1)S(1)}, bf16[80,768]{1,0:T(8,128)(2,1)S(1)}, u32[]{:S(2)}, u32[]{:S(2)}) %collective-permute-start.29) | collective-permute-done | bytes 122912 | tf_op jit(solution)/shard_map/ppermute | solution.py:723
  296.8 1.5 collective-permute-start.33
  298.3 1.8 finish.5
  300.1 2.7 collective-permute-done.32.other
  302.8 2.1 finish.3
  304.9 5.0 %place.3 = f32[4096,768]{1,0:T(8,128)} custom-call(s32[1]{0:T(128)} %bitcast.core, bf16[2048,768]{1,0:T(8,128)(2,1)} %collective-permute-done.31.other, f32[4096,768]{1,0:T(8,128)} %get-tuple-element.235.whole), custom_call_target="tpu_custom_call", output_to_operand_aliasing={{}: (2, {})} | custom-call | bytes 9437184 | tf_op jit(solution)/shard_map/place/pallas_call | solution.py:978
  310.6 2.3 collective-permute-done.33.other
  312.9 1.5 finish.4
  (84 shorter events, 9.1 us)
Async XLA Ops:
  3.2 5.5 %collective-permute-start = (bf16[784,768]{1,0:T(8,128)(2,1)}, bf16[784,768]{1,0:T(8,128)(2,1)S(1)}, u32[]{:S(2)}, u32[]{:S(2)}) collective-permute-start(bf16[784,768]{1,0:T(8,128)(2,1)} %get-tuple-element.132.a0.rest_10_), channel_id=1, source_target_pairs={{0,1},{1,0},{2,3},{3,2},{4,5},{5,4},{6,7},{7,6},{8,9},{9,8},{10,11... | collective-permute-start | bytes 3612680 | tf_op jit(solution)/shard_map/ppermute | solution.py:723
  3.7 29.9 %collective-permute-start.1 = (bf16[784,768]{1,0:T(8,128)(2,1)}, bf16[784,768]{1,0:T(8,128)(2,1)S(1)}, u32[]{:S(2)}, u32[]{:S(2)}) collective-permute-start(bf16[784,768]{1,0:T(8,128)(2,1)} %get-tuple-element.132.a0.rest_10_), channel_id=1, source_target_pairs={{0,2},{1,3},{2,0},{3,1},{4,6},{5,7},{6,4},{7,5},{8,10},{9,11},{10,... | collective-permute-start | bytes 3612680 | tf_op jit(solution)/shard_map/ppermute | solution.py:723
  8.7 1.0 copy-start.7
  33.6 5.1 %copy-start.8 = (bf16[784,768]{1,0:T(8,128)(2,1)}, bf16[784,768]{1,0:T(8,128)(2,1)S(1)}, u32[]{:S(2)}) copy-start(bf16[784,768]{1,0:T(8,128)(2,1)S(1)} %collective-permute-done.1.a2.rest_12_) | copy-start | bytes 3612676
  33.6 2.9 collective-permute-start.2
  36.4 2.2 copy-start.9
  36.4 17.0 %collective-permute-start.4 = (bf16[768,768]{1,0:T(8,128)(2,1)}, bf16[768,768]{1,0:T(8,128)(2,1)}, u32[]{:S(2)}, u32[]{:S(2)}) collective-permute-start(bf16[768,768]{1,0:T(8,128)(2,1)} %rest_0_.3), channel_id=1, source_target_pairs={{0,1},{1,0},{2,3},{3,2},{4,5},{5,4},{6,7},{7,6},{8,9},{9,8},{10,11... | collective-permute-start | bytes 3538952 | tf_op jit(solution)/shard_map/ppermute | solution.py:723
  36.6 16.9 %collective-permute-start.3 = (bf16[768,384]{1,0:T(8,128)(2,1)S(1)}, bf16[768,384]{1,0:T(8,128)(2,1)}, u32[]{:S(2)}, u32[]{:S(2)}) collective-permute-start(bf16[768,384]{1,0:T(8,128)(2,1)S(1)} %constant_dynamic-slice_fusion), channel_id=1, source_target_pairs={{0,2},{1,3},{2,0},{3,1},{4,6},{5,7},{6,4},{7,5},{8,10},{9,11},{10,... | collective-permute-start | bytes 1769480 | tf_op jit(solution)/shard_map/ppermute | solution.py:723
  38.4 39.2 %collective-permute-start.7 = (bf16[768,768]{1,0:T(8,128)(2,1)}, bf16[768,768]{1,0:T(8,128)(2,1)}, u32[]{:S(2)}, u32[]{:S(2)}) collective-permute-start(bf16[768,768]{1,0:T(8,128)(2,1)} %rest_6_.3), channel_id=1, source_target_pairs={{0,2},{1,3},{2,0},{3,1},{4,6},{5,7},{6,4},{7,5},{8,10},{9,11},{10,... | collective-permute-start | bytes 3538952 | tf_op jit(solution)/shard_map/ppermute | solution.py:723
  53.5 24.1 %collective-permute-start.8 = (bf16[768,768]{1,0:T(8,128)(2,1)}, bf16[768,768]{1,0:T(8,128)(2,1)S(1)}, u32[]{:S(2)}, u32[]{:S(2)}) collective-permute-start(bf16[768,768]{1,0:T(8,128)(2,1)} %rest_6_.3), channel_id=1, source_target_pairs={{0,1},{1,0},{2,3},{3,2},{4,5},{5,4},{6,7},{7,6},{8,9},{9,8},{10,11... | collective-permute-start | bytes 3538952 | tf_op jit(solution)/shard_map/ppermute | solution.py:723
  53.6 24.0 %collective-permute-start.6 = (bf16[768,384]{1,0:T(8,128)(2,1)}, bf16[768,384]{1,0:T(8,128)(2,1)S(1)}, u32[]{:S(2)}, u32[]{:S(2)}) collective-permute-start(bf16[768,384]{1,0:T(8,128)(2,1)} %collective-permute-done.3.rest_2_), channel_id=1, source_target_pairs={{0,1},{1,0},{2,3},{3,2},{4,5},{5,4},{6,7},{7,6},{8,9},{9,8},{10,11... | collective-permute-start | bytes 1769480 | tf_op jit(solution)/shard_map/ppermute | solution.py:723
  54.1 23.5 %collective-permute-start.5 = (bf16[768,384]{1,0:T(8,128)(2,1)}, bf16[768,384]{1,0:T(8,128)(2,1)S(1)}, u32[]{:S(2)}, u32[]{:S(2)}) collective-permute-start(bf16[768,384]{1,0:T(8,128)(2,1)} %collective-permute-done.3.rest_2_), channel_id=1, source_target_pairs={{0,4},{4,0},{8,12},{12,8},{16,20},{20,16},{24,28},{28,24},{1,5},{5... | collective-permute-start | bytes 1769480 | tf_op jit(solution)/shard_map/ppermute | solution.py:723
  77.6 4.6 %copy-start.13 = (bf16[768,384]{1,0:T(8,128)(2,1)}, bf16[768,384]{1,0:T(8,128)(2,1)S(1)}, u32[]{:S(2)}) copy-start(bf16[768,384]{1,0:T(8,128)(2,1)S(1)} %collective-permute-done.6.rest_3_) | copy-start | bytes 1769476
  77.6 4.6 %copy-start.14 = (bf16[768,384]{1,0:T(8,128)(2,1)}, bf16[768,384]{1,0:T(8,128)(2,1)S(1)}, u32[]{:S(2)}) copy-start(bf16[768,384]{1,0:T(8,128)(2,1)S(1)} %collective-permute-done.5.rest_4_) | copy-start | bytes 1769476
  77.6 4.5 %copy-start.10 = (bf16[768,768]{1,0:T(8,128)(2,1)}, bf16[768,768]{1,0:T(8,128)(2,1)S(1)}, u32[]{:S(2)}) copy-start(bf16[768,768]{1,0:T(8,128)(2,1)S(1)} %collective-permute-done.8.rest_7_) | copy-start | bytes 3538948
  77.6 4.5 %collective-permute-start.10 = (bf16[768,768]{1,0:T(8,128)(2,1)}, bf16[768,768]{1,0:T(8,128)(2,1)S(1)}, u32[]{:S(2)}, u32[]{:S(2)}) collective-permute-start(bf16[768,768]{1,0:T(8,128)(2,1)} %collective-permute-done.7.rest_8_), channel_id=1, source_target_pairs={{0,1},{1,0},{2,3},{3,2},{4,5},{5,4},{6,7},{7,6},{8,9},{9,8},{10,11... | collective-permute-start | bytes 3538952 | tf_op jit(solution)/shard_map/ppermute | solution.py:723
  77.7 3.6 %collective-permute-start.9 = (bf16[768,384]{1,0:T(8,128)(2,1)S(1)}, bf16[768,384]{1,0:T(8,128)(2,1)S(1)}, u32[]{:S(2)}, u32[]{:S(2)}) collective-permute-start(bf16[768,384]{1,0:T(8,128)(2,1)S(1)} %collective-permute-done.5.rest_4_), channel_id=1, source_target_pairs={{0,1},{1,0},{2,3},{3,2},{4,5},{5,4},{6,7},{7,6},{8,9},{9,8},{10,11... | collective-permute-start | bytes 1769480 | tf_op jit(solution)/shard_map/ppermute | solution.py:723
  82.1 1.0 copy-start.11
  129.5 3.1 collective-permute-start.11
  132.6 1.3 copy-start.1
  134.2 42.3 %collective-permute-start.13 = (bf16[2048,768]{1,0:T(8,128)(2,1)}, bf16[2048,768]{1,0:T(8,128)(2,1)}, u32[]{:S(2)}, u32[]{:S(2)}) collective-permute-start(bf16[2048,768]{1,0:T(8,128)(2,1)} %get-tuple-element.171), channel_id=1, source_target_pairs={{0,1},{1,0},{2,3},{3,2},{4,5},{5,4},{6,7},{7,6},{8,9},{9,8},{10,11... | collective-permute-start | bytes 9437192 | tf_op jit(solution)/shard_map/ppermute | solution.py:723
  134.4 42.1 %collective-permute-start.12 = (bf16[384,768]{1,0:T(8,128)(2,1)S(1)}, bf16[384,768]{1,0:T(8,128)(2,1)S(1)}, u32[]{:S(2)}, u32[]{:S(2)}) collective-permute-start(bf16[384,768]{1,0:T(8,128)(2,1)S(1)} %get-tuple-element.162), channel_id=1, source_target_pairs={{0,4},{4,0},{8,12},{12,8},{16,20},{20,16},{24,28},{28,24},{1,5},{5... | collective-permute-start | bytes 1769480 | tf_op jit(solution)/shard_map/ppermute | solution.py:723
  176.5 3.9 %copy-start = (bf16[1024,768]{1,0:T(8,128)(2,1)S(1)}, bf16[1024,768]{1,0:T(8,128)(2,1)}, u32[]{:S(2)}) copy-start(bf16[1024,768]{1,0:T(8,128)(2,1)} %get-tuple-element.174.mine) | copy-start | bytes 4718596
  176.7 3.7 %collective-permute-start.14 = (bf16[1024,768]{1,0:T(8,128)(2,1)}, bf16[1024,768]{1,0:T(8,128)(2,1)S(1)}, u32[]{:S(2)}, u32[]{:S(2)}) collective-permute-start(bf16[1024,768]{1,0:T(8,128)(2,1)} %get-tuple-element.178), channel_id=1, source_target_pairs={{0,1},{1,0},{2,3},{3,2},{4,5},{5,4},{6,7},{7,6},{8,9},{9,8},{10,11... | collective-permute-start | bytes 4718600 | tf_op jit(solution)/shard_map/ppermute | solution.py:723
  180.9 19.7 %collective-permute-start.16 = (bf16[512,768]{1,0:T(8,128)(2,1)S(1)}, bf16[512,768]{1,0:T(8,128)(2,1)S(1)}, u32[]{:S(2)}, u32[]{:S(2)}) collective-permute-start(bf16[512,768]{1,0:T(8,128)(2,1)S(1)} %get-tuple-element.179), channel_id=1, source_target_pairs={{0,4},{4,0},{8,12},{12,8},{16,20},{20,16},{24,28},{28,24},{1,5},{5... | collective-permute-start | bytes 2359304 | tf_op jit(solution)/shard_map/ppermute | solution.py:723
  181.3 19.3 %collective-permute-start.15 = (bf16[384,768]{1,0:T(8,128)(2,1)S(1)}, bf16[384,768]{1,0:T(8,128)(2,1)S(1)}, u32[]{:S(2)}, u32[]{:S(2)}) collective-permute-start(bf16[384,768]{1,0:T(8,128)(2,1)S(1)} %add.28.refs_0_), channel_id=1, source_target_pairs={{0,8},{4,12},{24,16},{28,20},{1,9},{5,13},{25,17},{29,21},{2,10},{... | collective-permute-start | bytes 1769480 | tf_op jit(solution)/shard_map/ppermute | solution.py:833
  200.8 26.2 %collective-permute-start.18 = (bf16[512,768]{1,0:T(8,128)(2,1)S(1)}, bf16[512,768]{1,0:T(8,128)(2,1)S(1)}, u32[]{:S(2)}, u32[]{:S(2)}) collective-permute-start(bf16[512,768]{1,0:T(8,128)(2,1)S(1)} %add.30.refs_0_), channel_id=1, source_target_pairs={{0,8},{4,12},{24,16},{28,20},{1,9},{5,13},{25,17},{29,21},{2,10},{... | collective-permute-start | bytes 2359304 | tf_op jit(solution)/shard_map/ppermute | solution.py:833
  204.5 22.5 %collective-permute-start.17 = (bf16[384,768]{1,0:T(8,128)(2,1)S(1)}, bf16[384,768]{1,0:T(8,128)(2,1)S(1)}, u32[]{:S(2)}, u32[]{:S(2)}) collective-permute-start(bf16[384,768]{1,0:T(8,128)(2,1)S(1)} %add.29.refs_0_), channel_id=1, source_target_pairs={{8,16},{12,20},{16,8},{20,12},{9,17},{13,21},{17,9},{21,13},{10,18... | collective-permute-start | bytes 1769480 | tf_op jit(solution)/shard_map/ppermute | solution.py:833
  227.0 1.2 copy-start.12
  227.0 3.8 %copy-start.2 = (bf16[640,768]{1,0:T(8,128)(2,1)S(1)}, bf16[640,768]{1,0:T(8,128)(2,1)}, u32[]{:S(2)}) copy-start(bf16[640,768]{1,0:T(8,128)(2,1)} %get-tuple-element.193.mine) | copy-start | bytes 2949124
  228.2 2.6 collective-permute-start.19
  228.2 21.1 %collective-permute-start.21 = (bf16[512,768]{1,0:T(8,128)(2,1)S(1)}, bf16[512,768]{1,0:T(8,128)(2,1)S(1)}, u32[]{:S(2)}, u32[]{:S(2)}) collective-permute-start(bf16[512,768]{1,0:T(8,128)(2,1)S(1)} %add.32.refs_0_), channel_id=1, source_target_pairs={{8,16},{12,20},{16,8},{20,12},{9,17},{13,21},{17,9},{21,13},{10,18... | collective-permute-start | bytes 2359304 | tf_op jit(solution)/shard_map/ppermute | solution.py:833
  228.9 20.4 %collective-permute-start.20 = (bf16[384,768]{1,0:T(8,128)(2,1)S(1)}, bf16[384,768]{1,0:T(8,128)(2,1)S(1)}, u32[]{:S(2)}, u32[]{:S(2)}) collective-permute-start(bf16[384,768]{1,0:T(8,128)(2,1)S(1)} %add.31.own), channel_id=1, source_target_pairs={{8,0},{12,4},{16,24},{20,28},{9,1},{13,5},{17,25},{21,29},{10,2},{... | collective-permute-start | bytes 1769480 | tf_op jit(solution)/shard_map/ppermute | solution.py:833
  231.8 17.4 %copy-start.3 = (bf16[320,768]{1,0:T(8,128)(2,1)}, bf16[320,768]{1,0:T(8,128)(2,1)S(1)}, u32[]{:S(2)}) copy-start(bf16[320,768]{1,0:T(8,128)(2,1)S(1)} %get-tuple-element.198.keep) | copy-start | bytes 1474564
  231.8 17.5 %collective-permute-start.22 = (bf16[320,768]{1,0:T(8,128)(2,1)}, bf16[320,768]{1,0:T(8,128)(2,1)S(1)}, u32[]{:S(2)}, u32[]{:S(2)}) collective-permute-start(bf16[320,768]{1,0:T(8,128)(2,1)} %get-tuple-element.203), channel_id=1, source_target_pairs={{0,4},{4,0},{8,12},{12,8},{16,20},{20,16},{24,28},{28,24},{1,5},{5... | collective-permute-start | bytes 1474568 | tf_op jit(solution)/shard_map/ppermute | solution.py:723
  249.3 3.9 %copy-start.4 = (bf16[320,768]{1,0:T(8,128)(2,1)S(1)}, bf16[320,768]{1,0:T(8,128)(2,1)}, u32[]{:S(2)}) copy-start(bf16[320,768]{1,0:T(8,128)(2,1)} %copy-done.3) | copy-start | bytes 1474564
  250.1 3.1 copy-start.6
  250.3 31.9 %collective-permute-start.24 = (bf16[512,768]{1,0:T(8,128)(2,1)S(1)}, bf16[512,768]{1,0:T(8,128)(2,1)S(1)}, u32[]{:S(2)}, u32[]{:S(2)}) collective-permute-start(bf16[512,768]{1,0:T(8,128)(2,1)S(1)} %add.33.own), channel_id=1, source_target_pairs={{8,0},{12,4},{16,24},{20,28},{9,1},{13,5},{17,25},{21,29},{10,2},{... | collective-permute-start | bytes 2359304 | tf_op jit(solution)/shard_map/ppermute | solution.py:833
  251.7 30.5 %collective-permute-start.23 = (bf16[384,768]{1,0:T(8,128)(2,1)S(1)}, bf16[384,768]{1,0:T(8,128)(2,1)S(1)}, u32[]{:S(2)}, u32[]{:S(2)}) collective-permute-start(bf16[384,768]{1,0:T(8,128)(2,1)S(1)} %choose.2.own), channel_id=1, source_target_pairs={{0,4},{4,0},{8,12},{12,8},{16,20},{20,16},{24,28},{28,24},{1,5},{5... | collective-permute-start | bytes 1769480 | tf_op jit(solution)/shard_map/ppermute | solution.py:723
  253.3 28.8 %collective-permute-start.25 = (bf16[80,768]{1,0:T(8,128)(2,1)S(1)}, bf16[80,768]{1,0:T(8,128)(2,1)S(1)}, u32[]{:S(2)}, u32[]{:S(2)}) collective-permute-start(bf16[80,768]{1,0:T(8,128)(2,1)S(1)} %get-tuple-element.209), channel_id=1, source_target_pairs={{0,8},{4,12},{8,0},{12,4},{16,24},{20,28},{24,16},{28,20},{1,9},{5... | collective-permute-start | bytes 368648 | tf_op jit(solution)/shard_map/ppermute | solution.py:723
  256.7 25.4 %collective-permute-start.26 = (bf16[80,768]{1,0:T(8,128)(2,1)S(1)}, bf16[80,768]{1,0:T(8,128)(2,1)S(1)}, u32[]{:S(2)}, u32[]{:S(2)}) collective-permute-start(bf16[80,768]{1,0:T(8,128)(2,1)S(1)} %get-tuple-element.216), channel_id=1, source_target_pairs={{0,16},{4,20},{8,24},{12,28},{16,0},{20,4},{24,8},{28,12},{1,17},{... | collective-permute-start | bytes 368648 | tf_op jit(solution)/shard_map/ppermute | solution.py:723
  257.8 24.3 %collective-permute-start.27 = (bf16[80,768]{1,0:T(8,128)(2,1)S(1)}, bf16[80,768]{1,0:T(8,128)(2,1)S(1)}, u32[]{:S(2)}, u32[]{:S(2)}) collective-permute-start(bf16[80,768]{1,0:T(8,128)(2,1)S(1)} %get-tuple-element.217), channel_id=1, source_target_pairs={{0,24},{4,28},{8,16},{12,20},{16,8},{20,12},{24,0},{28,4},{1,25},{... | collective-permute-start | bytes 368648 | tf_op jit(solution)/shard_map/ppermute | solution.py:723
  282.3 14.4 %collective-permute-start.31 = (bf16[2048,768]{1,0:T(8,128)(2,1)}, bf16[2048,768]{1,0:T(8,128)(2,1)}, u32[]{:S(2)}, u32[]{:S(2)}) collective-permute-start(bf16[2048,768]{1,0:T(8,128)(2,1)} %get-tuple-element.226), channel_id=1, source_target_pairs={{0,1},{1,0},{2,3},{3,2},{4,5},{5,4},{6,7},{7,6},{8,9},{9,8},{10,11... | collective-permute-start | bytes 9437192 | tf_op jit(solution)/shard_map/ppermute | solution.py:723
  282.4 20.4 %collective-permute-start.32 = (bf16[512,768]{1,0:T(8,128)(2,1)S(1)}, bf16[512,768]{1,0:T(8,128)(2,1)S(1)}, u32[]{:S(2)}, u32[]{:S(2)}) collective-permute-start(bf16[512,768]{1,0:T(8,128)(2,1)S(1)} %choose.3.own), channel_id=1, source_target_pairs={{0,4},{4,0},{8,12},{12,8},{16,20},{20,16},{24,28},{28,24},{1,5},{5... | collective-permute-start | bytes 2359304 | tf_op jit(solution)/shard_map/ppermute | solution.py:723
  283.0 8.6 %collective-permute-start.30 = (bf16[80,768]{1,0:T(8,128)(2,1)S(1)}, bf16[80,768]{1,0:T(8,128)(2,1)S(1)}, u32[]{:S(2)}, u32[]{:S(2)}) collective-permute-start(bf16[80,768]{1,0:T(8,128)(2,1)S(1)} %add.34.refs_0_), channel_id=1, source_target_pairs={{0,24},{4,28},{8,16},{12,20},{16,8},{20,12},{24,0},{28,4},{1,25},{... | collective-permute-start | bytes 368648 | tf_op jit(solution)/shard_map/ppermute | solution.py:723
  285.4 11.3 %collective-permute-start.29 = (bf16[80,768]{1,0:T(8,128)(2,1)S(1)}, bf16[80,768]{1,0:T(8,128)(2,1)S(1)}, u32[]{:S(2)}, u32[]{:S(2)}) collective-permute-start(bf16[80,768]{1,0:T(8,128)(2,1)S(1)} %add.34.refs_0_), channel_id=1, source_target_pairs={{0,16},{4,20},{8,24},{12,28},{16,0},{20,4},{24,8},{28,12},{1,17},{... | collective-permute-start | bytes 368648 | tf_op jit(solution)/shard_map/ppermute | solution.py:723
  285.5 11.3 %collective-permute-start.28 = (bf16[80,768]{1,0:T(8,128)(2,1)S(1)}, bf16[80,768]{1,0:T(8,128)(2,1)S(1)}, u32[]{:S(2)}, u32[]{:S(2)}) collective-permute-start(bf16[80,768]{1,0:T(8,128)(2,1)S(1)} %add.34.refs_0_), channel_id=1, source_target_pairs={{0,8},{4,12},{8,0},{12,4},{16,24},{20,28},{24,16},{28,20},{1,9},{5... | collective-permute-start | bytes 368648 | tf_op jit(solution)/shard_map/ppermute | solution.py:723
  296.8 16.1 %collective-permute-start.33 = (bf16[320,768]{1,0:T(8,128)(2,1)S(1)}, bf16[320,768]{1,0:T(8,128)(2,1)S(1)}, u32[]{:S(2)}, u32[]{:S(2)}) collective-permute-start(bf16[320,768]{1,0:T(8,128)(2,1)S(1)} %join_quarters.1.own), channel_id=1, source_target_pairs={{0,4},{4,0},{8,12},{12,8},{16,20},{20,16},{24,28},{28,24},{1,5},{5... | collective-permute-start | bytes 1474568 | tf_op jit(solution)/shard_map/ppermute | solution.py:723
  (2 other events, 1.6 us)
where the time goes:
time: 316 us; the launch traced here: 315 us
  Pallas kernels  238 us (75%)
  starting transfers between devices  36.5 us (12%)
  waiting for transfers between devices  30.1 us (10%)
  local copies, waits for them, and re-layouts  8.03 us (3%)
    pallas_call x1, Pallas kernels, per_device(): spread(functools.partial(ffn_forward_kernel, short_blocks), 'ffn_forward'...  46.3 us
    pallas_call x1, Pallas kernels, per_device(): spread(ffn_backward_kernel, 'ffn_backward', (blocks,), [row_spec, own_spe...  40.4 us
    pallas_call x2, Pallas kernels, far_backward(): spread(functools.partial(attention_input_kernel, start, short_blocks), 'a...  39.8 us
    pallas_call x2, Pallas kernels, near_backward(): spread(functools.partial(attention_backward_kernel, start, short_blocks),...  37.3 us
    pallas_call x2, Pallas kernels, far_forward(): spread(functools.partial(attention_finish_kernel, start, count, short_blo...  32.1 us
    ppermute x28, waiting for transfers between devices, swap(): return lax.ppermute(values, axis, [(i, i ^ bit) for i in range(size)])  30.1 us
    ppermute x28, starting transfers between devices, swap(): return lax.ppermute(values, axis, [(i, i ^ bit) for i in range(size)])  25.3 us
    pallas_call x1, Pallas kernels, per_device(): spread(functools.partial(attention_forward_kernel, 0, blocks, short_block...  21.5 us
  transfers between devices with their start and end apart: 34, of which 10 were waited for; matrix products, arithmetic and copies ran while one was open for 1% of the time, Pallas kernels for 59%

commit v1 on v0

--- a/solution.py
+++ b/solution.py
@@ -93,20 +93,30 @@
     return scale * inner
 
 
-def load_attention_weights(pieces, wqkv, wout, bias, sems):
-    width = wqkv.shape[0] // 6
+def attention_copies(pieces, sems, wqkv=None, wout=None, bias=None):
     copies = []
     for j, piece in enumerate(pieces):
-        for k in range(3):
-            copies.append(
-                (piece.at[pl.ds(k * width, width)], wqkv.at[pl.ds((2 * k + j) * width, width)])
-            )
-        copies.append((piece.at[pl.ds(3 * width, width)], wout.at[pl.ds(j * width, width)]))
-        copies.append((piece.at[pl.ds(4 * width, 16)], bias.at[pl.ds(16 * j, 16)]))
-    started = [pltpu.make_async_copy(s, d, sems.at[n]) for n, (s, d) in enumerate(copies)]
-    for copy in started:
+        width = (piece.shape[0] - 16) // 4
+        pairs = []
+        if wqkv is not None:
+            for k in range(3):
+                rows = pl.ds((2 * k + j) * width, width)
+                pairs.append((k, piece.at[pl.ds(k * width, width)], wqkv.at[rows]))
+        if wout is not None:
+            pairs.append((3, piece.at[pl.ds(3 * width, width)], wout.at[pl.ds(j * width, width)]))
+        if bias is not None:
+            pairs.append((4, piece.at[pl.ds(4 * width, 16)], bias.at[pl.ds(16 * j, 16)]))
+        copies += [pltpu.make_async_copy(s, d, sems.at[5 * j + n]) for n, s, d in pairs]
+    return copies
+
+
+def start_all(copies):
+    for copy in copies:
         copy.start()
-    for copy in started:
+
+
+def wait_all(copies):
+    for copy in copies:
         copy.wait()
 
 
@@ -290,9 +300,12 @@
     start, count, short_blocks, core, slen, llen, scount, lcount, x, a0, a1, qkv, mixed, logs,
     wqkv, wout, bias, sems, stat, head_bias,
 ):
+    copies = attention_copies((a0, a1), sems, wqkv=wqkv, bias=bias)
+
     @pl.when(pl.program_id(0) == 0)
     def _():
-        load_attention_weights((a0, a1), wqkv, wout, bias, sems)
+        start_all(copies)
+        wait_all(copies)
 
     meta = (core, slen, llen, scount, lcount)
     attention_heads_forward(start, count, short_blocks, meta, x, (wqkv, bias, head_bias), qkv, mixed, logs, stat)
@@ -303,23 +316,27 @@
 ):
     qkv, mixed, logs, normed, scale_rows, wqkv, wout, bias, near_out, sems, stat, head_bias = rest[-12:]
 
+    width = near_out.shape[0] // 2
+    needed = attention_copies((a2, a3), sems, wqkv=wqkv, bias=bias)
+    later = attention_copies((a2, a3), sems, wout=wout) + [
+        pltpu.make_async_copy(
+            piece.at[pl.ds(3 * width, width)], near_out.at[pl.ds(j * width, width)], sems.at[10 + j]
+        )
+        for j, piece in enumerate((a0, a1))
+    ]
+
     @pl.when(pl.program_id(0) == 0)
     def _():
-        width = near_out.shape[0] // 2
-        near = [
-            pltpu.make_async_copy(
-                piece.at[pl.ds(3 * width, width)], near_out.at[pl.ds(j * width, width)], sems.at[10 + j]
-            )
-            for j, piece in enumerate((a0, a1))
-        ]
-        for copy in near:
-            copy.start()
-        load_attention_weights((a2, a3), wqkv, wout, bias, sems)
-        for copy in near:
-            copy.wait()
+        start_all(needed + later)
+        wait_all(needed)
 
     meta = (core, slen, llen, scount, lcount)
     attention_heads_forward(start, count, short_blocks, meta, x, (wqkv, bias, head_bias), qkv, mixed, logs, stat)
+
+    @pl.when(pl.program_id(0) == 0)
+    def _():
+        wait_all(later)
+
     hidden = x[...].astype(F32) + vec[0:1]
     hidden = hidden + nn(mixed_near[...], near_out[...]) + nn(mixed[...], wout[...])
     rows, scale = norm_rows(hidden)
@@ -557,9 +574,12 @@
     half = mixed.shape[1]
     width = half // 2
 
+    copies = attention_copies((a0, a1), sems, wout=wout)
+
     @pl.when(block == 0)
     def _():
-        load_attention_weights((a0, a1), wqkv, wout, bias, sems)
+        start_all(copies)
+        wait_all(copies)
         if start:
             qkv_sum[...] = sums_in[...]
             vec_sum[...] = vec_in[...]
@@ -602,27 +622,31 @@
     wqkv, wout, bias, near_qkv, sems, low_qkv, mixed_grad, delta = rest[-8:]
     meta = (core, slen, llen, scount, lcount)
 
+    width = near_qkv.shape[0] // 6
+    needed = attention_copies((a2, a3), sems, wout=wout)
+    later = attention_copies((a2, a3), sems, wqkv=wqkv) + [
+        pltpu.make_async_copy(
+            piece.at[pl.ds(k * width, width)],
+            near_qkv.at[pl.ds((2 * k + j) * width, width)],
+            sems.at[10 + 2 * k + j],
+        )
+        for k in range(3)
+        for j, piece in enumerate((a0, a1))
+    ]
+
     @pl.when(pl.program_id(0) == 0)
     def _():
-        width = near_qkv.shape[0] // 6
-        near = [
-            pltpu.make_async_copy(
-                piece.at[pl.ds(k * width, width)],
-                near_qkv.at[pl.ds((2 * k + j) * width, width)],
-                sems.at[10 + 2 * k + j],
-            )
-            for k in range(3)
-            for j, piece in enumerate((a0, a1))
-        ]
-        for copy in near:
-            copy.start()
-        load_attention_weights((a2, a3), wqkv, wout, bias, sems)
-        for copy in near:
-            copy.wait()
+        start_all(needed + later)
+        wait_all(needed)
 
     low = hidden_low[...]
     mixed_grad[...] = nt(low, wout[...]).astype(BF16)
     attention_heads_backward(start, short_blocks, meta, stat, qkv, mixed, mixed_grad, low_qkv, delta)
+
+    @pl.when(pl.program_id(0) == 0)
+    def _():
+        wait_all(later)
+
     total = low.astype(F32) + nn(low_near[...], near_qkv[...]) + nn(low_qkv[...], wqkv[...])
     input_rows[...] = total.astype(BF16)
     input_grad[...] = total

time: 316 us -> 313 us (level)
  Pallas kernels: 238 us -> 234 us
  transfers between devices with their start and end apart: 34 -> 34, of which waited for: 10 -> 11; matrix products, arithmetic and copies ran while one was open for 1% -> 1% of each run, Pallas kernels for 59% -> 58%
where the time goes in v1:
time: 313 us; the launch traced here: 312 us
  Pallas kernels  234 us (75%)
  starting transfers between devices  36.6 us (12%)
  waiting for transfers between devices  31.3 us (10%)
  local copies, waits for them, and re-layouts  8.03 us (3%)
    pallas_call x1, Pallas kernels, per_device(): spread(functools.partial(ffn_forward_kernel, short_blocks), 'ffn_forward'...  46.3 us
    pallas_call x1, Pallas kernels, per_device(): spread(ffn_backward_kernel, 'ffn_backward', (blocks,), [row_spec, own_spe...  40.4 us
    pallas_call x2, Pallas kernels, far_backward(): spread(functools.partial(attention_input_kernel, start, short_blocks), 'a...  37.7 us
    pallas_call x2, Pallas kernels, near_backward(): spread(functools.partial(attention_backward_kernel, start, short_blocks),...  36.2 us
    pallas_call x2, Pallas kernels, far_forward(): spread(functools.partial(attention_finish_kernel, start, count, short_blo...  31.5 us
    ppermute x28, waiting for transfers between devices, swap(): return lax.ppermute(values, axis, [(i, i ^ bit) for i in range(size)])  31.3 us
    ppermute x28, starting transfers between devices, swap(): return lax.ppermute(values, axis, [(i, i ^ bit) for i in range(size)])  25.3 us
    pallas_call x1, Pallas kernels, per_device(): spread(functools.partial(attention_forward_kernel, 0, blocks, short_block...  21.3 us
  transfers between devices with their start and end apart: 34, of which 11 were waited for; matrix products, arithmetic and copies ran while one was open for 1% of the time, Pallas kernels for 58%

profile of v1, /device:TPU:0, one launch (start us, length us, event | category | flops | bytes accessed | tf_op | source)
XLA Modules:
  0.0 312.4 jit_solution(2774045000419721969)
XLA Ops:
  0.7 2.5 pack.1
  3.7 2.6 collective-permute-start.1
  7.6 1.1 constant_dynamic-slice_fusion
  8.7 1.0 copy-done.7
  9.7 21.3 %attention_near.1 = (bf16[2048,1152]{1,0:T(8,128)(2,1)}, bf16[2048,384]{1,0:T(8,128)(2,1)}, f32[32,512]{1,0:T(8,128)}) custom-call(s32[1]{0:T(128)} %bitcast.core, s32[16]{0:T(128)} %slen.15, s32[4]{0:T(128)} %llen.15, s32[1]{0:T(128)S(6)} %copy.56.scount, s32[1]{0:T(128)S(6)} %copy.57.lcount, bf16[4096,768]{1,0:T(8,128)(2,1)} %x.9, ...), custom_call_target="tpu_custom_call" | custom-call | flops 4630511616 | bytes 12582912 | tf_op jit(solution)/shard_map/attention_near/pallas_call | solution.py:793
  31.0 2.6 collective-permute-done.1.a2.rest_12_
  33.6 2.9 collective-permute-done.2.a3.rest_13_
  36.6 1.8 collective-permute-start.3
  38.6 14.5 %attention_far.2 = (bf16[2048,1152]{1,0:T(8,128)(2,1)}, bf16[2048,384]{1,0:T(8,128)(2,1)}, f32[32,512]{1,0:T(8,128)}, bf16[2048,768]{1,0:T(8,128)(2,1)}, f32[2048,128]{1,0:T(8,128)}) custom-call(s32[1]{0:T(128)} %bitcast.core, s32[16]{0:T(128)} %slen.15, s32[4]{0:T(128)} %llen.15, s32[1]{0:T(128)S(6)} %copy.56.scount, s32[1]{0:T(128)S(6)} %copy.57.lcount, ...), custom_call_target="tpu_custom_call" | custom-call | flops 3523215360 | bytes 7864320 | tf_op jit(solution)/shard_map/attention_far/pallas_call | solution.py:807
  53.7 1.7 collective-permute-start.5
  55.4 17.1 %attention_far.3 = (bf16[2048,1152]{1,0:T(8,128)(2,1)}, bf16[2048,384]{1,0:T(8,128)(2,1)}, f32[32,512]{1,0:T(8,128)}, bf16[2048,768]{1,0:T(8,128)(2,1)}, f32[2048,128]{1,0:T(8,128)}) custom-call(s32[1]{0:T(128)} %bitcast.core, s32[16]{0:T(128)} %slen.15, s32[4]{0:T(128)} %llen.15, ...), custom_call_target="tpu_custom_call", output_to_operand_aliasing={{0}: (12, {}), {1}: (13, {}), {2}: (14, {}), {3}: (15, {}),... | custom-call | flops 3523215360 | bytes 7864320 | tf_op jit(solution)/shard_map/attention_far/pallas_call | solution.py:807
  72.5 5.1 %collective-permute-done.7.rest_8_ = bf16[768,768]{1,0:T(8,128)(2,1)} collective-permute-done((bf16[768,768]{1,0:T(8,128)(2,1)}, bf16[768,768]{1,0:T(8,128)(2,1)}, u32[]{:S(2)}, u32[]{:S(2)}) %collective-permute-start.7) | collective-permute-done | bytes 1179680 | tf_op jit(solution)/shard_map/ppermute | solution.py:747
  78.2 3.1 collective-permute-done.9.rest_5_
  81.3 0.8 copy-done.15
  82.2 1.0 copy-done.11
  83.2 46.3 %ffn_forward.1 = (bf16[4096,768]{1,0:T(8,128)(2,1)}, bf16[2048,768]{1,0:T(8,128)(2,1)}, bf16[2048,768]{1,0:T(8,128)(2,1)}, bf16[2048,3072]{1,0:T(8,128)(2,1)}, b...) custom-call(s32[1]{0:T(128)} %bitcast.core, s32[16]{0:T(128)} %slen.15, s32[4]{0:T(128)} %llen.15, ...), custom_call_target="tpu_custom_call" | custom-call | flops 24159191040 | bytes 31457280 | tf_op jit(solution)/shard_map/ffn_forward/pallas_call | solution.py:836
  129.7 2.9 collective-permute-done.11.partner
  132.6 1.3 copy-done.1
  134.4 1.7 collective-permute-start.12
  136.1 40.4 %ffn_backward.1 = (bf16[2048,768]{1,0:T(8,128)(2,1)}, bf16[1024,768]{1,0:T(8,128)(2,1)}, bf16[1024,768]{1,0:T(8,128)(2,1)}) custom-call(s32[1]{0:T(128)} %bitcast.1.at.side, bf16[2048,768]{1,0:T(8,128)(2,1)} %get-tuple-element.163.grad_low, bf16[2048,3072]{1,0:T(8,128)(2,1)} %get-tuple-element.164.slope, bf16[2048,768]{1,0:T(8,128)(2,1)} %get-tuple-element.150.normed, ...), custom_call_target="tpu_custom_call" | custom-call | flops 24159191040 | bytes 25165824 | tf_op jit(solution)/shard_map/ffn_backward/pallas_call | solution.py:928
  176.9 3.5 %collective-permute-done.14.partner = bf16[1024,768]{1,0:T(8,128)(2,1)S(1)} collective-permute-done((bf16[1024,768]{1,0:T(8,128)(2,1)}, bf16[1024,768]{1,0:T(8,128)(2,1)S(1)}, u32[]{:S(2)}, u32[]{:S(2)}) %collective-permute-start.14) | collective-permute-done | bytes 1572896 | tf_op jit(solution)/shard_map/ppermute | solution.py:747
  181.3 3.8 %collective-permute-start.15 = (bf16[384,768]{1,0:T(8,128)(2,1)S(1)}, bf16[384,768]{1,0:T(8,128)(2,1)S(1)}, u32[]{:S(2)}, u32[]{:S(2)}) collective-permute-start(bf16[384,768]{1,0:T(8,128)(2,1)S(1)} %add.28.refs_0_), channel_id=1, source_target_pairs={{0,8},{4,12},{24,16},{28,20},{1,9},{5,13},{25,17},{29,21},{2,10},{... | collective-permute-start | bytes 1769480 | tf_op jit(solution)/shard_map/ppermute | solution.py:857
  185.0 15.0 %attention_near_backward.2 = (bf16[1024,1152]{1,0:T(8,128)(2,1)}, f32[3,384,768]{2,1,0:T(8,128)}, f32[2,8,384]{2,1,0:T(8,128)}) custom-call(s32[1]{0:T(128)} %bitcast.core, s32[16]{0:T(128)} %slen.15, s32[4]{0:T(128)} %llen.15, s32[1]{0:T(128)S(6)} %copy.56.scount, s32[1]{0:T(128)S(6)} %copy.57.lcount, bf16[2048,768]{1,0:T(8,128)(2,1)} %get-tuple-element.180.hidden_low, ...), custom_call_target="tpu_custom_call" | custom-call | flops 4278190080 | bytes 12582912 | tf_op jit(solution)/shard_map/attention_near_backward/pallas_call | solution.py:950
  200.8 3.5 %collective-permute-start.18 = (bf16[512,768]{1,0:T(8,128)(2,1)S(1)}, bf16[512,768]{1,0:T(8,128)(2,1)S(1)}, u32[]{:S(2)}, u32[]{:S(2)}) collective-permute-start(bf16[512,768]{1,0:T(8,128)(2,1)S(1)} %add.30.refs_0_), channel_id=1, source_target_pairs={{0,8},{4,12},{24,16},{28,20},{1,9},{5,13},{25,17},{29,21},{2,10},{... | collective-permute-start | bytes 2359304 | tf_op jit(solution)/shard_map/ppermute | solution.py:857
  205.2 21.2 %attention_near_backward.3 = (bf16[1024,1152]{1,0:T(8,128)(2,1)}, bf16[640,768]{1,0:T(8,128)(2,1)}, bf16[640,768]{1,0:T(8,128)(2,1)}) custom-call(s32[1]{0:T(128)} %bitcast.core, s32[16]{0:T(128)} %slen.15, s32[4]{0:T(128)} %llen.15, s32[1]{0:T(128)S(6)} %copy.56.scount, s32[1]{0:T(128)S(6)} %copy.57.lcount, ...), custom_call_target="tpu_custom_call" | custom-call | flops 4278190080 | bytes 12582912 | tf_op jit(solution)/shard_map/attention_near_backward/pallas_call | solution.py:950
  226.9 0.7 copy-done.12
  228.4 1.3 collective-permute-start.20
  230.2 1.1 halves.5
  231.8 15.8 %attention_far_backward.2 = (bf16[2048,768]{1,0:T(8,128)(2,1)}, f32[4096,768]{1,0:T(8,128)}) custom-call(s32[1]{0:T(128)} %bitcast.core, s32[16]{0:T(128)} %slen.15, s32[4]{0:T(128)} %llen.15, s32[1]{0:T(128)S(6)} %copy.56.scount, s32[1]{0:T(128)S(6)} %copy.57.lcount, bf16[2048,768]{1,0:T(8,128)(2,1)} %get-tuple-element.180.hidden_low, ...), custom_call_target="tpu_custom_call" | custom-call | flops 5486149632 | bytes 12582912 | tf_op jit(solution)/shard_map/attention_far_backward/pallas_call | solution.py:976
  247.7 0.8 copy-done.5
  248.7 1.3 collective-permute-start.24
  250.1 1.5 collective-permute-start.23
  251.8 3.4 %collective-permute-start.25 = (bf16[80,768]{1,0:T(8,128)(2,1)S(1)}, bf16[80,768]{1,0:T(8,128)(2,1)S(1)}, u32[]{:S(2)}, u32[]{:S(2)}) collective-permute-start(bf16[80,768]{1,0:T(8,128)(2,1)S(1)} %get-tuple-element.209), channel_id=1, source_target_pairs={{0,8},{4,12},{8,0},{12,4},{16,24},{20,28},{24,16},{28,20},{1,9},{5... | collective-permute-start | bytes 368648 | tf_op jit(solution)/shard_map/ppermute | solution.py:747
  255.2 1.1 collective-permute-start.26
  256.2 1.4 collective-permute-start.27
  257.6 21.9 %attention_far_backward.3 = (bf16[2048,768]{1,0:T(8,128)(2,1)}, f32[4096,768]{1,0:T(8,128)}) custom-call(s32[1]{0:T(128)} %bitcast.core, s32[16]{0:T(128)} %slen.15, s32[4]{0:T(128)} %llen.15, s32[1]{0:T(128)S(6)} %copy.56.scount, s32[1]{0:T(128)S(6)} %copy.57.lcount, ...), custom_call_target="tpu_custom_call", output_to_operand_aliasing={{0}: (14, {}), {1}: (15, {})} | custom-call | flops 5486149632 | bytes 12582912 | tf_op jit(solution)/shard_map/attention_far_backward/pallas_call | solution.py:976
  279.8 1.2 collective-permute-start.32
  281.0 2.1 collective-permute-start.30
  283.5 1.9 collective-permute-start.28
  285.4 4.2 %place.2 = bf16[4096,768]{1,0:T(8,128)(2,1)} custom-call(s32[1]{0:T(128)} %bitcast.core, bf16[2048,768]{1,0:T(8,128)(2,1)} %collective-permute-done.13.other, bf16[4096,768]{1,0:T(8,128)(2,1)} %get-tuple-element.224.whole), custom_call_target="tpu_custom_call", output_to_operand_aliasing={{}: (2, {})} | custom-call | bytes 9437184 | tf_op jit(solution)/shard_map/place/pallas_call | solution.py:1002
  289.6 5.2 %collective-permute-done.29.refs_2_ = bf16[80,768]{1,0:T(8,128)(2,1)S(1)} collective-permute-done((bf16[80,768]{1,0:T(8,128)(2,1)S(1)}, bf16[80,768]{1,0:T(8,128)(2,1)S(1)}, u32[]{:S(2)}, u32[]{:S(2)}) %collective-permute-start.29) | collective-permute-done | bytes 122912 | tf_op jit(solution)/shard_map/ppermute | solution.py:747
  294.8 1.0 collective-permute-start.33
  295.8 1.8 finish.5
  297.6 2.6 collective-permute-done.32.other
  300.2 2.1 finish.3
  302.3 5.0 %place.3 = f32[4096,768]{1,0:T(8,128)} custom-call(s32[1]{0:T(128)} %bitcast.core, bf16[2048,768]{1,0:T(8,128)(2,1)} %collective-permute-done.31.other, f32[4096,768]{1,0:T(8,128)} %get-tuple-element.235.whole), custom_call_target="tpu_custom_call", output_to_operand_aliasing={{}: (2, {})} | custom-call | bytes 9437184 | tf_op jit(solution)/shard_map/place/pallas_call | solution.py:1002
  308.0 2.3 collective-permute-done.33.other
  310.3 1.5 finish.4
  (84 shorter events, 10.0 us)
Async XLA Ops:
  3.2 5.5 %collective-permute-start = (bf16[784,768]{1,0:T(8,128)(2,1)}, bf16[784,768]{1,0:T(8,128)(2,1)S(1)}, u32[]{:S(2)}, u32[]{:S(2)}) collective-permute-start(bf16[784,768]{1,0:T(8,128)(2,1)} %get-tuple-element.132.a0.rest_10_), channel_id=1, source_target_pairs={{0,1},{1,0},{2,3},{3,2},{4,5},{5,4},{6,7},{7,6},{8,9},{9,8},{10,11... | collective-permute-start | bytes 3612680 | tf_op jit(solution)/shard_map/ppermute | solution.py:747
  3.7 29.9 %collective-permute-start.1 = (bf16[784,768]{1,0:T(8,128)(2,1)}, bf16[784,768]{1,0:T(8,128)(2,1)S(1)}, u32[]{:S(2)}, u32[]{:S(2)}) collective-permute-start(bf16[784,768]{1,0:T(8,128)(2,1)} %get-tuple-element.132.a0.rest_10_), channel_id=1, source_target_pairs={{0,2},{1,3},{2,0},{3,1},{4,6},{5,7},{6,4},{7,5},{8,10},{9,11},{10,... | collective-permute-start | bytes 3612680 | tf_op jit(solution)/shard_map/ppermute | solution.py:747
  8.7 1.0 copy-start.7
  33.6 5.1 %copy-start.8 = (bf16[784,768]{1,0:T(8,128)(2,1)}, bf16[784,768]{1,0:T(8,128)(2,1)S(1)}, u32[]{:S(2)}) copy-start(bf16[784,768]{1,0:T(8,128)(2,1)S(1)} %collective-permute-done.1.a2.rest_12_) | copy-start | bytes 3612676
  33.6 2.9 collective-permute-start.2
  36.4 2.2 copy-start.9
  36.4 16.7 %collective-permute-start.4 = (bf16[768,768]{1,0:T(8,128)(2,1)}, bf16[768,768]{1,0:T(8,128)(2,1)}, u32[]{:S(2)}, u32[]{:S(2)}) collective-permute-start(bf16[768,768]{1,0:T(8,128)(2,1)} %rest_0_.3), channel_id=1, source_target_pairs={{0,1},{1,0},{2,3},{3,2},{4,5},{5,4},{6,7},{7,6},{8,9},{9,8},{10,11... | collective-permute-start | bytes 3538952 | tf_op jit(solution)/shard_map/ppermute | solution.py:747
  36.6 16.5 %collective-permute-start.3 = (bf16[768,384]{1,0:T(8,128)(2,1)S(1)}, bf16[768,384]{1,0:T(8,128)(2,1)}, u32[]{:S(2)}, u32[]{:S(2)}) collective-permute-start(bf16[768,384]{1,0:T(8,128)(2,1)S(1)} %constant_dynamic-slice_fusion), channel_id=1, source_target_pairs={{0,2},{1,3},{2,0},{3,1},{4,6},{5,7},{6,4},{7,5},{8,10},{9,11},{10,... | collective-permute-start | bytes 1769480 | tf_op jit(solution)/shard_map/ppermute | solution.py:747
  38.4 39.2 %collective-permute-start.7 = (bf16[768,768]{1,0:T(8,128)(2,1)}, bf16[768,768]{1,0:T(8,128)(2,1)}, u32[]{:S(2)}, u32[]{:S(2)}) collective-permute-start(bf16[768,768]{1,0:T(8,128)(2,1)} %rest_6_.3), channel_id=1, source_target_pairs={{0,2},{1,3},{2,0},{3,1},{4,6},{5,7},{6,4},{7,5},{8,10},{9,11},{10,... | collective-permute-start | bytes 3538952 | tf_op jit(solution)/shard_map/ppermute | solution.py:747
  53.1 24.5 %collective-permute-start.8 = (bf16[768,768]{1,0:T(8,128)(2,1)}, bf16[768,768]{1,0:T(8,128)(2,1)S(1)}, u32[]{:S(2)}, u32[]{:S(2)}) collective-permute-start(bf16[768,768]{1,0:T(8,128)(2,1)} %rest_6_.3), channel_id=1, source_target_pairs={{0,1},{1,0},{2,3},{3,2},{4,5},{5,4},{6,7},{7,6},{8,9},{9,8},{10,11... | collective-permute-start | bytes 3538952 | tf_op jit(solution)/shard_map/ppermute | solution.py:747
  53.2 24.4 %collective-permute-start.6 = (bf16[768,384]{1,0:T(8,128)(2,1)}, bf16[768,384]{1,0:T(8,128)(2,1)S(1)}, u32[]{:S(2)}, u32[]{:S(2)}) collective-permute-start(bf16[768,384]{1,0:T(8,128)(2,1)} %collective-permute-done.3.rest_2_), channel_id=1, source_target_pairs={{0,1},{1,0},{2,3},{3,2},{4,5},{5,4},{6,7},{7,6},{8,9},{9,8},{10,11... | collective-permute-start | bytes 1769480 | tf_op jit(solution)/shard_map/ppermute | solution.py:747
  53.7 23.9 %collective-permute-start.5 = (bf16[768,384]{1,0:T(8,128)(2,1)}, bf16[768,384]{1,0:T(8,128)(2,1)S(1)}, u32[]{:S(2)}, u32[]{:S(2)}) collective-permute-start(bf16[768,384]{1,0:T(8,128)(2,1)} %collective-permute-done.3.rest_2_), channel_id=1, source_target_pairs={{0,4},{4,0},{8,12},{12,8},{16,20},{20,16},{24,28},{28,24},{1,5},{5... | collective-permute-start | bytes 1769480 | tf_op jit(solution)/shard_map/ppermute | solution.py:747
  77.6 4.6 %copy-start.13 = (bf16[768,384]{1,0:T(8,128)(2,1)}, bf16[768,384]{1,0:T(8,128)(2,1)S(1)}, u32[]{:S(2)}) copy-start(bf16[768,384]{1,0:T(8,128)(2,1)S(1)} %collective-permute-done.6.rest_3_) | copy-start | bytes 1769476
  77.6 4.6 %copy-start.14 = (bf16[768,384]{1,0:T(8,128)(2,1)}, bf16[768,384]{1,0:T(8,128)(2,1)S(1)}, u32[]{:S(2)}) copy-start(bf16[768,384]{1,0:T(8,128)(2,1)S(1)} %collective-permute-done.5.rest_4_) | copy-start | bytes 1769476
  77.6 4.5 %copy-start.10 = (bf16[768,768]{1,0:T(8,128)(2,1)}, bf16[768,768]{1,0:T(8,128)(2,1)S(1)}, u32[]{:S(2)}) copy-start(bf16[768,768]{1,0:T(8,128)(2,1)S(1)} %collective-permute-done.8.rest_7_) | copy-start | bytes 3538948
  77.6 4.5 %collective-permute-start.10 = (bf16[768,768]{1,0:T(8,128)(2,1)}, bf16[768,768]{1,0:T(8,128)(2,1)S(1)}, u32[]{:S(2)}, u32[]{:S(2)}) collective-permute-start(bf16[768,768]{1,0:T(8,128)(2,1)} %collective-permute-done.7.rest_8_), channel_id=1, source_target_pairs={{0,1},{1,0},{2,3},{3,2},{4,5},{5,4},{6,7},{7,6},{8,9},{9,8},{10,11... | collective-permute-start | bytes 3538952 | tf_op jit(solution)/shard_map/ppermute | solution.py:747
  77.7 3.6 %collective-permute-start.9 = (bf16[768,384]{1,0:T(8,128)(2,1)S(1)}, bf16[768,384]{1,0:T(8,128)(2,1)S(1)}, u32[]{:S(2)}, u32[]{:S(2)}) collective-permute-start(bf16[768,384]{1,0:T(8,128)(2,1)S(1)} %collective-permute-done.5.rest_4_), channel_id=1, source_target_pairs={{0,1},{1,0},{2,3},{3,2},{4,5},{5,4},{6,7},{7,6},{8,9},{9,8},{10,11... | collective-permute-start | bytes 1769480 | tf_op jit(solution)/shard_map/ppermute | solution.py:747
  82.1 1.0 copy-start.11
  129.5 3.1 collective-permute-start.11
  132.6 1.3 copy-start.1
  134.2 42.3 %collective-permute-start.13 = (bf16[2048,768]{1,0:T(8,128)(2,1)}, bf16[2048,768]{1,0:T(8,128)(2,1)}, u32[]{:S(2)}, u32[]{:S(2)}) collective-permute-start(bf16[2048,768]{1,0:T(8,128)(2,1)} %get-tuple-element.171), channel_id=1, source_target_pairs={{0,1},{1,0},{2,3},{3,2},{4,5},{5,4},{6,7},{7,6},{8,9},{9,8},{10,11... | collective-permute-start | bytes 9437192 | tf_op jit(solution)/shard_map/ppermute | solution.py:747
  134.4 42.1 %collective-permute-start.12 = (bf16[384,768]{1,0:T(8,128)(2,1)S(1)}, bf16[384,768]{1,0:T(8,128)(2,1)S(1)}, u32[]{:S(2)}, u32[]{:S(2)}) collective-permute-start(bf16[384,768]{1,0:T(8,128)(2,1)S(1)} %get-tuple-element.162), channel_id=1, source_target_pairs={{0,4},{4,0},{8,12},{12,8},{16,20},{20,16},{24,28},{28,24},{1,5},{5... | collective-permute-start | bytes 1769480 | tf_op jit(solution)/shard_map/ppermute | solution.py:747
  176.5 3.9 %copy-start = (bf16[1024,768]{1,0:T(8,128)(2,1)S(1)}, bf16[1024,768]{1,0:T(8,128)(2,1)}, u32[]{:S(2)}) copy-start(bf16[1024,768]{1,0:T(8,128)(2,1)} %get-tuple-element.174.mine) | copy-start | bytes 4718596
  176.7 3.7 %collective-permute-start.14 = (bf16[1024,768]{1,0:T(8,128)(2,1)}, bf16[1024,768]{1,0:T(8,128)(2,1)S(1)}, u32[]{:S(2)}, u32[]{:S(2)}) collective-permute-start(bf16[1024,768]{1,0:T(8,128)(2,1)} %get-tuple-element.178), channel_id=1, source_target_pairs={{0,1},{1,0},{2,3},{3,2},{4,5},{5,4},{6,7},{7,6},{8,9},{9,8},{10,11... | collective-permute-start | bytes 4718600 | tf_op jit(solution)/shard_map/ppermute | solution.py:747
  180.9 19.6 %collective-permute-start.16 = (bf16[512,768]{1,0:T(8,128)(2,1)S(1)}, bf16[512,768]{1,0:T(8,128)(2,1)S(1)}, u32[]{:S(2)}, u32[]{:S(2)}) collective-permute-start(bf16[512,768]{1,0:T(8,128)(2,1)S(1)} %get-tuple-element.179), channel_id=1, source_target_pairs={{0,4},{4,0},{8,12},{12,8},{16,20},{20,16},{24,28},{28,24},{1,5},{5... | collective-permute-start | bytes 2359304 | tf_op jit(solution)/shard_map/ppermute | solution.py:747
  181.3 18.8 %collective-permute-start.15 = (bf16[384,768]{1,0:T(8,128)(2,1)S(1)}, bf16[384,768]{1,0:T(8,128)(2,1)S(1)}, u32[]{:S(2)}, u32[]{:S(2)}) collective-permute-start(bf16[384,768]{1,0:T(8,128)(2,1)S(1)} %add.28.refs_0_), channel_id=1, source_target_pairs={{0,8},{4,12},{24,16},{28,20},{1,9},{5,13},{25,17},{29,21},{2,10},{... | collective-permute-start | bytes 1769480 | tf_op jit(solution)/shard_map/ppermute | solution.py:857
  200.8 25.7 %collective-permute-start.18 = (bf16[512,768]{1,0:T(8,128)(2,1)S(1)}, bf16[512,768]{1,0:T(8,128)(2,1)S(1)}, u32[]{:S(2)}, u32[]{:S(2)}) collective-permute-start(bf16[512,768]{1,0:T(8,128)(2,1)S(1)} %add.30.refs_0_), channel_id=1, source_target_pairs={{0,8},{4,12},{24,16},{28,20},{1,9},{5,13},{25,17},{29,21},{2,10},{... | collective-permute-start | bytes 2359304 | tf_op jit(solution)/shard_map/ppermute | solution.py:857
  204.5 22.0 %collective-permute-start.17 = (bf16[384,768]{1,0:T(8,128)(2,1)S(1)}, bf16[384,768]{1,0:T(8,128)(2,1)S(1)}, u32[]{:S(2)}, u32[]{:S(2)}) collective-permute-start(bf16[384,768]{1,0:T(8,128)(2,1)S(1)} %add.29.refs_0_), channel_id=1, source_target_pairs={{8,16},{12,20},{16,8},{20,12},{9,17},{13,21},{17,9},{21,13},{10,18... | collective-permute-start | bytes 1769480 | tf_op jit(solution)/shard_map/ppermute | solution.py:857
  226.4 1.2 copy-start.12
  226.4 3.8 %copy-start.2 = (bf16[640,768]{1,0:T(8,128)(2,1)S(1)}, bf16[640,768]{1,0:T(8,128)(2,1)}, u32[]{:S(2)}) copy-start(bf16[640,768]{1,0:T(8,128)(2,1)} %get-tuple-element.193.mine) | copy-start | bytes 2949124
  227.6 2.6 collective-permute-start.19
  227.6 20.1 %collective-permute-start.21 = (bf16[512,768]{1,0:T(8,128)(2,1)S(1)}, bf16[512,768]{1,0:T(8,128)(2,1)S(1)}, u32[]{:S(2)}, u32[]{:S(2)}) collective-permute-start(bf16[512,768]{1,0:T(8,128)(2,1)S(1)} %add.32.refs_0_), channel_id=1, source_target_pairs={{8,16},{12,20},{16,8},{20,12},{9,17},{13,21},{17,9},{21,13},{10,18... | collective-permute-start | bytes 2359304 | tf_op jit(solution)/shard_map/ppermute | solution.py:857
  228.4 19.3 %collective-permute-start.20 = (bf16[384,768]{1,0:T(8,128)(2,1)S(1)}, bf16[384,768]{1,0:T(8,128)(2,1)S(1)}, u32[]{:S(2)}, u32[]{:S(2)}) collective-permute-start(bf16[384,768]{1,0:T(8,128)(2,1)S(1)} %add.31.own), channel_id=1, source_target_pairs={{8,0},{12,4},{16,24},{20,28},{9,1},{13,5},{17,25},{21,29},{10,2},{... | collective-permute-start | bytes 1769480 | tf_op jit(solution)/shard_map/ppermute | solution.py:857
  231.3 16.4 %copy-start.3 = (bf16[320,768]{1,0:T(8,128)(2,1)}, bf16[320,768]{1,0:T(8,128)(2,1)S(1)}, u32[]{:S(2)}) copy-start(bf16[320,768]{1,0:T(8,128)(2,1)S(1)} %get-tuple-element.198.keep) | copy-start | bytes 1474564
  231.3 16.4 %collective-permute-start.22 = (bf16[320,768]{1,0:T(8,128)(2,1)}, bf16[320,768]{1,0:T(8,128)(2,1)S(1)}, u32[]{:S(2)}, u32[]{:S(2)}) collective-permute-start(bf16[320,768]{1,0:T(8,128)(2,1)} %get-tuple-element.203), channel_id=1, source_target_pairs={{0,4},{4,0},{8,12},{12,8},{16,20},{20,16},{24,28},{28,24},{1,5},{5... | collective-permute-start | bytes 1474568 | tf_op jit(solution)/shard_map/ppermute | solution.py:747
  247.7 3.9 %copy-start.4 = (bf16[320,768]{1,0:T(8,128)(2,1)S(1)}, bf16[320,768]{1,0:T(8,128)(2,1)}, u32[]{:S(2)}) copy-start(bf16[320,768]{1,0:T(8,128)(2,1)} %copy-done.3) | copy-start | bytes 1474564
  248.5 3.1 %copy-start.6 = (bf16[320,768]{1,0:T(8,128)(2,1)S(1)}, bf16[320,768]{1,0:T(8,128)(2,1)}, u32[]{:S(2)}) copy-start(bf16[320,768]{1,0:T(8,128)(2,1)} %copy-done.5) | copy-start | bytes 1474564
  248.7 30.8 %collective-permute-start.24 = (bf16[512,768]{1,0:T(8,128)(2,1)S(1)}, bf16[512,768]{1,0:T(8,128)(2,1)S(1)}, u32[]{:S(2)}, u32[]{:S(2)}) collective-permute-start(bf16[512,768]{1,0:T(8,128)(2,1)S(1)} %add.33.own), channel_id=1, source_target_pairs={{8,0},{12,4},{16,24},{20,28},{9,1},{13,5},{17,25},{21,29},{10,2},{... | collective-permute-start | bytes 2359304 | tf_op jit(solution)/shard_map/ppermute | solution.py:857
  250.1 29.5 %collective-permute-start.23 = (bf16[384,768]{1,0:T(8,128)(2,1)S(1)}, bf16[384,768]{1,0:T(8,128)(2,1)S(1)}, u32[]{:S(2)}, u32[]{:S(2)}) collective-permute-start(bf16[384,768]{1,0:T(8,128)(2,1)S(1)} %choose.2.own), channel_id=1, source_target_pairs={{0,4},{4,0},{8,12},{12,8},{16,20},{20,16},{24,28},{28,24},{1,5},{5... | collective-permute-start | bytes 1769480 | tf_op jit(solution)/shard_map/ppermute | solution.py:747
  251.8 27.8 %collective-permute-start.25 = (bf16[80,768]{1,0:T(8,128)(2,1)S(1)}, bf16[80,768]{1,0:T(8,128)(2,1)S(1)}, u32[]{:S(2)}, u32[]{:S(2)}) collective-permute-start(bf16[80,768]{1,0:T(8,128)(2,1)S(1)} %get-tuple-element.209), channel_id=1, source_target_pairs={{0,8},{4,12},{8,0},{12,4},{16,24},{20,28},{24,16},{28,20},{1,9},{5... | collective-permute-start | bytes 368648 | tf_op jit(solution)/shard_map/ppermute | solution.py:747
  255.2 24.4 %collective-permute-start.26 = (bf16[80,768]{1,0:T(8,128)(2,1)S(1)}, bf16[80,768]{1,0:T(8,128)(2,1)S(1)}, u32[]{:S(2)}, u32[]{:S(2)}) collective-permute-start(bf16[80,768]{1,0:T(8,128)(2,1)S(1)} %get-tuple-element.216), channel_id=1, source_target_pairs={{0,16},{4,20},{8,24},{12,28},{16,0},{20,4},{24,8},{28,12},{1,17},{... | collective-permute-start | bytes 368648 | tf_op jit(solution)/shard_map/ppermute | solution.py:747
  256.2 23.3 %collective-permute-start.27 = (bf16[80,768]{1,0:T(8,128)(2,1)S(1)}, bf16[80,768]{1,0:T(8,128)(2,1)S(1)}, u32[]{:S(2)}, u32[]{:S(2)}) collective-permute-start(bf16[80,768]{1,0:T(8,128)(2,1)S(1)} %get-tuple-element.217), channel_id=1, source_target_pairs={{0,24},{4,28},{8,16},{12,20},{16,8},{20,12},{24,0},{28,4},{1,25},{... | collective-permute-start | bytes 368648 | tf_op jit(solution)/shard_map/ppermute | solution.py:747
  279.7 15.0 %collective-permute-start.31 = (bf16[2048,768]{1,0:T(8,128)(2,1)}, bf16[2048,768]{1,0:T(8,128)(2,1)}, u32[]{:S(2)}, u32[]{:S(2)}) collective-permute-start(bf16[2048,768]{1,0:T(8,128)(2,1)} %get-tuple-element.226), channel_id=1, source_target_pairs={{0,1},{1,0},{2,3},{3,2},{4,5},{5,4},{6,7},{7,6},{8,9},{9,8},{10,11... | collective-permute-start | bytes 9437192 | tf_op jit(solution)/shard_map/ppermute | solution.py:747
  279.8 20.4 %collective-permute-start.32 = (bf16[512,768]{1,0:T(8,128)(2,1)S(1)}, bf16[512,768]{1,0:T(8,128)(2,1)S(1)}, u32[]{:S(2)}, u32[]{:S(2)}) collective-permute-start(bf16[512,768]{1,0:T(8,128)(2,1)S(1)} %choose.3.own), channel_id=1, source_target_pairs={{0,4},{4,0},{8,12},{12,8},{16,20},{20,16},{24,28},{28,24},{1,5},{5... | collective-permute-start | bytes 2359304 | tf_op jit(solution)/shard_map/ppermute | solution.py:747
  281.0 8.6 %collective-permute-start.30 = (bf16[80,768]{1,0:T(8,128)(2,1)S(1)}, bf16[80,768]{1,0:T(8,128)(2,1)S(1)}, u32[]{:S(2)}, u32[]{:S(2)}) collective-permute-start(bf16[80,768]{1,0:T(8,128)(2,1)S(1)} %add.34.refs_0_), channel_id=1, source_target_pairs={{0,24},{4,28},{8,16},{12,20},{16,8},{20,12},{24,0},{28,4},{1,25},{... | collective-permute-start | bytes 368648 | tf_op jit(solution)/shard_map/ppermute | solution.py:747
  283.1 11.7 %collective-permute-start.29 = (bf16[80,768]{1,0:T(8,128)(2,1)S(1)}, bf16[80,768]{1,0:T(8,128)(2,1)S(1)}, u32[]{:S(2)}, u32[]{:S(2)}) collective-permute-start(bf16[80,768]{1,0:T(8,128)(2,1)S(1)} %add.34.refs_0_), channel_id=1, source_target_pairs={{0,16},{4,20},{8,24},{12,28},{16,0},{20,4},{24,8},{28,12},{1,17},{... | collective-permute-start | bytes 368648 | tf_op jit(solution)/shard_map/ppermute | solution.py:747
  283.5 11.3 %collective-permute-start.28 = (bf16[80,768]{1,0:T(8,128)(2,1)S(1)}, bf16[80,768]{1,0:T(8,128)(2,1)S(1)}, u32[]{:S(2)}, u32[]{:S(2)}) collective-permute-start(bf16[80,768]{1,0:T(8,128)(2,1)S(1)} %add.34.refs_0_), channel_id=1, source_target_pairs={{0,8},{4,12},{8,0},{12,4},{16,24},{20,28},{24,16},{28,20},{1,9},{5... | collective-permute-start | bytes 368648 | tf_op jit(solution)/shard_map/ppermute | solution.py:747
  294.8 15.5 %collective-permute-start.33 = (bf16[320,768]{1,0:T(8,128)(2,1)S(1)}, bf16[320,768]{1,0:T(8,128)(2,1)S(1)}, u32[]{:S(2)}, u32[]{:S(2)}) collective-permute-start(bf16[320,768]{1,0:T(8,128)(2,1)S(1)} %join_quarters.1.own), channel_id=1, source_target_pairs={{0,4},{4,0},{8,12},{12,8},{16,20},{20,16},{24,28},{28,24},{1,5},{5... | collective-permute-start | bytes 1474568 | tf_op jit(solution)/shard_map/ppermute | solution.py:747
  (2 other events, 1.6 us)

commit v2 on v1

--- a/solution.py
+++ b/solution.py
@@ -575,13 +575,15 @@
     width = half // 2
 
     copies = attention_copies((a0, a1), sems, wout=wout)
+    carried = pltpu.make_async_copy(sums_in, qkv_sum, sems.at[15]) if start else None
 
     @pl.when(block == 0)
     def _():
         start_all(copies)
+        if start:
+            carried.start()
         wait_all(copies)
         if start:
-            qkv_sum[...] = sums_in[...]
             vec_sum[...] = vec_in[...]
         else:
             clear(qkv_sum)
@@ -592,13 +594,21 @@
     vec_sum[0] += fold_rows(low_qkv[:, 0:half].astype(F32))
     vec_sum[1] += fold_rows(low_qkv[:, 2 * half : 3 * half].astype(F32))
 
+    if start:
+
+        @pl.when(block == 0)
+        def _():
+            carried.wait()
+
     for k in range(3):
         qkv_sum[k] += tn(low_qkv[:, k * half : (k + 1) * half], x[...])
 
     @pl.when(block == pl.num_programs(0) - 1)
     def _():
         if not start:
-            qkv_out[...] = qkv_sum[...]
+            leaving = pltpu.make_async_copy(qkv_sum, qkv_out, sems.at[15])
+            leaving.start()
+            leaving.wait()
             vec_out[...] = vec_sum[...]
         else:
             index = lax.broadcasted_iota(jnp.int32, (16, 1), 0)
@@ -944,7 +954,7 @@
 
     qkv_rows = 3 * width + 64
     sums = [sds((3, half, d), F32), sds((2, 8, half), F32)]
-    sum_specs = [const_spec(v.shape) for v in sums]
+    sum_specs = [any_spec(), const_spec(sums[1].shape)]
 
     def near_backward(start, count, extra, extra_specs, outs, out_specs, alias):
         return spread(

time: 313 us -> 312 us (level)
  no operation moved by 1% of the time
where the time goes in v2:
time: 312 us; the launch traced here: 311 us
  Pallas kernels  233 us (75%)
  starting transfers between devices  36.6 us (12%)
  waiting for transfers between devices  30.9 us (10%)
  local copies, waits for them, and re-layouts  8.03 us (3%)
    pallas_call x1, Pallas kernels, per_device(): spread(functools.partial(ffn_forward_kernel, short_blocks), 'ffn_forward'...  46.3 us
    pallas_call x1, Pallas kernels, per_device(): spread(ffn_backward_kernel, 'ffn_backward', (blocks,), [row_spec, own_spe...  40.4 us
    pallas_call x2, Pallas kernels, far_backward(): spread(functools.partial(attention_input_kernel, start, short_blocks), 'a...  37.7 us
    pallas_call x2, Pallas kernels, near_backward(): spread(functools.partial(attention_backward_kernel, start, short_blocks),...  35.5 us
    pallas_call x2, Pallas kernels, far_forward(): spread(functools.partial(attention_finish_kernel, start, count, short_blo...  31.5 us
    ppermute x28, waiting for transfers between devices, swap(): return lax.ppermute(values, axis, [(i, i ^ bit) for i in range(size)])  30.9 us
    ppermute x28, starting transfers between devices, swap(): return lax.ppermute(values, axis, [(i, i ^ bit) for i in range(size)])  25.3 us
    pallas_call x1, Pallas kernels, per_device(): spread(functools.partial(attention_forward_kernel, 0, blocks, short_block...  21.3 us
  transfers between devices with their start and end apart: 34, of which 11 were waited for; matrix products, arithmetic and copies ran while one was open for 1% of the time, Pallas kernels for 58%

profile of v2, /device:TPU:0, one launch (start us, length us, event | category | flops | bytes accessed | tf_op | source)
XLA Modules:
  0.0 311.2 jit_solution(7401954913683361560)
XLA Ops:
  0.7 2.5 pack.1
  3.7 2.6 collective-permute-start.1
  7.6 1.1 constant_dynamic-slice_fusion
  8.7 1.0 copy-done.7
  9.7 21.3 %attention_near.1 = (bf16[2048,1152]{1,0:T(8,128)(2,1)}, bf16[2048,384]{1,0:T(8,128)(2,1)}, f32[32,512]{1,0:T(8,128)}) custom-call(s32[1]{0:T(128)} %bitcast.core, s32[16]{0:T(128)} %slen.15, s32[4]{0:T(128)} %llen.15, s32[1]{0:T(128)S(6)} %copy.56.scount, s32[1]{0:T(128)S(6)} %copy.57.lcount, bf16[4096,768]{1,0:T(8,128)(2,1)} %x.9, ...), custom_call_target="tpu_custom_call" | custom-call | flops 4630511616 | bytes 12582912 | tf_op jit(solution)/shard_map/attention_near/pallas_call | solution.py:803
  31.0 2.6 collective-permute-done.1.a2.rest_12_
  33.6 2.9 collective-permute-done.2.a3.rest_13_
  36.6 1.8 collective-permute-start.3
  38.6 14.5 %attention_far.2 = (bf16[2048,1152]{1,0:T(8,128)(2,1)}, bf16[2048,384]{1,0:T(8,128)(2,1)}, f32[32,512]{1,0:T(8,128)}, bf16[2048,768]{1,0:T(8,128)(2,1)}, f32[2048,128]{1,0:T(8,128)}) custom-call(s32[1]{0:T(128)} %bitcast.core, s32[16]{0:T(128)} %slen.15, s32[4]{0:T(128)} %llen.15, s32[1]{0:T(128)S(6)} %copy.56.scount, s32[1]{0:T(128)S(6)} %copy.57.lcount, ...), custom_call_target="tpu_custom_call" | custom-call | flops 3523215360 | bytes 7864320 | tf_op jit(solution)/shard_map/attention_far/pallas_call | solution.py:817
  53.7 1.7 collective-permute-start.5
  55.4 17.1 %attention_far.3 = (bf16[2048,1152]{1,0:T(8,128)(2,1)}, bf16[2048,384]{1,0:T(8,128)(2,1)}, f32[32,512]{1,0:T(8,128)}, bf16[2048,768]{1,0:T(8,128)(2,1)}, f32[2048,128]{1,0:T(8,128)}) custom-call(s32[1]{0:T(128)} %bitcast.core, s32[16]{0:T(128)} %slen.15, s32[4]{0:T(128)} %llen.15, ...), custom_call_target="tpu_custom_call", output_to_operand_aliasing={{0}: (12, {}), {1}: (13, {}), {2}: (14, {}), {3}: (15, {}),... | custom-call | flops 3523215360 | bytes 7864320 | tf_op jit(solution)/shard_map/attention_far/pallas_call | solution.py:817
  72.5 5.1 %collective-permute-done.7.rest_8_ = bf16[768,768]{1,0:T(8,128)(2,1)} collective-permute-done((bf16[768,768]{1,0:T(8,128)(2,1)}, bf16[768,768]{1,0:T(8,128)(2,1)}, u32[]{:S(2)}, u32[]{:S(2)}) %collective-permute-start.7) | collective-permute-done | bytes 1179680 | tf_op jit(solution)/shard_map/ppermute | solution.py:757
  78.2 3.1 %collective-permute-done.9.rest_5_ = bf16[768,384]{1,0:T(8,128)(2,1)S(1)} collective-permute-done((bf16[768,384]{1,0:T(8,128)(2,1)S(1)}, bf16[768,384]{1,0:T(8,128)(2,1)S(1)}, u32[]{:S(2)}, u32[]{:S(2)}) %collective-permute-start.9) | collective-permute-done | bytes 589856 | tf_op jit(solution)/shard_map/ppermute | solution.py:757
  81.3 0.8 copy-done.15
  82.2 1.0 copy-done.11
  83.2 46.3 %ffn_forward.1 = (bf16[4096,768]{1,0:T(8,128)(2,1)}, bf16[2048,768]{1,0:T(8,128)(2,1)}, bf16[2048,768]{1,0:T(8,128)(2,1)}, bf16[2048,3072]{1,0:T(8,128)(2,1)}, b...) custom-call(s32[1]{0:T(128)} %bitcast.core, s32[16]{0:T(128)} %slen.15, s32[4]{0:T(128)} %llen.15, ...), custom_call_target="tpu_custom_call" | custom-call | flops 24159191040 | bytes 31457280 | tf_op jit(solution)/shard_map/ffn_forward/pallas_call | solution.py:846
  129.7 2.9 collective-permute-done.11.partner
  132.6 1.3 copy-done.1
  134.4 1.7 collective-permute-start.12
  136.1 40.4 %ffn_backward.1 = (bf16[2048,768]{1,0:T(8,128)(2,1)}, bf16[1024,768]{1,0:T(8,128)(2,1)}, bf16[1024,768]{1,0:T(8,128)(2,1)}) custom-call(s32[1]{0:T(128)} %bitcast.1.at.side, bf16[2048,768]{1,0:T(8,128)(2,1)} %get-tuple-element.163.grad_low, bf16[2048,3072]{1,0:T(8,128)(2,1)} %get-tuple-element.164.slope, bf16[2048,768]{1,0:T(8,128)(2,1)} %get-tuple-element.150.normed, ...), custom_call_target="tpu_custom_call" | custom-call | flops 24159191040 | bytes 25165824 | tf_op jit(solution)/shard_map/ffn_backward/pallas_call | solution.py:938
  176.9 3.5 %collective-permute-done.14.partner = bf16[1024,768]{1,0:T(8,128)(2,1)S(1)} collective-permute-done((bf16[1024,768]{1,0:T(8,128)(2,1)}, bf16[1024,768]{1,0:T(8,128)(2,1)S(1)}, u32[]{:S(2)}, u32[]{:S(2)}) %collective-permute-start.14) | collective-permute-done | bytes 1572896 | tf_op jit(solution)/shard_map/ppermute | solution.py:757
  181.3 3.8 %collective-permute-start.15 = (bf16[384,768]{1,0:T(8,128)(2,1)S(1)}, bf16[384,768]{1,0:T(8,128)(2,1)S(1)}, u32[]{:S(2)}, u32[]{:S(2)}) collective-permute-start(bf16[384,768]{1,0:T(8,128)(2,1)S(1)} %add.28.refs_0_), channel_id=1, source_target_pairs={{0,8},{4,12},{24,16},{28,20},{1,9},{5,13},{25,17},{29,21},{2,10},{... | collective-permute-start | bytes 1769480 | tf_op jit(solution)/shard_map/ppermute | solution.py:867
  185.0 15.4 %attention_near_backward.2 = (bf16[1024,1152]{1,0:T(8,128)(2,1)}, f32[3,384,768]{2,1,0:T(8,128)}, f32[2,8,384]{2,1,0:T(8,128)}) custom-call(s32[1]{0:T(128)} %bitcast.core, s32[16]{0:T(128)} %slen.15, s32[4]{0:T(128)} %llen.15, s32[1]{0:T(128)S(6)} %copy.56.scount, s32[1]{0:T(128)S(6)} %copy.57.lcount, bf16[2048,768]{1,0:T(8,128)(2,1)} %get-tuple-element.180.hidden_low, ...), custom_call_target="tpu_custom_call" | custom-call | flops 4278190080 | bytes 12582912 | tf_op jit(solution)/shard_map/attention_near_backward/pallas_call | solution.py:960
  200.8 3.5 %collective-permute-start.18 = (bf16[512,768]{1,0:T(8,128)(2,1)S(1)}, bf16[512,768]{1,0:T(8,128)(2,1)S(1)}, u32[]{:S(2)}, u32[]{:S(2)}) collective-permute-start(bf16[512,768]{1,0:T(8,128)(2,1)S(1)} %add.30.refs_0_), channel_id=1, source_target_pairs={{0,8},{4,12},{24,16},{28,20},{1,9},{5,13},{25,17},{29,21},{2,10},{... | collective-permute-start | bytes 2359304 | tf_op jit(solution)/shard_map/ppermute | solution.py:867
  205.2 20.1 %attention_near_backward.3 = (bf16[1024,1152]{1,0:T(8,128)(2,1)}, bf16[640,768]{1,0:T(8,128)(2,1)}, bf16[640,768]{1,0:T(8,128)(2,1)}) custom-call(s32[1]{0:T(128)} %bitcast.core, s32[16]{0:T(128)} %slen.15, s32[4]{0:T(128)} %llen.15, s32[1]{0:T(128)S(6)} %copy.56.scount, s32[1]{0:T(128)S(6)} %copy.57.lcount, ...), custom_call_target="tpu_custom_call" | custom-call | flops 4278190080 | bytes 12582912 | tf_op jit(solution)/shard_map/attention_near_backward/pallas_call | solution.py:960
  225.7 0.7 copy-done.12
  227.2 1.3 collective-permute-start.20
  229.0 1.1 halves.5
  230.7 15.8 %attention_far_backward.2 = (bf16[2048,768]{1,0:T(8,128)(2,1)}, f32[4096,768]{1,0:T(8,128)}) custom-call(s32[1]{0:T(128)} %bitcast.core, s32[16]{0:T(128)} %slen.15, s32[4]{0:T(128)} %llen.15, s32[1]{0:T(128)S(6)} %copy.56.scount, s32[1]{0:T(128)S(6)} %copy.57.lcount, bf16[2048,768]{1,0:T(8,128)(2,1)} %get-tuple-element.180.hidden_low, ...), custom_call_target="tpu_custom_call" | custom-call | flops 5486149632 | bytes 12582912 | tf_op jit(solution)/shard_map/attention_far_backward/pallas_call | solution.py:986
  246.6 0.8 copy-done.5
  247.6 1.3 collective-permute-start.24
  248.9 1.5 collective-permute-start.23
  250.6 3.4 %collective-permute-start.25 = (bf16[80,768]{1,0:T(8,128)(2,1)S(1)}, bf16[80,768]{1,0:T(8,128)(2,1)S(1)}, u32[]{:S(2)}, u32[]{:S(2)}) collective-permute-start(bf16[80,768]{1,0:T(8,128)(2,1)S(1)} %get-tuple-element.209), channel_id=1, source_target_pairs={{0,8},{4,12},{8,0},{12,4},{16,24},{20,28},{24,16},{28,20},{1,9},{5... | collective-permute-start | bytes 368648 | tf_op jit(solution)/shard_map/ppermute | solution.py:757
  254.0 1.1 collective-permute-start.26
  255.0 1.4 collective-permute-start.27
  256.4 21.9 %attention_far_backward.3 = (bf16[2048,768]{1,0:T(8,128)(2,1)}, f32[4096,768]{1,0:T(8,128)}) custom-call(s32[1]{0:T(128)} %bitcast.core, s32[16]{0:T(128)} %slen.15, s32[4]{0:T(128)} %llen.15, s32[1]{0:T(128)S(6)} %copy.56.scount, s32[1]{0:T(128)S(6)} %copy.57.lcount, ...), custom_call_target="tpu_custom_call", output_to_operand_aliasing={{0}: (14, {}), {1}: (15, {})} | custom-call | flops 5486149632 | bytes 12582912 | tf_op jit(solution)/shard_map/attention_far_backward/pallas_call | solution.py:986
  278.6 1.2 collective-permute-start.32
  279.8 2.1 collective-permute-start.30
  282.3 1.9 collective-permute-start.28
  284.2 4.2 %place.2 = bf16[4096,768]{1,0:T(8,128)(2,1)} custom-call(s32[1]{0:T(128)} %bitcast.core, bf16[2048,768]{1,0:T(8,128)(2,1)} %collective-permute-done.13.other, bf16[4096,768]{1,0:T(8,128)(2,1)} %get-tuple-element.224.whole), custom_call_target="tpu_custom_call", output_to_operand_aliasing={{}: (2, {})} | custom-call | bytes 9437184 | tf_op jit(solution)/shard_map/place/pallas_call | solution.py:1012
  288.4 5.2 %collective-permute-done.29.refs_2_ = bf16[80,768]{1,0:T(8,128)(2,1)S(1)} collective-permute-done((bf16[80,768]{1,0:T(8,128)(2,1)S(1)}, bf16[80,768]{1,0:T(8,128)(2,1)S(1)}, u32[]{:S(2)}, u32[]{:S(2)}) %collective-permute-start.29) | collective-permute-done | bytes 122912 | tf_op jit(solution)/shard_map/ppermute | solution.py:757
  293.6 0.9 collective-permute-start.33
  294.6 1.8 finish.5
  296.4 2.6 collective-permute-done.32.other
  299.0 2.1 finish.3
  301.1 5.0 %place.3 = f32[4096,768]{1,0:T(8,128)} custom-call(s32[1]{0:T(128)} %bitcast.core, bf16[2048,768]{1,0:T(8,128)(2,1)} %collective-permute-done.31.other, f32[4096,768]{1,0:T(8,128)} %get-tuple-element.235.whole), custom_call_target="tpu_custom_call", output_to_operand_aliasing={{}: (2, {})} | custom-call | bytes 9437184 | tf_op jit(solution)/shard_map/place/pallas_call | solution.py:1012
  306.8 2.3 collective-permute-done.33.other
  309.1 1.5 finish.4
  (84 shorter events, 9.7 us)
Async XLA Ops:
  3.2 5.5 %collective-permute-start = (bf16[784,768]{1,0:T(8,128)(2,1)}, bf16[784,768]{1,0:T(8,128)(2,1)S(1)}, u32[]{:S(2)}, u32[]{:S(2)}) collective-permute-start(bf16[784,768]{1,0:T(8,128)(2,1)} %get-tuple-element.132.a0.rest_10_), channel_id=1, source_target_pairs={{0,1},{1,0},{2,3},{3,2},{4,5},{5,4},{6,7},{7,6},{8,9},{9,8},{10,11... | collective-permute-start | bytes 3612680 | tf_op jit(solution)/shard_map/ppermute | solution.py:757
  3.7 29.9 %collective-permute-start.1 = (bf16[784,768]{1,0:T(8,128)(2,1)}, bf16[784,768]{1,0:T(8,128)(2,1)S(1)}, u32[]{:S(2)}, u32[]{:S(2)}) collective-permute-start(bf16[784,768]{1,0:T(8,128)(2,1)} %get-tuple-element.132.a0.rest_10_), channel_id=1, source_target_pairs={{0,2},{1,3},{2,0},{3,1},{4,6},{5,7},{6,4},{7,5},{8,10},{9,11},{10,... | collective-permute-start | bytes 3612680 | tf_op jit(solution)/shard_map/ppermute | solution.py:757
  8.7 1.0 copy-start.7
  33.6 5.1 %copy-start.8 = (bf16[784,768]{1,0:T(8,128)(2,1)}, bf16[784,768]{1,0:T(8,128)(2,1)S(1)}, u32[]{:S(2)}) copy-start(bf16[784,768]{1,0:T(8,128)(2,1)S(1)} %collective-permute-done.1.a2.rest_12_) | copy-start | bytes 3612676
  33.6 2.9 collective-permute-start.2
  36.4 2.2 copy-start.9
  36.4 16.7 %collective-permute-start.4 = (bf16[768,768]{1,0:T(8,128)(2,1)}, bf16[768,768]{1,0:T(8,128)(2,1)}, u32[]{:S(2)}, u32[]{:S(2)}) collective-permute-start(bf16[768,768]{1,0:T(8,128)(2,1)} %rest_0_.3), channel_id=1, source_target_pairs={{0,1},{1,0},{2,3},{3,2},{4,5},{5,4},{6,7},{7,6},{8,9},{9,8},{10,11... | collective-permute-start | bytes 3538952 | tf_op jit(solution)/shard_map/ppermute | solution.py:757
  36.6 16.5 %collective-permute-start.3 = (bf16[768,384]{1,0:T(8,128)(2,1)S(1)}, bf16[768,384]{1,0:T(8,128)(2,1)}, u32[]{:S(2)}, u32[]{:S(2)}) collective-permute-start(bf16[768,384]{1,0:T(8,128)(2,1)S(1)} %constant_dynamic-slice_fusion), channel_id=1, source_target_pairs={{0,2},{1,3},{2,0},{3,1},{4,6},{5,7},{6,4},{7,5},{8,10},{9,11},{10,... | collective-permute-start | bytes 1769480 | tf_op jit(solution)/shard_map/ppermute | solution.py:757
  38.4 39.2 %collective-permute-start.7 = (bf16[768,768]{1,0:T(8,128)(2,1)}, bf16[768,768]{1,0:T(8,128)(2,1)}, u32[]{:S(2)}, u32[]{:S(2)}) collective-permute-start(bf16[768,768]{1,0:T(8,128)(2,1)} %rest_6_.3), channel_id=1, source_target_pairs={{0,2},{1,3},{2,0},{3,1},{4,6},{5,7},{6,4},{7,5},{8,10},{9,11},{10,... | collective-permute-start | bytes 3538952 | tf_op jit(solution)/shard_map/ppermute | solution.py:757
  53.1 24.5 %collective-permute-start.8 = (bf16[768,768]{1,0:T(8,128)(2,1)}, bf16[768,768]{1,0:T(8,128)(2,1)S(1)}, u32[]{:S(2)}, u32[]{:S(2)}) collective-permute-start(bf16[768,768]{1,0:T(8,128)(2,1)} %rest_6_.3), channel_id=1, source_target_pairs={{0,1},{1,0},{2,3},{3,2},{4,5},{5,4},{6,7},{7,6},{8,9},{9,8},{10,11... | collective-permute-start | bytes 3538952 | tf_op jit(solution)/shard_map/ppermute | solution.py:757
  53.2 24.4 %collective-permute-start.6 = (bf16[768,384]{1,0:T(8,128)(2,1)}, bf16[768,384]{1,0:T(8,128)(2,1)S(1)}, u32[]{:S(2)}, u32[]{:S(2)}) collective-permute-start(bf16[768,384]{1,0:T(8,128)(2,1)} %collective-permute-done.3.rest_2_), channel_id=1, source_target_pairs={{0,1},{1,0},{2,3},{3,2},{4,5},{5,4},{6,7},{7,6},{8,9},{9,8},{10,11... | collective-permute-start | bytes 1769480 | tf_op jit(solution)/shard_map/ppermute | solution.py:757
  53.7 23.9 %collective-permute-start.5 = (bf16[768,384]{1,0:T(8,128)(2,1)}, bf16[768,384]{1,0:T(8,128)(2,1)S(1)}, u32[]{:S(2)}, u32[]{:S(2)}) collective-permute-start(bf16[768,384]{1,0:T(8,128)(2,1)} %collective-permute-done.3.rest_2_), channel_id=1, source_target_pairs={{0,4},{4,0},{8,12},{12,8},{16,20},{20,16},{24,28},{28,24},{1,5},{5... | collective-permute-start | bytes 1769480 | tf_op jit(solution)/shard_map/ppermute | solution.py:757
  77.6 4.6 %copy-start.13 = (bf16[768,384]{1,0:T(8,128)(2,1)}, bf16[768,384]{1,0:T(8,128)(2,1)S(1)}, u32[]{:S(2)}) copy-start(bf16[768,384]{1,0:T(8,128)(2,1)S(1)} %collective-permute-done.6.rest_3_) | copy-start | bytes 1769476
  77.6 4.6 %copy-start.14 = (bf16[768,384]{1,0:T(8,128)(2,1)}, bf16[768,384]{1,0:T(8,128)(2,1)S(1)}, u32[]{:S(2)}) copy-start(bf16[768,384]{1,0:T(8,128)(2,1)S(1)} %collective-permute-done.5.rest_4_) | copy-start | bytes 1769476
  77.6 4.5 %copy-start.10 = (bf16[768,768]{1,0:T(8,128)(2,1)}, bf16[768,768]{1,0:T(8,128)(2,1)S(1)}, u32[]{:S(2)}) copy-start(bf16[768,768]{1,0:T(8,128)(2,1)S(1)} %collective-permute-done.8.rest_7_) | copy-start | bytes 3538948
  77.6 4.5 %collective-permute-start.10 = (bf16[768,768]{1,0:T(8,128)(2,1)}, bf16[768,768]{1,0:T(8,128)(2,1)S(1)}, u32[]{:S(2)}, u32[]{:S(2)}) collective-permute-start(bf16[768,768]{1,0:T(8,128)(2,1)} %collective-permute-done.7.rest_8_), channel_id=1, source_target_pairs={{0,1},{1,0},{2,3},{3,2},{4,5},{5,4},{6,7},{7,6},{8,9},{9,8},{10,11... | collective-permute-start | bytes 3538952 | tf_op jit(solution)/shard_map/ppermute | solution.py:757
  77.7 3.6 %collective-permute-start.9 = (bf16[768,384]{1,0:T(8,128)(2,1)S(1)}, bf16[768,384]{1,0:T(8,128)(2,1)S(1)}, u32[]{:S(2)}, u32[]{:S(2)}) collective-permute-start(bf16[768,384]{1,0:T(8,128)(2,1)S(1)} %collective-permute-done.5.rest_4_), channel_id=1, source_target_pairs={{0,1},{1,0},{2,3},{3,2},{4,5},{5,4},{6,7},{7,6},{8,9},{9,8},{10,11... | collective-permute-start | bytes 1769480 | tf_op jit(solution)/shard_map/ppermute | solution.py:757
  82.1 1.0 copy-start.11
  129.5 3.1 %collective-permute-start.11 = (bf16[768,768]{1,0:T(8,128)(2,1)}, bf16[768,768]{1,0:T(8,128)(2,1)S(1)}, u32[]{:S(2)}, u32[]{:S(2)}) collective-permute-start(bf16[768,768]{1,0:T(8,128)(2,1)} %get-tuple-element.161), channel_id=1, source_target_pairs={{0,1},{1,0},{2,3},{3,2},{4,5},{5,4},{6,7},{7,6},{8,9},{9,8},{10,11... | collective-permute-start | bytes 3538952 | tf_op jit(solution)/shard_map/ppermute | solution.py:757
  132.6 1.3 copy-start.1
  134.2 42.3 %collective-permute-start.13 = (bf16[2048,768]{1,0:T(8,128)(2,1)}, bf16[2048,768]{1,0:T(8,128)(2,1)}, u32[]{:S(2)}, u32[]{:S(2)}) collective-permute-start(bf16[2048,768]{1,0:T(8,128)(2,1)} %get-tuple-element.171), channel_id=1, source_target_pairs={{0,1},{1,0},{2,3},{3,2},{4,5},{5,4},{6,7},{7,6},{8,9},{9,8},{10,11... | collective-permute-start | bytes 9437192 | tf_op jit(solution)/shard_map/ppermute | solution.py:757
  134.4 42.1 %collective-permute-start.12 = (bf16[384,768]{1,0:T(8,128)(2,1)S(1)}, bf16[384,768]{1,0:T(8,128)(2,1)S(1)}, u32[]{:S(2)}, u32[]{:S(2)}) collective-permute-start(bf16[384,768]{1,0:T(8,128)(2,1)S(1)} %get-tuple-element.162), channel_id=1, source_target_pairs={{0,4},{4,0},{8,12},{12,8},{16,20},{20,16},{24,28},{28,24},{1,5},{5... | collective-permute-start | bytes 1769480 | tf_op jit(solution)/shard_map/ppermute | solution.py:757
  176.5 3.9 %copy-start = (bf16[1024,768]{1,0:T(8,128)(2,1)S(1)}, bf16[1024,768]{1,0:T(8,128)(2,1)}, u32[]{:S(2)}) copy-start(bf16[1024,768]{1,0:T(8,128)(2,1)} %get-tuple-element.174.mine) | copy-start | bytes 4718596
  176.7 3.7 %collective-permute-start.14 = (bf16[1024,768]{1,0:T(8,128)(2,1)}, bf16[1024,768]{1,0:T(8,128)(2,1)S(1)}, u32[]{:S(2)}, u32[]{:S(2)}) collective-permute-start(bf16[1024,768]{1,0:T(8,128)(2,1)} %get-tuple-element.178), channel_id=1, source_target_pairs={{0,1},{1,0},{2,3},{3,2},{4,5},{5,4},{6,7},{7,6},{8,9},{9,8},{10,11... | collective-permute-start | bytes 4718600 | tf_op jit(solution)/shard_map/ppermute | solution.py:757
  180.9 19.6 %collective-permute-start.16 = (bf16[512,768]{1,0:T(8,128)(2,1)S(1)}, bf16[512,768]{1,0:T(8,128)(2,1)S(1)}, u32[]{:S(2)}, u32[]{:S(2)}) collective-permute-start(bf16[512,768]{1,0:T(8,128)(2,1)S(1)} %get-tuple-element.179), channel_id=1, source_target_pairs={{0,4},{4,0},{8,12},{12,8},{16,20},{20,16},{24,28},{28,24},{1,5},{5... | collective-permute-start | bytes 2359304 | tf_op jit(solution)/shard_map/ppermute | solution.py:757
  181.3 19.2 %collective-permute-start.15 = (bf16[384,768]{1,0:T(8,128)(2,1)S(1)}, bf16[384,768]{1,0:T(8,128)(2,1)S(1)}, u32[]{:S(2)}, u32[]{:S(2)}) collective-permute-start(bf16[384,768]{1,0:T(8,128)(2,1)S(1)} %add.28.refs_0_), channel_id=1, source_target_pairs={{0,8},{4,12},{24,16},{28,20},{1,9},{5,13},{25,17},{29,21},{2,10},{... | collective-permute-start | bytes 1769480 | tf_op jit(solution)/shard_map/ppermute | solution.py:867
  200.8 24.5 %collective-permute-start.18 = (bf16[512,768]{1,0:T(8,128)(2,1)S(1)}, bf16[512,768]{1,0:T(8,128)(2,1)S(1)}, u32[]{:S(2)}, u32[]{:S(2)}) collective-permute-start(bf16[512,768]{1,0:T(8,128)(2,1)S(1)} %add.30.refs_0_), channel_id=1, source_target_pairs={{0,8},{4,12},{24,16},{28,20},{1,9},{5,13},{25,17},{29,21},{2,10},{... | collective-permute-start | bytes 2359304 | tf_op jit(solution)/shard_map/ppermute | solution.py:867
  204.5 20.8 %collective-permute-start.17 = (bf16[384,768]{1,0:T(8,128)(2,1)S(1)}, bf16[384,768]{1,0:T(8,128)(2,1)S(1)}, u32[]{:S(2)}, u32[]{:S(2)}) collective-permute-start(bf16[384,768]{1,0:T(8,128)(2,1)S(1)} %add.29.refs_0_), channel_id=1, source_target_pairs={{8,16},{12,20},{16,8},{20,12},{9,17},{13,21},{17,9},{21,13},{10,18... | collective-permute-start | bytes 1769480 | tf_op jit(solution)/shard_map/ppermute | solution.py:867
  225.3 1.2 copy-start.12
  225.3 3.8 %copy-start.2 = (bf16[640,768]{1,0:T(8,128)(2,1)S(1)}, bf16[640,768]{1,0:T(8,128)(2,1)}, u32[]{:S(2)}) copy-start(bf16[640,768]{1,0:T(8,128)(2,1)} %get-tuple-element.193.mine) | copy-start | bytes 2949124
  226.5 2.6 collective-permute-start.19
  226.5 20.1 %collective-permute-start.21 = (bf16[512,768]{1,0:T(8,128)(2,1)S(1)}, bf16[512,768]{1,0:T(8,128)(2,1)S(1)}, u32[]{:S(2)}, u32[]{:S(2)}) collective-permute-start(bf16[512,768]{1,0:T(8,128)(2,1)S(1)} %add.32.refs_0_), channel_id=1, source_target_pairs={{8,16},{12,20},{16,8},{20,12},{9,17},{13,21},{17,9},{21,13},{10,18... | collective-permute-start | bytes 2359304 | tf_op jit(solution)/shard_map/ppermute | solution.py:867
  227.2 19.3 %collective-permute-start.20 = (bf16[384,768]{1,0:T(8,128)(2,1)S(1)}, bf16[384,768]{1,0:T(8,128)(2,1)S(1)}, u32[]{:S(2)}, u32[]{:S(2)}) collective-permute-start(bf16[384,768]{1,0:T(8,128)(2,1)S(1)} %add.31.own), channel_id=1, source_target_pairs={{8,0},{12,4},{16,24},{20,28},{9,1},{13,5},{17,25},{21,29},{10,2},{... | collective-permute-start | bytes 1769480 | tf_op jit(solution)/shard_map/ppermute | solution.py:867
  230.1 16.4 %copy-start.3 = (bf16[320,768]{1,0:T(8,128)(2,1)}, bf16[320,768]{1,0:T(8,128)(2,1)S(1)}, u32[]{:S(2)}) copy-start(bf16[320,768]{1,0:T(8,128)(2,1)S(1)} %get-tuple-element.198.keep) | copy-start | bytes 1474564
  230.1 16.4 %collective-permute-start.22 = (bf16[320,768]{1,0:T(8,128)(2,1)}, bf16[320,768]{1,0:T(8,128)(2,1)S(1)}, u32[]{:S(2)}, u32[]{:S(2)}) collective-permute-start(bf16[320,768]{1,0:T(8,128)(2,1)} %get-tuple-element.203), channel_id=1, source_target_pairs={{0,4},{4,0},{8,12},{12,8},{16,20},{20,16},{24,28},{28,24},{1,5},{5... | collective-permute-start | bytes 1474568 | tf_op jit(solution)/shard_map/ppermute | solution.py:757
  246.5 3.9 %copy-start.4 = (bf16[320,768]{1,0:T(8,128)(2,1)S(1)}, bf16[320,768]{1,0:T(8,128)(2,1)}, u32[]{:S(2)}) copy-start(bf16[320,768]{1,0:T(8,128)(2,1)} %copy-done.3) | copy-start | bytes 1474564
  247.3 3.1 %copy-start.6 = (bf16[320,768]{1,0:T(8,128)(2,1)S(1)}, bf16[320,768]{1,0:T(8,128)(2,1)}, u32[]{:S(2)}) copy-start(bf16[320,768]{1,0:T(8,128)(2,1)} %copy-done.5) | copy-start | bytes 1474564
  247.6 30.8 %collective-permute-start.24 = (bf16[512,768]{1,0:T(8,128)(2,1)S(1)}, bf16[512,768]{1,0:T(8,128)(2,1)S(1)}, u32[]{:S(2)}, u32[]{:S(2)}) collective-permute-start(bf16[512,768]{1,0:T(8,128)(2,1)S(1)} %add.33.own), channel_id=1, source_target_pairs={{8,0},{12,4},{16,24},{20,28},{9,1},{13,5},{17,25},{21,29},{10,2},{... | collective-permute-start | bytes 2359304 | tf_op jit(solution)/shard_map/ppermute | solution.py:867
  248.9 29.5 %collective-permute-start.23 = (bf16[384,768]{1,0:T(8,128)(2,1)S(1)}, bf16[384,768]{1,0:T(8,128)(2,1)S(1)}, u32[]{:S(2)}, u32[]{:S(2)}) collective-permute-start(bf16[384,768]{1,0:T(8,128)(2,1)S(1)} %choose.2.own), channel_id=1, source_target_pairs={{0,4},{4,0},{8,12},{12,8},{16,20},{20,16},{24,28},{28,24},{1,5},{5... | collective-permute-start | bytes 1769480 | tf_op jit(solution)/shard_map/ppermute | solution.py:757
  250.6 27.8 %collective-permute-start.25 = (bf16[80,768]{1,0:T(8,128)(2,1)S(1)}, bf16[80,768]{1,0:T(8,128)(2,1)S(1)}, u32[]{:S(2)}, u32[]{:S(2)}) collective-permute-start(bf16[80,768]{1,0:T(8,128)(2,1)S(1)} %get-tuple-element.209), channel_id=1, source_target_pairs={{0,8},{4,12},{8,0},{12,4},{16,24},{20,28},{24,16},{28,20},{1,9},{5... | collective-permute-start | bytes 368648 | tf_op jit(solution)/shard_map/ppermute | solution.py:757
  254.0 24.4 %collective-permute-start.26 = (bf16[80,768]{1,0:T(8,128)(2,1)S(1)}, bf16[80,768]{1,0:T(8,128)(2,1)S(1)}, u32[]{:S(2)}, u32[]{:S(2)}) collective-permute-start(bf16[80,768]{1,0:T(8,128)(2,1)S(1)} %get-tuple-element.216), channel_id=1, source_target_pairs={{0,16},{4,20},{8,24},{12,28},{16,0},{20,4},{24,8},{28,12},{1,17},{... | collective-permute-start | bytes 368648 | tf_op jit(solution)/shard_map/ppermute | solution.py:757
  255.0 23.3 %collective-permute-start.27 = (bf16[80,768]{1,0:T(8,128)(2,1)S(1)}, bf16[80,768]{1,0:T(8,128)(2,1)S(1)}, u32[]{:S(2)}, u32[]{:S(2)}) collective-permute-start(bf16[80,768]{1,0:T(8,128)(2,1)S(1)} %get-tuple-element.217), channel_id=1, source_target_pairs={{0,24},{4,28},{8,16},{12,20},{16,8},{20,12},{24,0},{28,4},{1,25},{... | collective-permute-start | bytes 368648 | tf_op jit(solution)/shard_map/ppermute | solution.py:757
  278.5 15.0 %collective-permute-start.31 = (bf16[2048,768]{1,0:T(8,128)(2,1)}, bf16[2048,768]{1,0:T(8,128)(2,1)}, u32[]{:S(2)}, u32[]{:S(2)}) collective-permute-start(bf16[2048,768]{1,0:T(8,128)(2,1)} %get-tuple-element.226), channel_id=1, source_target_pairs={{0,1},{1,0},{2,3},{3,2},{4,5},{5,4},{6,7},{7,6},{8,9},{9,8},{10,11... | collective-permute-start | bytes 9437192 | tf_op jit(solution)/shard_map/ppermute | solution.py:757
  278.6 20.4 %collective-permute-start.32 = (bf16[512,768]{1,0:T(8,128)(2,1)S(1)}, bf16[512,768]{1,0:T(8,128)(2,1)S(1)}, u32[]{:S(2)}, u32[]{:S(2)}) collective-permute-start(bf16[512,768]{1,0:T(8,128)(2,1)S(1)} %choose.3.own), channel_id=1, source_target_pairs={{0,4},{4,0},{8,12},{12,8},{16,20},{20,16},{24,28},{28,24},{1,5},{5... | collective-permute-start | bytes 2359304 | tf_op jit(solution)/shard_map/ppermute | solution.py:757
  279.8 8.6 %collective-permute-start.30 = (bf16[80,768]{1,0:T(8,128)(2,1)S(1)}, bf16[80,768]{1,0:T(8,128)(2,1)S(1)}, u32[]{:S(2)}, u32[]{:S(2)}) collective-permute-start(bf16[80,768]{1,0:T(8,128)(2,1)S(1)} %add.34.refs_0_), channel_id=1, source_target_pairs={{0,24},{4,28},{8,16},{12,20},{16,8},{20,12},{24,0},{28,4},{1,25},{... | collective-permute-start | bytes 368648 | tf_op jit(solution)/shard_map/ppermute | solution.py:757
  281.9 11.7 %collective-permute-start.29 = (bf16[80,768]{1,0:T(8,128)(2,1)S(1)}, bf16[80,768]{1,0:T(8,128)(2,1)S(1)}, u32[]{:S(2)}, u32[]{:S(2)}) collective-permute-start(bf16[80,768]{1,0:T(8,128)(2,1)S(1)} %add.34.refs_0_), channel_id=1, source_target_pairs={{0,16},{4,20},{8,24},{12,28},{16,0},{20,4},{24,8},{28,12},{1,17},{... | collective-permute-start | bytes 368648 | tf_op jit(solution)/shard_map/ppermute | solution.py:757
  282.3 11.3 %collective-permute-start.28 = (bf16[80,768]{1,0:T(8,128)(2,1)S(1)}, bf16[80,768]{1,0:T(8,128)(2,1)S(1)}, u32[]{:S(2)}, u32[]{:S(2)}) collective-permute-start(bf16[80,768]{1,0:T(8,128)(2,1)S(1)} %add.34.refs_0_), channel_id=1, source_target_pairs={{0,8},{4,12},{8,0},{12,4},{16,24},{20,28},{24,16},{28,20},{1,9},{5... | collective-permute-start | bytes 368648 | tf_op jit(solution)/shard_map/ppermute | solution.py:757
  293.6 15.5 %collective-permute-start.33 = (bf16[320,768]{1,0:T(8,128)(2,1)S(1)}, bf16[320,768]{1,0:T(8,128)(2,1)S(1)}, u32[]{:S(2)}, u32[]{:S(2)}) collective-permute-start(bf16[320,768]{1,0:T(8,128)(2,1)S(1)} %join_quarters.1.own), channel_id=1, source_target_pairs={{0,4},{4,0},{8,12},{12,8},{16,20},{20,16},{24,28},{28,24},{1,5},{5... | collective-permute-start | bytes 1474568 | tf_op jit(solution)/shard_map/ppermute | solution.py:757
  (2 other events, 1.6 us)

commit v3 on v2

--- a/solution.py
+++ b/solution.py
@@ -978,9 +978,8 @@
         [sds((qkv_rows, d), BF16)] * 2, [const_spec((qkv_rows, d))] * 2, None,
     )
     low_long, mine, partner = settle(low_long, [down_reduce, up_reduce], mine, partner)
-    ties = [down_reduce.step(), up_reduce.step()]
-    qkv_reduce = Reduction(mine, after(partner, *ties), False)
-    ties += [qkv_reduce.step()]
+    qkv_reduce = Reduction(mine, partner, False)
+    ties = [down_reduce.step(), up_reduce.step(), qkv_reduce.step()]
 
     def far_backward(start, count, low_near, extra, alias):
         return spread(

time: 312 us -> 311 us (level)
  no operation moved by 1% of the time
where the time goes in v3:
time: 311 us
  Pallas kernels  233 us (75%)
  starting transfers between devices  36.8 us (12%)
  waiting for transfers between devices  30.8 us (10%)
  local copies, waits for them, and re-layouts  7.29 us (2%)
    pallas_call x1, Pallas kernels, per_device(): spread(functools.partial(ffn_forward_kernel, short_blocks), 'ffn_forward'...  46.3 us
    pallas_call x1, Pallas kernels, per_device(): spread(ffn_backward_kernel, 'ffn_backward', (blocks,), [row_spec, own_spe...  40.4 us
    pallas_call x2, Pallas kernels, far_backward(): spread(functools.partial(attention_input_kernel, start, short_blocks), 'a...  37.7 us
    pallas_call x2, Pallas kernels, near_backward(): spread(functools.partial(attention_backward_kernel, start, short_blocks),...  35.4 us
    pallas_call x2, Pallas kernels, far_forward(): spread(functools.partial(attention_finish_kernel, start, count, short_blo...  31.5 us
    ppermute x28, waiting for transfers between devices, swap(): return lax.ppermute(values, axis, [(i, i ^ bit) for i in range(size)])  30.7 us
    ppermute x28, starting transfers between devices, swap(): return lax.ppermute(values, axis, [(i, i ^ bit) for i in range(size)])  25.5 us
    pallas_call x1, Pallas kernels, per_device(): spread(functools.partial(attention_forward_kernel, 0, blocks, short_block...  21.3 us
  transfers between devices with their start and end apart: 34, of which 11 were waited for; matrix products, arithmetic and copies ran while one was open for 1% of the time, Pallas kernels for 58%

profile of v3, /device:TPU:0, one launch (start us, length us, event | category | flops | bytes accessed | tf_op | source)
XLA Modules:
  0.0 310.5 jit_solution(3240183453674812288)
XLA Ops:
  0.7 2.5 pack.1
  3.7 2.6 collective-permute-start.1
  7.5 1.1 constant_dynamic-slice_fusion
  8.7 1.0 copy-done.7
  9.7 21.3 %attention_near.1 = (bf16[2048,1152]{1,0:T(8,128)(2,1)}, bf16[2048,384]{1,0:T(8,128)(2,1)}, f32[32,512]{1,0:T(8,128)}) custom-call(s32[1]{0:T(128)} %bitcast.core, s32[16]{0:T(128)} %slen.15, s32[4]{0:T(128)} %llen.15, s32[1]{0:T(128)S(6)} %copy.56.scount, s32[1]{0:T(128)S(6)} %copy.57.lcount, bf16[4096,768]{1,0:T(8,128)(2,1)} %x.9, ...), custom_call_target="tpu_custom_call" | custom-call | flops 4630511616 | bytes 12582912 | tf_op jit(solution)/shard_map/attention_near/pallas_call | solution.py:803
  31.0 2.6 collective-permute-done.1.a2.rest_12_
  33.6 2.9 collective-permute-done.2.a3.rest_13_
  36.6 1.8 collective-permute-start.3
  38.6 14.5 %attention_far.2 = (bf16[2048,1152]{1,0:T(8,128)(2,1)}, bf16[2048,384]{1,0:T(8,128)(2,1)}, f32[32,512]{1,0:T(8,128)}, bf16[2048,768]{1,0:T(8,128)(2,1)}, f32[2048,128]{1,0:T(8,128)}) custom-call(s32[1]{0:T(128)} %bitcast.core, s32[16]{0:T(128)} %slen.15, s32[4]{0:T(128)} %llen.15, s32[1]{0:T(128)S(6)} %copy.56.scount, s32[1]{0:T(128)S(6)} %copy.57.lcount, ...), custom_call_target="tpu_custom_call" | custom-call | flops 3523215360 | bytes 7864320 | tf_op jit(solution)/shard_map/attention_far/pallas_call | solution.py:817
  53.7 1.7 collective-permute-start.5
  55.4 17.1 %attention_far.3 = (bf16[2048,1152]{1,0:T(8,128)(2,1)}, bf16[2048,384]{1,0:T(8,128)(2,1)}, f32[32,512]{1,0:T(8,128)}, bf16[2048,768]{1,0:T(8,128)(2,1)}, f32[2048,128]{1,0:T(8,128)}) custom-call(s32[1]{0:T(128)} %bitcast.core, s32[16]{0:T(128)} %slen.15, s32[4]{0:T(128)} %llen.15, ...), custom_call_target="tpu_custom_call", output_to_operand_aliasing={{0}: (12, {}), {1}: (13, {}), {2}: (14, {}), {3}: (15, {}),... | custom-call | flops 3523215360 | bytes 7864320 | tf_op jit(solution)/shard_map/attention_far/pallas_call | solution.py:817
  72.5 5.1 %collective-permute-done.7.rest_8_ = bf16[768,768]{1,0:T(8,128)(2,1)} collective-permute-done((bf16[768,768]{1,0:T(8,128)(2,1)}, bf16[768,768]{1,0:T(8,128)(2,1)}, u32[]{:S(2)}, u32[]{:S(2)}) %collective-permute-start.7) | collective-permute-done | bytes 1179680 | tf_op jit(solution)/shard_map/ppermute | solution.py:757
  78.2 3.1 %collective-permute-done.9.rest_5_ = bf16[768,384]{1,0:T(8,128)(2,1)S(1)} collective-permute-done((bf16[768,384]{1,0:T(8,128)(2,1)S(1)}, bf16[768,384]{1,0:T(8,128)(2,1)S(1)}, u32[]{:S(2)}, u32[]{:S(2)}) %collective-permute-start.9) | collective-permute-done | bytes 589856 | tf_op jit(solution)/shard_map/ppermute | solution.py:757
  81.3 0.8 copy-done.14
  82.2 1.0 copy-done.11
  83.2 46.3 %ffn_forward.1 = (bf16[4096,768]{1,0:T(8,128)(2,1)}, bf16[2048,768]{1,0:T(8,128)(2,1)}, bf16[2048,768]{1,0:T(8,128)(2,1)}, bf16[2048,3072]{1,0:T(8,128)(2,1)}, b...) custom-call(s32[1]{0:T(128)} %bitcast.core, s32[16]{0:T(128)} %slen.15, s32[4]{0:T(128)} %llen.15, ...), custom_call_target="tpu_custom_call" | custom-call | flops 24159191040 | bytes 31457280 | tf_op jit(solution)/shard_map/ffn_forward/pallas_call | solution.py:846
  129.7 2.9 collective-permute-done.11.partner
  132.6 1.3 copy-done.1
  134.4 1.7 collective-permute-start.12
  136.1 40.4 %ffn_backward.1 = (bf16[2048,768]{1,0:T(8,128)(2,1)}, bf16[1024,768]{1,0:T(8,128)(2,1)}, bf16[1024,768]{1,0:T(8,128)(2,1)}) custom-call(s32[1]{0:T(128)} %bitcast.1.at.side, bf16[2048,768]{1,0:T(8,128)(2,1)} %get-tuple-element.162.grad_low, bf16[2048,3072]{1,0:T(8,128)(2,1)} %get-tuple-element.163.slope, bf16[2048,768]{1,0:T(8,128)(2,1)} %get-tuple-element.149.normed, ...), custom_call_target="tpu_custom_call" | custom-call | flops 24159191040 | bytes 25165824 | tf_op jit(solution)/shard_map/ffn_backward/pallas_call | solution.py:938
  176.9 3.5 %collective-permute-done.14.partner = bf16[1024,768]{1,0:T(8,128)(2,1)S(1)} collective-permute-done((bf16[1024,768]{1,0:T(8,128)(2,1)}, bf16[1024,768]{1,0:T(8,128)(2,1)S(1)}, u32[]{:S(2)}, u32[]{:S(2)}) %collective-permute-start.14) | collective-permute-done | bytes 1572896 | tf_op jit(solution)/shard_map/ppermute | solution.py:757
  181.3 3.7 %collective-permute-start.15 = (bf16[384,768]{1,0:T(8,128)(2,1)S(1)}, bf16[384,768]{1,0:T(8,128)(2,1)S(1)}, u32[]{:S(2)}, u32[]{:S(2)}) collective-permute-start(bf16[384,768]{1,0:T(8,128)(2,1)S(1)} %add.28.refs_0_), channel_id=1, source_target_pairs={{0,8},{4,12},{24,16},{28,20},{1,9},{5,13},{25,17},{29,21},{2,10},{... | collective-permute-start | bytes 1769480 | tf_op jit(solution)/shard_map/ppermute | solution.py:867
  185.0 15.4 %attention_near_backward.2 = (bf16[1024,1152]{1,0:T(8,128)(2,1)}, f32[3,384,768]{2,1,0:T(8,128)}, f32[2,8,384]{2,1,0:T(8,128)}) custom-call(s32[1]{0:T(128)} %bitcast.core, s32[16]{0:T(128)} %slen.15, s32[4]{0:T(128)} %llen.15, s32[1]{0:T(128)S(6)} %copy.56.scount, s32[1]{0:T(128)S(6)} %copy.57.lcount, bf16[2048,768]{1,0:T(8,128)(2,1)} %get-tuple-element.179.hidden_low, ...), custom_call_target="tpu_custom_call" | custom-call | flops 4278190080 | bytes 12582912 | tf_op jit(solution)/shard_map/attention_near_backward/pallas_call | solution.py:960
  200.8 3.5 %collective-permute-start.18 = (bf16[512,768]{1,0:T(8,128)(2,1)S(1)}, bf16[512,768]{1,0:T(8,128)(2,1)S(1)}, u32[]{:S(2)}, u32[]{:S(2)}) collective-permute-start(bf16[512,768]{1,0:T(8,128)(2,1)S(1)} %add.30.refs_0_), channel_id=1, source_target_pairs={{0,8},{4,12},{24,16},{28,20},{1,9},{5,13},{25,17},{29,21},{2,10},{... | collective-permute-start | bytes 2359304 | tf_op jit(solution)/shard_map/ppermute | solution.py:867
  205.2 20.1 %attention_near_backward.3 = (bf16[1024,1152]{1,0:T(8,128)(2,1)}, bf16[640,768]{1,0:T(8,128)(2,1)}, bf16[640,768]{1,0:T(8,128)(2,1)}) custom-call(s32[1]{0:T(128)} %bitcast.core, s32[16]{0:T(128)} %slen.15, s32[4]{0:T(128)} %llen.15, s32[1]{0:T(128)S(6)} %copy.56.scount, s32[1]{0:T(128)S(6)} %copy.57.lcount, ...), custom_call_target="tpu_custom_call" | custom-call | flops 4278190080 | bytes 12582912 | tf_op jit(solution)/shard_map/attention_near_backward/pallas_call | solution.py:960
  225.6 0.7 collective-permute-start.21
  226.5 1.3 collective-permute-start.20
  228.1 1.1 halves.5
  229.7 15.8 %attention_far_backward.2 = (bf16[2048,768]{1,0:T(8,128)(2,1)}, f32[4096,768]{1,0:T(8,128)}) custom-call(s32[1]{0:T(128)} %bitcast.core, s32[16]{0:T(128)} %slen.15, s32[4]{0:T(128)} %llen.15, s32[1]{0:T(128)S(6)} %copy.56.scount, s32[1]{0:T(128)S(6)} %copy.57.lcount, bf16[2048,768]{1,0:T(8,128)(2,1)} %get-tuple-element.179.hidden_low, ...), custom_call_target="tpu_custom_call" | custom-call | flops 5486149632 | bytes 12582912 | tf_op jit(solution)/shard_map/attention_far_backward/pallas_call | solution.py:985
  245.6 0.8 copy-done.5
  246.6 1.3 collective-permute-start.24
  248.0 1.6 collective-permute-start.23
  249.7 3.6 %collective-permute-start.25 = (bf16[80,768]{1,0:T(8,128)(2,1)S(1)}, bf16[80,768]{1,0:T(8,128)(2,1)S(1)}, u32[]{:S(2)}, u32[]{:S(2)}) collective-permute-start(bf16[80,768]{1,0:T(8,128)(2,1)S(1)} %get-tuple-element.207), channel_id=1, source_target_pairs={{0,8},{4,12},{8,0},{12,4},{16,24},{20,28},{24,16},{28,20},{1,9},{5... | collective-permute-start | bytes 368648 | tf_op jit(solution)/shard_map/ppermute | solution.py:757
  253.3 1.1 collective-permute-start.26
  254.4 1.4 collective-permute-start.27
  255.7 21.9 %attention_far_backward.3 = (bf16[2048,768]{1,0:T(8,128)(2,1)}, f32[4096,768]{1,0:T(8,128)}) custom-call(s32[1]{0:T(128)} %bitcast.core, s32[16]{0:T(128)} %slen.15, s32[4]{0:T(128)} %llen.15, s32[1]{0:T(128)S(6)} %copy.56.scount, s32[1]{0:T(128)S(6)} %copy.57.lcount, ...), custom_call_target="tpu_custom_call", output_to_operand_aliasing={{0}: (14, {}), {1}: (15, {})} | custom-call | flops 5486149632 | bytes 12582912 | tf_op jit(solution)/shard_map/attention_far_backward/pallas_call | solution.py:985
  277.9 1.0 collective-permute-start.32
  278.9 2.3 collective-permute-start.30
  281.4 1.9 collective-permute-start.28
  283.3 4.2 %place.2 = bf16[4096,768]{1,0:T(8,128)(2,1)} custom-call(s32[1]{0:T(128)} %bitcast.core, bf16[2048,768]{1,0:T(8,128)(2,1)} %collective-permute-done.13.other, bf16[4096,768]{1,0:T(8,128)(2,1)} %get-tuple-element.222.whole), custom_call_target="tpu_custom_call", output_to_operand_aliasing={{}: (2, {})} | custom-call | bytes 9437184 | tf_op jit(solution)/shard_map/place/pallas_call | solution.py:1011
  287.5 5.2 %collective-permute-done.29.refs_2_ = bf16[80,768]{1,0:T(8,128)(2,1)S(1)} collective-permute-done((bf16[80,768]{1,0:T(8,128)(2,1)S(1)}, bf16[80,768]{1,0:T(8,128)(2,1)S(1)}, u32[]{:S(2)}, u32[]{:S(2)}) %collective-permute-start.29) | collective-permute-done | bytes 122912 | tf_op jit(solution)/shard_map/ppermute | solution.py:757
  292.7 1.1 collective-permute-start.33
  293.9 1.8 finish.5
  295.7 2.6 collective-permute-done.32.other
  298.3 2.1 finish.3
  300.5 5.0 %place.3 = f32[4096,768]{1,0:T(8,128)} custom-call(s32[1]{0:T(128)} %bitcast.core, bf16[2048,768]{1,0:T(8,128)(2,1)} %collective-permute-done.31.other, f32[4096,768]{1,0:T(8,128)} %get-tuple-element.233.whole), custom_call_target="tpu_custom_call", output_to_operand_aliasing={{}: (2, {})} | custom-call | bytes 9437184 | tf_op jit(solution)/shard_map/place/pallas_call | solution.py:1011
  306.1 2.3 collective-permute-done.33.other
  308.4 1.5 finish.4
  (82 shorter events, 8.6 us)
Async XLA Ops:
  3.2 5.5 %collective-permute-start = (bf16[784,768]{1,0:T(8,128)(2,1)}, bf16[784,768]{1,0:T(8,128)(2,1)S(1)}, u32[]{:S(2)}, u32[]{:S(2)}) collective-permute-start(bf16[784,768]{1,0:T(8,128)(2,1)} %get-tuple-element.131.a0.rest_10_), channel_id=1, source_target_pairs={{0,1},{1,0},{2,3},{3,2},{4,5},{5,4},{6,7},{7,6},{8,9},{9,8},{10,11... | collective-permute-start | bytes 3612680 | tf_op jit(solution)/shard_map/ppermute | solution.py:757
  3.7 29.9 %collective-permute-start.1 = (bf16[784,768]{1,0:T(8,128)(2,1)}, bf16[784,768]{1,0:T(8,128)(2,1)S(1)}, u32[]{:S(2)}, u32[]{:S(2)}) collective-permute-start(bf16[784,768]{1,0:T(8,128)(2,1)} %get-tuple-element.131.a0.rest_10_), channel_id=1, source_target_pairs={{0,2},{1,3},{2,0},{3,1},{4,6},{5,7},{6,4},{7,5},{8,10},{9,11},{10,... | collective-permute-start | bytes 3612680 | tf_op jit(solution)/shard_map/ppermute | solution.py:757
  8.7 1.0 copy-start.7
  33.5 5.1 %copy-start.8 = (bf16[784,768]{1,0:T(8,128)(2,1)}, bf16[784,768]{1,0:T(8,128)(2,1)S(1)}, u32[]{:S(2)}) copy-start(bf16[784,768]{1,0:T(8,128)(2,1)S(1)} %collective-permute-done.1.a2.rest_12_) | copy-start | bytes 3612676
  33.6 2.9 collective-permute-start.2
  36.4 2.2 copy-start.9
  36.4 16.7 %collective-permute-start.4 = (bf16[768,768]{1,0:T(8,128)(2,1)}, bf16[768,768]{1,0:T(8,128)(2,1)}, u32[]{:S(2)}, u32[]{:S(2)}) collective-permute-start(bf16[768,768]{1,0:T(8,128)(2,1)} %rest_0_.3), channel_id=1, source_target_pairs={{0,1},{1,0},{2,3},{3,2},{4,5},{5,4},{6,7},{7,6},{8,9},{9,8},{10,11... | collective-permute-start | bytes 3538952 | tf_op jit(solution)/shard_map/ppermute | solution.py:757
  36.6 16.5 %collective-permute-start.3 = (bf16[768,384]{1,0:T(8,128)(2,1)S(1)}, bf16[768,384]{1,0:T(8,128)(2,1)}, u32[]{:S(2)}, u32[]{:S(2)}) collective-permute-start(bf16[768,384]{1,0:T(8,128)(2,1)S(1)} %constant_dynamic-slice_fusion), channel_id=1, source_target_pairs={{0,2},{1,3},{2,0},{3,1},{4,6},{5,7},{6,4},{7,5},{8,10},{9,11},{10,... | collective-permute-start | bytes 1769480 | tf_op jit(solution)/shard_map/ppermute | solution.py:757
  38.3 39.2 %collective-permute-start.7 = (bf16[768,768]{1,0:T(8,128)(2,1)}, bf16[768,768]{1,0:T(8,128)(2,1)}, u32[]{:S(2)}, u32[]{:S(2)}) collective-permute-start(bf16[768,768]{1,0:T(8,128)(2,1)} %rest_6_.3), channel_id=1, source_target_pairs={{0,2},{1,3},{2,0},{3,1},{4,6},{5,7},{6,4},{7,5},{8,10},{9,11},{10,... | collective-permute-start | bytes 3538952 | tf_op jit(solution)/shard_map/ppermute | solution.py:757
  53.1 24.5 %collective-permute-start.8 = (bf16[768,768]{1,0:T(8,128)(2,1)}, bf16[768,768]{1,0:T(8,128)(2,1)S(1)}, u32[]{:S(2)}, u32[]{:S(2)}) collective-permute-start(bf16[768,768]{1,0:T(8,128)(2,1)} %rest_6_.3), channel_id=1, source_target_pairs={{0,1},{1,0},{2,3},{3,2},{4,5},{5,4},{6,7},{7,6},{8,9},{9,8},{10,11... | collective-permute-start | bytes 3538952 | tf_op jit(solution)/shard_map/ppermute | solution.py:757
  53.2 24.4 %collective-permute-start.6 = (bf16[768,384]{1,0:T(8,128)(2,1)}, bf16[768,384]{1,0:T(8,128)(2,1)S(1)}, u32[]{:S(2)}, u32[]{:S(2)}) collective-permute-start(bf16[768,384]{1,0:T(8,128)(2,1)} %collective-permute-done.3.rest_2_), channel_id=1, source_target_pairs={{0,1},{1,0},{2,3},{3,2},{4,5},{5,4},{6,7},{7,6},{8,9},{9,8},{10,11... | collective-permute-start | bytes 1769480 | tf_op jit(solution)/shard_map/ppermute | solution.py:757
  53.7 23.9 %collective-permute-start.5 = (bf16[768,384]{1,0:T(8,128)(2,1)}, bf16[768,384]{1,0:T(8,128)(2,1)S(1)}, u32[]{:S(2)}, u32[]{:S(2)}) collective-permute-start(bf16[768,384]{1,0:T(8,128)(2,1)} %collective-permute-done.3.rest_2_), channel_id=1, source_target_pairs={{0,4},{4,0},{8,12},{12,8},{16,20},{20,16},{24,28},{28,24},{1,5},{5... | collective-permute-start | bytes 1769480 | tf_op jit(solution)/shard_map/ppermute | solution.py:757
  77.6 4.6 %copy-start.12 = (bf16[768,384]{1,0:T(8,128)(2,1)}, bf16[768,384]{1,0:T(8,128)(2,1)S(1)}, u32[]{:S(2)}) copy-start(bf16[768,384]{1,0:T(8,128)(2,1)S(1)} %collective-permute-done.6.rest_3_) | copy-start | bytes 1769476
  77.6 4.6 %copy-start.13 = (bf16[768,384]{1,0:T(8,128)(2,1)}, bf16[768,384]{1,0:T(8,128)(2,1)S(1)}, u32[]{:S(2)}) copy-start(bf16[768,384]{1,0:T(8,128)(2,1)S(1)} %collective-permute-done.5.rest_4_) | copy-start | bytes 1769476
  77.6 4.5 %copy-start.10 = (bf16[768,768]{1,0:T(8,128)(2,1)}, bf16[768,768]{1,0:T(8,128)(2,1)S(1)}, u32[]{:S(2)}) copy-start(bf16[768,768]{1,0:T(8,128)(2,1)S(1)} %collective-permute-done.8.rest_7_) | copy-start | bytes 3538948
  77.6 4.5 %collective-permute-start.10 = (bf16[768,768]{1,0:T(8,128)(2,1)}, bf16[768,768]{1,0:T(8,128)(2,1)S(1)}, u32[]{:S(2)}, u32[]{:S(2)}) collective-permute-start(bf16[768,768]{1,0:T(8,128)(2,1)} %collective-permute-done.7.rest_8_), channel_id=1, source_target_pairs={{0,1},{1,0},{2,3},{3,2},{4,5},{5,4},{6,7},{7,6},{8,9},{9,8},{10,11... | collective-permute-start | bytes 3538952 | tf_op jit(solution)/shard_map/ppermute | solution.py:757
  77.7 3.6 %collective-permute-start.9 = (bf16[768,384]{1,0:T(8,128)(2,1)S(1)}, bf16[768,384]{1,0:T(8,128)(2,1)S(1)}, u32[]{:S(2)}, u32[]{:S(2)}) collective-permute-start(bf16[768,384]{1,0:T(8,128)(2,1)S(1)} %collective-permute-done.5.rest_4_), channel_id=1, source_target_pairs={{0,1},{1,0},{2,3},{3,2},{4,5},{5,4},{6,7},{7,6},{8,9},{9,8},{10,11... | collective-permute-start | bytes 1769480 | tf_op jit(solution)/shard_map/ppermute | solution.py:757
  81.3 0.8 copy-start.14
  82.1 1.0 copy-start.11
  129.5 3.1 %collective-permute-start.11 = (bf16[768,768]{1,0:T(8,128)(2,1)}, bf16[768,768]{1,0:T(8,128)(2,1)S(1)}, u32[]{:S(2)}, u32[]{:S(2)}) collective-permute-start(bf16[768,768]{1,0:T(8,128)(2,1)} %get-tuple-element.160), channel_id=1, source_target_pairs={{0,1},{1,0},{2,3},{3,2},{4,5},{5,4},{6,7},{7,6},{8,9},{9,8},{10,11... | collective-permute-start | bytes 3538952 | tf_op jit(solution)/shard_map/ppermute | solution.py:757
  132.6 1.3 copy-start.1
  134.2 42.4 %collective-permute-start.13 = (bf16[2048,768]{1,0:T(8,128)(2,1)}, bf16[2048,768]{1,0:T(8,128)(2,1)}, u32[]{:S(2)}, u32[]{:S(2)}) collective-permute-start(bf16[2048,768]{1,0:T(8,128)(2,1)} %get-tuple-element.170), channel_id=1, source_target_pairs={{0,1},{1,0},{2,3},{3,2},{4,5},{5,4},{6,7},{7,6},{8,9},{9,8},{10,11... | collective-permute-start | bytes 9437192 | tf_op jit(solution)/shard_map/ppermute | solution.py:757
  134.4 42.1 %collective-permute-start.12 = (bf16[384,768]{1,0:T(8,128)(2,1)S(1)}, bf16[384,768]{1,0:T(8,128)(2,1)S(1)}, u32[]{:S(2)}, u32[]{:S(2)}) collective-permute-start(bf16[384,768]{1,0:T(8,128)(2,1)S(1)} %get-tuple-element.161), channel_id=1, source_target_pairs={{0,4},{4,0},{8,12},{12,8},{16,20},{20,16},{24,28},{28,24},{1,5},{5... | collective-permute-start | bytes 1769480 | tf_op jit(solution)/shard_map/ppermute | solution.py:757
  176.5 3.9 %copy-start = (bf16[1024,768]{1,0:T(8,128)(2,1)S(1)}, bf16[1024,768]{1,0:T(8,128)(2,1)}, u32[]{:S(2)}) copy-start(bf16[1024,768]{1,0:T(8,128)(2,1)} %get-tuple-element.173.mine) | copy-start | bytes 4718596
  176.8 3.7 %collective-permute-start.14 = (bf16[1024,768]{1,0:T(8,128)(2,1)}, bf16[1024,768]{1,0:T(8,128)(2,1)S(1)}, u32[]{:S(2)}, u32[]{:S(2)}) collective-permute-start(bf16[1024,768]{1,0:T(8,128)(2,1)} %get-tuple-element.177), channel_id=1, source_target_pairs={{0,1},{1,0},{2,3},{3,2},{4,5},{5,4},{6,7},{7,6},{8,9},{9,8},{10,11... | collective-permute-start | bytes 4718600 | tf_op jit(solution)/shard_map/ppermute | solution.py:757
  180.9 19.6 %collective-permute-start.16 = (bf16[512,768]{1,0:T(8,128)(2,1)S(1)}, bf16[512,768]{1,0:T(8,128)(2,1)S(1)}, u32[]{:S(2)}, u32[]{:S(2)}) collective-permute-start(bf16[512,768]{1,0:T(8,128)(2,1)S(1)} %get-tuple-element.178), channel_id=1, source_target_pairs={{0,4},{4,0},{8,12},{12,8},{16,20},{20,16},{24,28},{28,24},{1,5},{5... | collective-permute-start | bytes 2359304 | tf_op jit(solution)/shard_map/ppermute | solution.py:757
  181.3 19.1 %collective-permute-start.15 = (bf16[384,768]{1,0:T(8,128)(2,1)S(1)}, bf16[384,768]{1,0:T(8,128)(2,1)S(1)}, u32[]{:S(2)}, u32[]{:S(2)}) collective-permute-start(bf16[384,768]{1,0:T(8,128)(2,1)S(1)} %add.28.refs_0_), channel_id=1, source_target_pairs={{0,8},{4,12},{24,16},{28,20},{1,9},{5,13},{25,17},{29,21},{2,10},{... | collective-permute-start | bytes 1769480 | tf_op jit(solution)/shard_map/ppermute | solution.py:867
  200.8 24.5 %collective-permute-start.18 = (bf16[512,768]{1,0:T(8,128)(2,1)S(1)}, bf16[512,768]{1,0:T(8,128)(2,1)S(1)}, u32[]{:S(2)}, u32[]{:S(2)}) collective-permute-start(bf16[512,768]{1,0:T(8,128)(2,1)S(1)} %add.30.refs_0_), channel_id=1, source_target_pairs={{0,8},{4,12},{24,16},{28,20},{1,9},{5,13},{25,17},{29,21},{2,10},{... | collective-permute-start | bytes 2359304 | tf_op jit(solution)/shard_map/ppermute | solution.py:867
  204.5 20.8 %collective-permute-start.17 = (bf16[384,768]{1,0:T(8,128)(2,1)S(1)}, bf16[384,768]{1,0:T(8,128)(2,1)S(1)}, u32[]{:S(2)}, u32[]{:S(2)}) collective-permute-start(bf16[384,768]{1,0:T(8,128)(2,1)S(1)} %add.29.refs_0_), channel_id=1, source_target_pairs={{8,16},{12,20},{16,8},{20,12},{9,17},{13,21},{17,9},{21,13},{10,18... | collective-permute-start | bytes 1769480 | tf_op jit(solution)/shard_map/ppermute | solution.py:867
  225.3 2.9 copy-start.2
  225.3 2.8 collective-permute-start.19
  225.6 20.0 %collective-permute-start.21 = (bf16[512,768]{1,0:T(8,128)(2,1)S(1)}, bf16[512,768]{1,0:T(8,128)(2,1)S(1)}, u32[]{:S(2)}, u32[]{:S(2)}) collective-permute-start(bf16[512,768]{1,0:T(8,128)(2,1)S(1)} %add.32.refs_0_), channel_id=1, source_target_pairs={{8,16},{12,20},{16,8},{20,12},{9,17},{13,21},{17,9},{21,13},{10,18... | collective-permute-start | bytes 2359304 | tf_op jit(solution)/shard_map/ppermute | solution.py:867
  226.5 19.1 %collective-permute-start.20 = (bf16[384,768]{1,0:T(8,128)(2,1)S(1)}, bf16[384,768]{1,0:T(8,128)(2,1)S(1)}, u32[]{:S(2)}, u32[]{:S(2)}) collective-permute-start(bf16[384,768]{1,0:T(8,128)(2,1)S(1)} %add.31.own), channel_id=1, source_target_pairs={{8,0},{12,4},{16,24},{20,28},{9,1},{13,5},{17,25},{21,29},{10,2},{... | collective-permute-start | bytes 1769480 | tf_op jit(solution)/shard_map/ppermute | solution.py:867
  229.2 16.4 %copy-start.3 = (bf16[320,768]{1,0:T(8,128)(2,1)}, bf16[320,768]{1,0:T(8,128)(2,1)S(1)}, u32[]{:S(2)}) copy-start(bf16[320,768]{1,0:T(8,128)(2,1)S(1)} %get-tuple-element.194.keep) | copy-start | bytes 1474564
  229.2 16.4 %collective-permute-start.22 = (bf16[320,768]{1,0:T(8,128)(2,1)}, bf16[320,768]{1,0:T(8,128)(2,1)S(1)}, u32[]{:S(2)}, u32[]{:S(2)}) collective-permute-start(bf16[320,768]{1,0:T(8,128)(2,1)} %get-tuple-element.201), channel_id=1, source_target_pairs={{0,4},{4,0},{8,12},{12,8},{16,20},{20,16},{24,28},{28,24},{1,5},{5... | collective-permute-start | bytes 1474568 | tf_op jit(solution)/shard_map/ppermute | solution.py:757
  245.6 4.0 %copy-start.4 = (bf16[320,768]{1,0:T(8,128)(2,1)S(1)}, bf16[320,768]{1,0:T(8,128)(2,1)}, u32[]{:S(2)}) copy-start(bf16[320,768]{1,0:T(8,128)(2,1)} %copy-done.3) | copy-start | bytes 1474564
  246.4 3.2 %copy-start.6 = (bf16[320,768]{1,0:T(8,128)(2,1)S(1)}, bf16[320,768]{1,0:T(8,128)(2,1)}, u32[]{:S(2)}) copy-start(bf16[320,768]{1,0:T(8,128)(2,1)} %copy-done.5) | copy-start | bytes 1474564
  246.6 31.1 %collective-permute-start.24 = (bf16[512,768]{1,0:T(8,128)(2,1)S(1)}, bf16[512,768]{1,0:T(8,128)(2,1)S(1)}, u32[]{:S(2)}, u32[]{:S(2)}) collective-permute-start(bf16[512,768]{1,0:T(8,128)(2,1)S(1)} %add.33.own), channel_id=1, source_target_pairs={{8,0},{12,4},{16,24},{20,28},{9,1},{13,5},{17,25},{21,29},{10,2},{... | collective-permute-start | bytes 2359304 | tf_op jit(solution)/shard_map/ppermute | solution.py:867
  248.0 29.7 %collective-permute-start.23 = (bf16[384,768]{1,0:T(8,128)(2,1)S(1)}, bf16[384,768]{1,0:T(8,128)(2,1)S(1)}, u32[]{:S(2)}, u32[]{:S(2)}) collective-permute-start(bf16[384,768]{1,0:T(8,128)(2,1)S(1)} %choose.2.own), channel_id=1, source_target_pairs={{0,4},{4,0},{8,12},{12,8},{16,20},{20,16},{24,28},{28,24},{1,5},{5... | collective-permute-start | bytes 1769480 | tf_op jit(solution)/shard_map/ppermute | solution.py:757
  249.7 28.0 %collective-permute-start.25 = (bf16[80,768]{1,0:T(8,128)(2,1)S(1)}, bf16[80,768]{1,0:T(8,128)(2,1)S(1)}, u32[]{:S(2)}, u32[]{:S(2)}) collective-permute-start(bf16[80,768]{1,0:T(8,128)(2,1)S(1)} %get-tuple-element.207), channel_id=1, source_target_pairs={{0,8},{4,12},{8,0},{12,4},{16,24},{20,28},{24,16},{28,20},{1,9},{5... | collective-permute-start | bytes 368648 | tf_op jit(solution)/shard_map/ppermute | solution.py:757
  253.3 24.4 %collective-permute-start.26 = (bf16[80,768]{1,0:T(8,128)(2,1)S(1)}, bf16[80,768]{1,0:T(8,128)(2,1)S(1)}, u32[]{:S(2)}, u32[]{:S(2)}) collective-permute-start(bf16[80,768]{1,0:T(8,128)(2,1)S(1)} %get-tuple-element.214), channel_id=1, source_target_pairs={{0,16},{4,20},{8,24},{12,28},{16,0},{20,4},{24,8},{28,12},{1,17},{... | collective-permute-start | bytes 368648 | tf_op jit(solution)/shard_map/ppermute | solution.py:757
  254.4 23.3 %collective-permute-start.27 = (bf16[80,768]{1,0:T(8,128)(2,1)S(1)}, bf16[80,768]{1,0:T(8,128)(2,1)S(1)}, u32[]{:S(2)}, u32[]{:S(2)}) collective-permute-start(bf16[80,768]{1,0:T(8,128)(2,1)S(1)} %get-tuple-element.215), channel_id=1, source_target_pairs={{0,24},{4,28},{8,16},{12,20},{16,8},{20,12},{24,0},{28,4},{1,25},{... | collective-permute-start | bytes 368648 | tf_op jit(solution)/shard_map/ppermute | solution.py:757
  277.9 14.8 %collective-permute-start.31 = (bf16[2048,768]{1,0:T(8,128)(2,1)}, bf16[2048,768]{1,0:T(8,128)(2,1)}, u32[]{:S(2)}, u32[]{:S(2)}) collective-permute-start(bf16[2048,768]{1,0:T(8,128)(2,1)} %get-tuple-element.224), channel_id=1, source_target_pairs={{0,1},{1,0},{2,3},{3,2},{4,5},{5,4},{6,7},{7,6},{8,9},{9,8},{10,11... | collective-permute-start | bytes 9437192 | tf_op jit(solution)/shard_map/ppermute | solution.py:757
  277.9 20.4 %collective-permute-start.32 = (bf16[512,768]{1,0:T(8,128)(2,1)S(1)}, bf16[512,768]{1,0:T(8,128)(2,1)S(1)}, u32[]{:S(2)}, u32[]{:S(2)}) collective-permute-start(bf16[512,768]{1,0:T(8,128)(2,1)S(1)} %choose.3.own), channel_id=1, source_target_pairs={{0,4},{4,0},{8,12},{12,8},{16,20},{20,16},{24,28},{28,24},{1,5},{5... | collective-permute-start | bytes 2359304 | tf_op jit(solution)/shard_map/ppermute | solution.py:757
  278.9 8.6 %collective-permute-start.30 = (bf16[80,768]{1,0:T(8,128)(2,1)S(1)}, bf16[80,768]{1,0:T(8,128)(2,1)S(1)}, u32[]{:S(2)}, u32[]{:S(2)}) collective-permute-start(bf16[80,768]{1,0:T(8,128)(2,1)S(1)} %add.34.refs_0_), channel_id=1, source_target_pairs={{0,24},{4,28},{8,16},{12,20},{16,8},{20,12},{24,0},{28,4},{1,25},{... | collective-permute-start | bytes 368648 | tf_op jit(solution)/shard_map/ppermute | solution.py:757
  281.2 11.5 %collective-permute-start.29 = (bf16[80,768]{1,0:T(8,128)(2,1)S(1)}, bf16[80,768]{1,0:T(8,128)(2,1)S(1)}, u32[]{:S(2)}, u32[]{:S(2)}) collective-permute-start(bf16[80,768]{1,0:T(8,128)(2,1)S(1)} %add.34.refs_0_), channel_id=1, source_target_pairs={{0,16},{4,20},{8,24},{12,28},{16,0},{20,4},{24,8},{28,12},{1,17},{... | collective-permute-start | bytes 368648 | tf_op jit(solution)/shard_map/ppermute | solution.py:757
  281.4 11.3 %collective-permute-start.28 = (bf16[80,768]{1,0:T(8,128)(2,1)S(1)}, bf16[80,768]{1,0:T(8,128)(2,1)S(1)}, u32[]{:S(2)}, u32[]{:S(2)}) collective-permute-start(bf16[80,768]{1,0:T(8,128)(2,1)S(1)} %add.34.refs_0_), channel_id=1, source_target_pairs={{0,8},{4,12},{8,0},{12,4},{16,24},{20,28},{24,16},{28,20},{1,9},{5... | collective-permute-start | bytes 368648 | tf_op jit(solution)/shard_map/ppermute | solution.py:757
  292.7 15.7 %collective-permute-start.33 = (bf16[320,768]{1,0:T(8,128)(2,1)S(1)}, bf16[320,768]{1,0:T(8,128)(2,1)S(1)}, u32[]{:S(2)}, u32[]{:S(2)}) collective-permute-start(bf16[320,768]{1,0:T(8,128)(2,1)S(1)} %join_quarters.1.own), channel_id=1, source_target_pairs={{0,4},{4,0},{8,12},{12,8},{16,20},{20,16},{24,28},{28,24},{1,5},{5... | collective-permute-start | bytes 1474568 | tf_op jit(solution)/shard_map/ppermute | solution.py:757
  (1 other events, 0.8 us)
